TPU v7x, 128 devices: a whole 4x4x4 slice. The times are simulated.
128 devices in a mesh: occ: 8 (over y, core), vir: 16 (over z, x).
Axes of the slice: x: 4, y: 4, z: 4, core: 2. Of those that a mesh axis runs over, the one named last changes fastest.
Arguments:
- amplitudes: bfloat16 [9216, 16384], P('occ', 'vir'), may hold values from -6 to 6
- integrals: bfloat16 [16, 8, 1024, 1024], P('vir'), may hold values from -0.0625 to 0.0625
- cd_tiles: int32 [16, 8], P('vir'), may hold values from 0 to 15, as said below
- cd_count: int32 [16], P('vir'), may hold values from 1 to 8, as said below
Outputs:
- residual: bfloat16 [9216, 16384], P('occ', 'vir')
Inputs may be any that keep to these rules, and one draw needn't show every extreme that they name: `cd_tiles`: entries of one row are distinct and the first is the row's own pair tile. `cd_count`: slots at or past the count are unused.
All inputs are finite; a program needn't handle non-finite values.
Results may differ from a plain program's by a relative error of at most 0.0075.
Values may be sent and summed in bfloat16 or wider, within the bound.
No kernel may reach another device: no remote copies, remote signals or barrier semaphores. Data moves between devices by JAX's collectives and lax.ppermute only.
A program may use at most 128 MiB of HBM per device.

v0:
```python
import jax
import jax.numpy as jnp
from jax import lax
from jax.sharding import PartitionSpec as P

TW = 32
K = 1024
OCC_DEV = 12
CD_MAX = 8


def swapped(shard, axis, apart):
    return lax.ppermute(shard, axis, [(i, i ^ 1 << apart) for i in range(lax.axis_size(axis))])


def reflect_rows(matrix):
    occ_devices = lax.axis_size("occ")
    reshaped = matrix.reshape(OCC_DEV, occ_devices, OCC_DEV, matrix.shape[1])
    arrived = lax.all_to_all(reshaped, "occ", split_axis=1, concat_axis=1, tiled=True)
    return arrived.transpose(2, 1, 0, 3).reshape(matrix.shape)


def reflect_tiles(matrix):
    arrived = swapped(matrix, "vir", 0)
    row_count = matrix.shape[0]
    return arrived.reshape(row_count, TW, TW).transpose(0, 2, 1).reshape(row_count, K)


def on_device(amplitudes, integrals, cd_tiles, cd_count):
    row_count = amplitudes.shape[0]
    listed = cd_tiles[0]
    live_count = cd_count[0]
    blocks = integrals[0]
    zero_block = jnp.zeros((row_count, K), jnp.float32)

    def product(col_tile, slot_index):
        int_block = lax.dynamic_index_in_dim(blocks, slot_index, 0, keepdims=False)
        return lax.dot_general(
            col_tile, int_block, (((1,), (1,)), ((), ())), preferred_element_type=jnp.float32
        )

    gathered = lax.all_gather(amplitudes, "vir", axis=1, tiled=True)

    def visit_slot(slot_pos, running):
        tile_id = listed[slot_pos]

        def apply_block(current):
            col_tile = lax.dynamic_slice_in_dim(gathered, tile_id * K, K, 1)
            return current + product(col_tile, slot_pos)

        return lax.cond(slot_pos < live_count, apply_block, lambda current: current, running)

    ladder = lax.fori_loop(0, CD_MAX, visit_slot, zero_block)
    ladder = ladder.astype(jnp.bfloat16)
    mirrored = reflect_tiles(reflect_rows(ladder))
    summed = ladder.astype(jnp.float32) + mirrored.astype(jnp.float32)
    return summed.astype(jnp.bfloat16)


def solution(mesh):
    placed = (P("occ", "vir"), P("vir", None, None, None), P("vir", None), P("vir"))
    return jax.shard_map(
        on_device, mesh=mesh, in_specs=placed, out_specs=P("occ", "vir"), check_vma=False
    )
```

profile of v0, /device:TPU:38, one launch (start us, length us, event | category | flops | bytes accessed | tf_op | source)
XLA Modules:
  0.0 454.4 jit_solution(4664653060656685572)
XLA Ops:
  6.5 0.0 copy-start
  6.5 0.0 all-gather.2.cloned.1.call-start
  6.5 0.7 all-gather.2.cloned.1.call-update
  7.3 221.4 %all-gather.2.cloned.1.call-done = bf16[1152,16384]{1,0:T(8,128)(2,1)} async-done(((bf16[1152,1024]{1,0:T(8,128)(2,1)}), bf16[1152,16384]{1,0:T(8,128)(2,1)}) %all-gather.2.cloned.1.call-update) | async-done | bytes 37748752 | tf_op jit(solution)/shard_map/all_gather | solution.py:42
  228.6 2.8 broadcast_in_dim.3
  231.4 0.0 copy-done
  231.4 83.6 %while.16 = (s32[]{:T(128)}, f32[1152,1024]{1,0:T(8,128)}, s32[]{:T(128)}, s32[8]{0:T(128)S(1)}, bf16[1152,16384]{1,0:T(8,128)(2,1)}, /*index=5*/bf16[8,1024,1024]{2,1,0:T(8,128)(2,1)}, s32[]{:T(128)}) while((s32[]{:T(128)}, f32[1152,1024]{1,0:T(8,128)}, s32[]{:T(128)}, s32[8]{0:T(128)S(1)}, bf16[1152,16384]{1,0:T(8,128)(2,1)}, ...), condition=%wide.region_3.4_spmd, body=%wide.region_0.3_spmd.sunk | while | flops 2417098752 | bytes 13893871 | solution.py:53
  232.0 9.8 %conditional.2 = (f32[1152,1024]{1,0:T(8,128)}) conditional(s32[]{:T(128)} %convert_element_type.41, f32[1152,1024]{1,0:T(8,128)} %get-tuple-element.236, (s32[]{:T(128)}, s32[8]{0:T(128)S(1)}, bf16[1152,16384]{1,0:T(8,128)(2,1)}, bf16[8,1024,1024]{2,1,0:T(8,128)(2,1)}, f32[1152,1024]{1,0:T(8,128)}) %tuple.45), branch_computations={%region_1.0_spmd, %region_2.2_spmd} | conditional | flops 2417098752 | bytes 13893740 | solution.py:51
  232.1 0.6 dynamic_slice.18
  233.3 8.5 %convolution_add_fusion = f32[1152,1024]{1,0:T(8,128)} fusion(f32[1152,1024]{1,0:T(8,128)} %get-tuple-element.165, bf16[1152,16384]{1,0:T(8,128)(2,1)} %get-tuple-element.166, s32[]{:T(128)S(6)} %select_n.19, bf16[8,1024,1024]{2,1,0:T(8,128)(2,1)} %get-tuple-element.169, s32[]{:T(128)S(6)} %select_n.18), kind=kOutput, calls=%fused_computation | convolution fusion | flops 2417098752 | bytes 13893640 | tf_op jit(solution)/shard_map/while/body/eval_jaxpr/cond/branch_1_fun/dot_general | solution.py:38
  242.5 9.8 %conditional.2 = (f32[1152,1024]{1,0:T(8,128)}) conditional(s32[]{:T(128)} %convert_element_type.41, f32[1152,1024]{1,0:T(8,128)} %get-tuple-element.236, (s32[]{:T(128)}, s32[8]{0:T(128)S(1)}, bf16[1152,16384]{1,0:T(8,128)(2,1)}, bf16[8,1024,1024]{2,1,0:T(8,128)(2,1)}, f32[1152,1024]{1,0:T(8,128)}) %tuple.45), branch_computations={%region_1.0_spmd, %region_2.2_spmd} | conditional | flops 2417098752 | bytes 13893740 | solution.py:51
  242.5 0.6 dynamic_slice.18
  243.8 8.5 %convolution_add_fusion = f32[1152,1024]{1,0:T(8,128)} fusion(f32[1152,1024]{1,0:T(8,128)} %get-tuple-element.165, bf16[1152,16384]{1,0:T(8,128)(2,1)} %get-tuple-element.166, s32[]{:T(128)S(6)} %select_n.19, bf16[8,1024,1024]{2,1,0:T(8,128)(2,1)} %get-tuple-element.169, s32[]{:T(128)S(6)} %select_n.18), kind=kOutput, calls=%fused_computation | convolution fusion | flops 2417098752 | bytes 13893640 | tf_op jit(solution)/shard_map/while/body/eval_jaxpr/cond/branch_1_fun/dot_general | solution.py:38
  252.9 9.8 %conditional.2 = (f32[1152,1024]{1,0:T(8,128)}) conditional(s32[]{:T(128)} %convert_element_type.41, f32[1152,1024]{1,0:T(8,128)} %get-tuple-element.236, (s32[]{:T(128)}, s32[8]{0:T(128)S(1)}, bf16[1152,16384]{1,0:T(8,128)(2,1)}, bf16[8,1024,1024]{2,1,0:T(8,128)(2,1)}, f32[1152,1024]{1,0:T(8,128)}) %tuple.45), branch_computations={%region_1.0_spmd, %region_2.2_spmd} | conditional | flops 2417098752 | bytes 13893740 | solution.py:51
  252.9 0.6 dynamic_slice.18
  254.2 8.5 %convolution_add_fusion = f32[1152,1024]{1,0:T(8,128)} fusion(f32[1152,1024]{1,0:T(8,128)} %get-tuple-element.165, bf16[1152,16384]{1,0:T(8,128)(2,1)} %get-tuple-element.166, s32[]{:T(128)S(6)} %select_n.19, bf16[8,1024,1024]{2,1,0:T(8,128)(2,1)} %get-tuple-element.169, s32[]{:T(128)S(6)} %select_n.18), kind=kOutput, calls=%fused_computation | convolution fusion | flops 2417098752 | bytes 13893640 | tf_op jit(solution)/shard_map/while/body/eval_jaxpr/cond/branch_1_fun/dot_general | solution.py:38
  263.4 9.8 %conditional.2 = (f32[1152,1024]{1,0:T(8,128)}) conditional(s32[]{:T(128)} %convert_element_type.41, f32[1152,1024]{1,0:T(8,128)} %get-tuple-element.236, (s32[]{:T(128)}, s32[8]{0:T(128)S(1)}, bf16[1152,16384]{1,0:T(8,128)(2,1)}, bf16[8,1024,1024]{2,1,0:T(8,128)(2,1)}, f32[1152,1024]{1,0:T(8,128)}) %tuple.45), branch_computations={%region_1.0_spmd, %region_2.2_spmd} | conditional | flops 2417098752 | bytes 13893740 | solution.py:51
  263.4 0.6 dynamic_slice.18
  264.6 8.5 %convolution_add_fusion = f32[1152,1024]{1,0:T(8,128)} fusion(f32[1152,1024]{1,0:T(8,128)} %get-tuple-element.165, bf16[1152,16384]{1,0:T(8,128)(2,1)} %get-tuple-element.166, s32[]{:T(128)S(6)} %select_n.19, bf16[8,1024,1024]{2,1,0:T(8,128)(2,1)} %get-tuple-element.169, s32[]{:T(128)S(6)} %select_n.18), kind=kOutput, calls=%fused_computation | convolution fusion | flops 2417098752 | bytes 13893640 | tf_op jit(solution)/shard_map/while/body/eval_jaxpr/cond/branch_1_fun/dot_general | solution.py:38
  273.8 9.8 %conditional.2 = (f32[1152,1024]{1,0:T(8,128)}) conditional(s32[]{:T(128)} %convert_element_type.41, f32[1152,1024]{1,0:T(8,128)} %get-tuple-element.236, (s32[]{:T(128)}, s32[8]{0:T(128)S(1)}, bf16[1152,16384]{1,0:T(8,128)(2,1)}, bf16[8,1024,1024]{2,1,0:T(8,128)(2,1)}, f32[1152,1024]{1,0:T(8,128)}) %tuple.45), branch_computations={%region_1.0_spmd, %region_2.2_spmd} | conditional | flops 2417098752 | bytes 13893740 | solution.py:51
  273.8 0.6 dynamic_slice.18
  275.1 8.5 %convolution_add_fusion = f32[1152,1024]{1,0:T(8,128)} fusion(f32[1152,1024]{1,0:T(8,128)} %get-tuple-element.165, bf16[1152,16384]{1,0:T(8,128)(2,1)} %get-tuple-element.166, s32[]{:T(128)S(6)} %select_n.19, bf16[8,1024,1024]{2,1,0:T(8,128)(2,1)} %get-tuple-element.169, s32[]{:T(128)S(6)} %select_n.18), kind=kOutput, calls=%fused_computation | convolution fusion | flops 2417098752 | bytes 13893640 | tf_op jit(solution)/shard_map/while/body/eval_jaxpr/cond/branch_1_fun/dot_general | solution.py:38
  284.3 9.8 %conditional.2 = (f32[1152,1024]{1,0:T(8,128)}) conditional(s32[]{:T(128)} %convert_element_type.41, f32[1152,1024]{1,0:T(8,128)} %get-tuple-element.236, (s32[]{:T(128)}, s32[8]{0:T(128)S(1)}, bf16[1152,16384]{1,0:T(8,128)(2,1)}, bf16[8,1024,1024]{2,1,0:T(8,128)(2,1)}, f32[1152,1024]{1,0:T(8,128)}) %tuple.45), branch_computations={%region_1.0_spmd, %region_2.2_spmd} | conditional | flops 2417098752 | bytes 13893740 | solution.py:51
  284.3 0.6 dynamic_slice.18
  285.5 8.5 %convolution_add_fusion = f32[1152,1024]{1,0:T(8,128)} fusion(f32[1152,1024]{1,0:T(8,128)} %get-tuple-element.165, bf16[1152,16384]{1,0:T(8,128)(2,1)} %get-tuple-element.166, s32[]{:T(128)S(6)} %select_n.19, bf16[8,1024,1024]{2,1,0:T(8,128)(2,1)} %get-tuple-element.169, s32[]{:T(128)S(6)} %select_n.18), kind=kOutput, calls=%fused_computation | convolution fusion | flops 2417098752 | bytes 13893640 | tf_op jit(solution)/shard_map/while/body/eval_jaxpr/cond/branch_1_fun/dot_general | solution.py:38
  294.7 9.8 %conditional.2 = (f32[1152,1024]{1,0:T(8,128)}) conditional(s32[]{:T(128)} %convert_element_type.41, f32[1152,1024]{1,0:T(8,128)} %get-tuple-element.236, (s32[]{:T(128)}, s32[8]{0:T(128)S(1)}, bf16[1152,16384]{1,0:T(8,128)(2,1)}, bf16[8,1024,1024]{2,1,0:T(8,128)(2,1)}, f32[1152,1024]{1,0:T(8,128)}) %tuple.45), branch_computations={%region_1.0_spmd, %region_2.2_spmd} | conditional | flops 2417098752 | bytes 13893740 | solution.py:51
  294.7 0.6 dynamic_slice.18
  296.0 8.5 %convolution_add_fusion = f32[1152,1024]{1,0:T(8,128)} fusion(f32[1152,1024]{1,0:T(8,128)} %get-tuple-element.165, bf16[1152,16384]{1,0:T(8,128)(2,1)} %get-tuple-element.166, s32[]{:T(128)S(6)} %select_n.19, bf16[8,1024,1024]{2,1,0:T(8,128)(2,1)} %get-tuple-element.169, s32[]{:T(128)S(6)} %select_n.18), kind=kOutput, calls=%fused_computation | convolution fusion | flops 2417098752 | bytes 13893640 | tf_op jit(solution)/shard_map/while/body/eval_jaxpr/cond/branch_1_fun/dot_general | solution.py:38
  305.2 9.8 %conditional.2 = (f32[1152,1024]{1,0:T(8,128)}) conditional(s32[]{:T(128)} %convert_element_type.41, f32[1152,1024]{1,0:T(8,128)} %get-tuple-element.236, (s32[]{:T(128)}, s32[8]{0:T(128)S(1)}, bf16[1152,16384]{1,0:T(8,128)(2,1)}, bf16[8,1024,1024]{2,1,0:T(8,128)(2,1)}, f32[1152,1024]{1,0:T(8,128)}) %tuple.45), branch_computations={%region_1.0_spmd, %region_2.2_spmd} | conditional | flops 2417098752 | bytes 13893740 | solution.py:51
  305.2 0.6 dynamic_slice.18
  306.4 8.5 %convolution_add_fusion = f32[1152,1024]{1,0:T(8,128)} fusion(f32[1152,1024]{1,0:T(8,128)} %get-tuple-element.165, bf16[1152,16384]{1,0:T(8,128)(2,1)} %get-tuple-element.166, s32[]{:T(128)S(6)} %select_n.19, bf16[8,1024,1024]{2,1,0:T(8,128)(2,1)} %get-tuple-element.169, s32[]{:T(128)S(6)} %select_n.18), kind=kOutput, calls=%fused_computation | convolution fusion | flops 2417098752 | bytes 13893640 | tf_op jit(solution)/shard_map/while/body/eval_jaxpr/cond/branch_1_fun/dot_general | solution.py:38
  314.9 3.6 copy.11
  318.5 2.5 copy.12
  321.0 4.8 %reshape.14 = bf16[12,8,12,1024]{3,2,1,0:T(8,128)(2,1)} reshape(bf16[1152,1024]{1,0:T(8,128)(2,1)} %copy.12) | data formatting | bytes 4718592 | tf_op jit(solution)/shard_map/reshape | solution.py:18
  325.9 2.4 copy.13
  328.3 42.5 %all_to_all.5 = bf16[12,8,12,1024]{3,2,0,1:T(8,128)(2,1)S(1)} all-to-all(bf16[12,8,12,1024]{3,2,0,1:T(8,128)(2,1)S(1)} %copy.13), channel_id=1, replica_groups=mesh['occ'=8,'vir'=16] {'occ'}, dimensions={1} | all-to-all | bytes 4718592 | tf_op jit(solution)/shard_map/all_to_all | solution.py:19
  370.9 3.0 copy.14
  373.9 4.9 %reshape.15 = bf16[1152,1024]{1,0:T(8,128)(2,1)} reshape(bf16[12,8,12,1024]{3,2,1,0:T(8,128)(2,1)} %copy.14) | data formatting | bytes 4718592 | tf_op jit(solution)/shard_map/reshape | solution.py:20
  378.8 0.0 collective-permute-start
  378.8 52.9 %collective-permute-done = bf16[1152,1024]{1,0:T(8,128)(2,1)} collective-permute-done((bf16[1152,1024]{1,0:T(8,128)(2,1)}, bf16[1152,1024]{1,0:T(8,128)(2,1)}, u32[]{:S(2)}, u32[]{:S(2)}) %collective-permute-start) | collective-permute-done | bytes 2359328 | tf_op jit(solution)/shard_map/ppermute | solution.py:13
  431.7 4.6 %copy.15 = f32[1152,1024]{0,1:T(8,128)} copy(bf16[1152,1024]{1,0:T(8,128)(2,1)} %collective-permute-done) | data formatting | bytes 7077888 | tf_op jit(solution)/shard_map/convert_element_type | solution.py:56
  436.3 5.1 %copy.16 = f32[1152,32,32]{0,2,1:T(8,128)S(1)} copy(f32[1152,32,32]{0,1,2:T(8,128)} %bitcast.15) | data formatting | bytes 9437184 | tf_op jit(solution)/shard_map/convert_element_type | solution.py:56
  441.3 2.0 fusion.4
  443.3 4.3 copy.17
Async XLA Ops:
  6.5 224.8 %copy-start = (s32[1,8]{1,0:T(1,128)S(1)}, s32[1,8]{1,0:T(1,128)}, u32[]{:S(2)}) copy-start(s32[1,8]{1,0:T(1,128)} %param.10) | copy-start | bytes 100
  6.5 222.1 %all-gather.2.cloned.1.call-start = ((), (), s32[]{:S(2)}) async-start(), calls=%async_computation.1 | async-start | bytes 40108032 | tf_op jit(solution)/shard_map/all_gather | solution.py:42
  378.8 52.9 %collective-permute-start = (bf16[1152,1024]{1,0:T(8,128)(2,1)}, bf16[1152,1024]{1,0:T(8,128)(2,1)}, u32[]{:S(2)}, u32[]{:S(2)}) collective-permute-start(bf16[1152,1024]{1,0:T(8,128)(2,1)} %reshape.15), channel_id=1, source_target_pairs={{0,1},{1,0},{2,3},{3,2},{4,5},{5,4},{6,7},{7,6},{8,9},{9,8},{10,11... | collective-permute-start | bytes 7077896 | tf_op jit(solution)/shard_map/ppermute | solution.py:13
Sparse Core Ops, SparseCore 0:
  9.5 219.0 all-gather.1
where the time goes:
time: 457 us; the launch traced here: 454 us
  waiting for transfers between devices  275 us (60%)
  matrix products  68.2 us (15%)
  local copies, waits for them, and re-layouts  42.8 us (9%)
  blocking collectives  42.5 us (9%)
  between operations  13.4 us (3%)
  loops' own time  10.5 us (2%)
    all_gather x1, waiting for transfers between devices, on_device(): gathered = lax.all_gather(amplitudes, 'vir', axis=1, tiled=True)  221 us
    dot_general x8, matrix products, product(): lax.dot_general(col_tile, int_block, (((1,), (1,)), ((), ())), preferred_...  68.2 us
    ppermute x1, waiting for transfers between devices, swapped(): lax.ppermute(shard, axis, [(i, i ^ 1 << apart) for i in range(lax.axis_si...  52.9 us
    all_to_all x1, blocking collectives, reflect_rows(): lax.all_to_all(reshaped, 'occ', split_axis=1, concat_axis=1, tiled=True)  42.5 us
    convert_element_type x2, local copies, waits for them, and re-layouts, on_device(): summed = ladder.astype(jnp.float32) + mirrored.astype(jnp.float32)  9.62 us
  transfers between devices with their start and end apart: 2, of which 2 were waited for; matrix products, arithmetic and copies ran while one was open for 0% of the time, Pallas kernels for 0%

commit v1 on v0

v1 whole, which is shorter than its diff:
```python
import functools

import jax
import jax.numpy as jnp
from jax import lax
from jax.experimental import pallas as pl
from jax.experimental.pallas import tpu as pltpu
from jax.sharding import PartitionSpec as P

TW = 32
K = 1024
OCC = 8
OI = 12
BLK = OI * OI
NO = OCC * OI
BF = jnp.bfloat16
F32 = jnp.float32

HALF = ((2, 3, 4, 0), (6, 7, 5, 1))
CHUNKS = ((0, 1), (2,), (3,))


def half_of(v):
    return 0 if v % 4 in (1, 2) else 1


def permute(value, pairs, axis):
    return lax.ppermute(value, axis, pairs)


def pair_perm(value):
    return permute(value, [(v, v ^ 1) for v in range(16)], "vir")


def group_perm(value):
    return permute(value, [(v, v ^ 3) for v in range(16)], "vir")


def z_perm(value, step):
    return permute(value, [(v, (v + 4 * step) % 16) for v in range(16)], "vir")


def y_perm(value, step):
    return permute(value, [(o, (o + 2 * step) % 8) for o in range(8)], "occ")


def core_perm(value):
    return permute(value, [(o, o ^ 1) for o in range(8)], "occ")


def mirror_perm(value, pos):
    pairs = [(o * 16 + v, (o ^ HALF[half_of(v)][pos]) * 16 + v) for o in range(8) for v in range(16)]
    return permute(value, pairs, ("occ", "vir"))


def my_half():
    x = lax.rem(lax.axis_index("vir"), 4)
    return jnp.where((x == 1) | (x == 2), 0, 1)


def any_spec():
    return pl.BlockSpec(memory_space=pl.ANY)


LANES = 256


def split_kernel(a_ref, *refs):
    outs, wide, cut = refs[:-2], refs[-2], refs[-1]
    me = lax.axis_index("occ")
    half = my_half()
    wide[...] = a_ref[...].astype(F32)
    for owner in range(OCC):
        kk = owner ^ me
        for ii in range(OI):
            cut[kk, ii * OI:(ii + 1) * OI, :] = wide[ii * NO + owner * OI:ii * NO + (owner + 1) * OI, :]
    for hh in range(2):
        for chunk, members in enumerate(CHUNKS):
            for slot, pos in enumerate(members):
                rows = cut[HALF[hh][pos]].astype(BF)

                @pl.when(half == hh)
                def _():
                    outs[chunk][slot * BLK:(slot + 1) * BLK, :] = rows

                @pl.when(half != hh)
                def _():
                    outs[3 + chunk][slot * BLK:(slot + 1) * BLK, :] = rows


def split_rows(amplitudes):
    sizes = [len(members) * BLK for members in CHUNKS] * 2
    return pl.pallas_call(
        split_kernel,
        grid=(K // LANES,),
        in_specs=[pl.BlockSpec((OI * NO, LANES), lambda g: (0, g))],
        out_specs=[pl.BlockSpec((n, LANES), lambda g: (0, g)) for n in sizes],
        out_shape=[jax.ShapeDtypeStruct((n, K), BF) for n in sizes],
        scratch_shapes=[pltpu.VMEM((OI * NO, LANES), F32), pltpu.VMEM((OCC, BLK, LANES), F32)],
        name="split_rows",
    )(amplitudes)


def join_kernel(*refs):
    mine, mirror, other = refs[0:3], refs[3:7], refs[7:10]
    out, cut, wide = refs[10], refs[11], refs[12]
    me = lax.axis_index("occ")
    half = my_half()
    for chunk, members in enumerate(CHUNKS):
        for slot, pos in enumerate(members):
            own = mine[chunk][slot * BLK:(slot + 1) * BLK, :].astype(F32) + mirror[pos][...].astype(F32)
            got = other[chunk][slot * BLK:(slot + 1) * BLK, :].astype(F32)
            for hh in range(2):
                cut[HALF[hh][pos]] = jnp.where(half == hh, own, got)
    for owner in range(OCC):
        kk = owner ^ me
        for ii in range(OI):
            wide[ii * NO + owner * OI:ii * NO + (owner + 1) * OI, :] = cut[kk, ii * OI:(ii + 1) * OI, :]
    out[...] = wide[...].astype(BF)


def join_rows(mine, mirror, other):
    def spec(leading, n):
        if leading:
            return pl.BlockSpec((None, n, LANES), lambda g: (0, 0, g))
        return pl.BlockSpec((n, LANES), lambda g: (0, g))

    sizes = [len(members) * BLK for members in CHUNKS]
    return pl.pallas_call(
        join_kernel,
        grid=(K // LANES,),
        in_specs=[spec(True, n) for n in sizes] + [spec(True, BLK)] * 4 + [spec(False, n) for n in sizes],
        out_specs=pl.BlockSpec((OI * NO, LANES), lambda g: (0, g)),
        out_shape=jax.ShapeDtypeStruct((OI * NO, K), BF),
        scratch_shapes=[pltpu.VMEM((OCC, BLK, LANES), F32), pltpu.VMEM((OI * NO, LANES), F32)],
        name="join_rows",
    )(*mine, *mirror, *other)


NBUF = 3


def ladder_kernel(blocks, own_list, own_count, far, *refs):
    pieces, own_int, far_int = refs[0:16], refs[16], refs[17:33]
    swap_cols, swap_rows = refs[33], refs[34]
    ladder, mirrors = refs[35], refs[36:36 + blocks]
    acc, held, ints, cols, piece_sem, int_sem, col_sem = refs[36 + blocks:]
    v, o = lax.axis_index("vir"), lax.axis_index("occ")
    x, z = lax.rem(v, 4), lax.div(v, 4)
    y, c = lax.div(o, 2), lax.rem(o, 2)
    count0, count1 = own_count[0], far[8]
    total = count0 + count1

    def int_copies(item, start):
        slot = lax.rem(item, NBUF)

        def go(copy):
            copy.start() if start else copy.wait()

        first = item < count0
        if not start:
            go(pltpu.make_async_copy(own_int.at[0], ints.at[slot], int_sem.at[slot]))
            return

        @pl.when(first)
        def _():
            go(pltpu.make_async_copy(own_int.at[item], ints.at[slot], int_sem.at[slot]))

        s = item - count0
        dy = (lax.div(s, 2) - y) & 3
        dc = (s & 1) ^ c
        for rel in range(8):
            @pl.when(jnp.logical_not(first) & (dy * 2 + dc == rel))
            def _():
                for part in range(2):
                    go(pltpu.make_async_copy(
                        far_int[part * 8 + rel],
                        ints.at[slot, pl.ds(part * (K // 2), K // 2), :],
                        int_sem.at[slot]))

    copies = [pltpu.make_async_copy(pieces[q], held.at[q], piece_sem.at[q]) for q in range(16)]
    for ahead in range(NBUF - 1):
        @pl.when(ahead < total)
        def _():
            int_copies(jnp.int32(ahead), True)
    for copy in copies:
        copy.start()
    col_copy = pltpu.make_async_copy(swap_cols, cols, col_sem)
    col_copy.start()
    acc[...] = jnp.zeros_like(acc)
    for copy in copies:
        copy.wait()

    def step(item, carry):
        @pl.when(item + NBUF - 1 < total)
        def _():
            int_copies(item + NBUF - 1, True)

        first = item < count0
        s = jnp.where(first, item, item - count0)
        tile = jnp.where(first, own_list[s], far[s])
        side = jnp.where(first, 0, 1)
        flip = lax.rem(tile, 4) ^ x
        q = ((lax.div(tile, 4) - z) & 3) * 4 + (flip ^ lax.div(flip, 2))
        int_copies(item, False)
        acc[side] += lax.dot_general(
            held[q], ints[lax.rem(item, NBUF)], (((1,), (1,)), ((), ())), preferred_element_type=F32)
        return carry

    lax.fori_loop(0, total, step, 0)
    col_copy.wait()
    for side in range(2):
        rounded = acc[side].astype(BF)
        ladder[side] = rounded
        turned = jnp.dot(rounded, cols[...], preferred_element_type=F32).astype(BF)
        for b in range(blocks):
            mirrors[b][1 - side] = jnp.dot(
                swap_rows[...], turned[b * BLK:(b + 1) * BLK, :], preferred_element_type=F32).astype(BF)


def ladder_chunk(blocks, own_list, own_count, far, pieces, own_int, far_int, swap_cols, swap_rows):
    rows = blocks * BLK
    vmem = pl.BlockSpec(memory_space=pltpu.VMEM)
    outs = pl.pallas_call(
        functools.partial(ladder_kernel, blocks),
        grid_spec=pltpu.PrefetchScalarGridSpec(
            num_scalar_prefetch=3,
            grid=(),
            in_specs=[any_spec()] * 34 + [vmem],
            out_specs=[vmem] * (1 + blocks),
            scratch_shapes=[
                pltpu.VMEM((2, rows, K), F32),
                pltpu.VMEM((16, rows, K), BF),
                pltpu.VMEM((NBUF, K, K), BF),
                pltpu.VMEM((K, K), BF),
                pltpu.SemaphoreType.DMA((16,)),
                pltpu.SemaphoreType.DMA((NBUF,)),
                pltpu.SemaphoreType.DMA,
            ],
        ),
        out_shape=[jax.ShapeDtypeStruct((2, rows, K), BF)] + [jax.ShapeDtypeStruct((2, BLK, K), BF)] * blocks,
        compiler_params=pltpu.CompilerParams(vmem_limit_bytes=48 << 20),
    )(own_list, own_count, far, *pieces, own_int, *far_int, swap_cols, swap_rows)
    return outs[0], outs[1:]


def gather_chunk(own, sent):
    m = own
    n = pair_perm(sent)
    mg = group_perm(m)
    ng = group_perm(n)
    four = (m, n, mg, ng)
    up = [z_perm(t, 1) for t in four]
    down = [z_perm(t, -1) for t in four]
    m2 = z_perm(up[0], 1)
    n2 = z_perm(down[1], -1)
    two = [m2, n2, group_perm(m2), group_perm(n2)]
    return list(four) + down + two + up


def gather_integrals(blocks):
    mine = lax.dynamic_index_in_dim(blocks, lax.axis_index("occ"), 0, keepdims=False)
    halves = []
    for part in range(2):
        b = pair_perm(mine[part * (K // 2):(part + 1) * (K // 2)])
        up = y_perm(b, 1)
        down = y_perm(b, -1)
        far = y_perm(up, 1) if part == 0 else y_perm(down, -1)
        for t in (b, down, far, up):
            halves += [t, core_perm(t)]
    return halves


def on_device(amplitudes, integrals, cd_tiles, cd_count):
    listed = cd_tiles[0]
    blocks = integrals[0]
    far = pair_perm(jnp.concatenate([listed, cd_count, jnp.zeros((7,), jnp.int32)]))
    col = jnp.arange(K, dtype=jnp.int32)
    swap_cols = (col[:, None] == ((col % TW) * TW + col // TW)[None, :]).astype(BF)
    row = jnp.arange(BLK, dtype=jnp.int32)
    swap_rows = (row[:, None] == ((row % OI) * OI + row // OI)[None, :]).astype(BF)
    split = split_rows(amplitudes)
    far_int = gather_integrals(blocks)
    mine, mirror, other = [], [], []
    for chunk, members in enumerate(CHUNKS):
        pieces = gather_chunk(split[chunk], split[3 + chunk])
        ladder, mirrors = ladder_chunk(
            len(members), listed, cd_count, far, pieces, blocks, far_int, swap_cols, swap_rows)
        got = [mirror_perm(mirrors[slot], pos) for slot, pos in enumerate(members)]
        there = jnp.concatenate(
            [ladder[1, s * BLK:(s + 1) * BLK].astype(F32) + got[s][1].astype(F32) for s in range(len(members))], 0)
        other.append(pair_perm(there.astype(BF)))
        mine.append(ladder)
        mirror += got
    return join_rows(mine, mirror, other)


def solution(mesh):
    placed = (P("occ", "vir"), P("vir", None, None, None), P("vir", None), P("vir"))
    return jax.shard_map(
        on_device, mesh=mesh, in_specs=placed, out_specs=P("occ", "vir"), check_vma=False
    )
```

time: 457 us -> 319 us (0.70)
  waiting for transfers between devices: 275 us -> 161 us
  starting transfers between devices: 0.01 us -> 86.8 us
  matrix products: 68.2 us -> 0 us
  Pallas kernels: 0 us -> 59.9 us
  blocking collectives: 42.5 us -> 0 us
  local copies, waits for them, and re-layouts: 42.8 us -> 4.15 us
  between operations: 13.4 us -> 1.24 us
  loops' own time: 10.5 us -> 0 us
    all_gather x1 -> x0, waiting for transfers between devices: 221 us -> none  [on_device(): gathered = lax.all_gather(amplitudes, 'vir', axis=1, tiled=True)]
    ppermute x1 -> x69, waiting for transfers between devices: 52.9 us -> 161 us  [permute(): return lax.ppermute(value, axis, pairs)]
    ppermute x1 -> x69, starting transfers between devices: 0.01 us -> 86.8 us  [permute(): return lax.ppermute(value, axis, pairs)]
    dot_general x8 -> x0, matrix products: 68.2 us -> none  [product(): lax.dot_general(col_tile, int_block, (((1,), (1,)), ((), ())), preferred_...]
    pallas_call x0 -> x5, Pallas kernels: none -> 59.9 us  [the longest x3 50.8 us: ladder_chunk(): pl.pallas_call(functools.partial(ladder_kernel, blocks), grid_spec=pltpu....]
    all_to_all x1 -> x0, blocking collectives: 42.5 us -> none  [reflect_rows(): lax.all_to_all(reshaped, 'occ', split_axis=1, concat_axis=1, tiled=True)]
    convert_element_type x4 -> x0, local copies, waits for them, and re-layouts: 16.4 us -> none  [the longest x2 9.62 us: on_device(): summed = ladder.astype(jnp.float32) + mirrored.astype(jnp.float32)]
    reshape x3 -> x0, local copies, waits for them, and re-layouts: 12.2 us -> none  [the longest x2 7.29 us: reflect_rows(): reshaped = matrix.reshape(OCC_DEV, occ_devices, OCC_DEV, matrix.shape[1])]
  transfers between devices with their start and end apart: 2 -> 69, of which waited for: 2 -> 25; matrix products, arithmetic and copies ran while one was open for 0% -> 1% of each run, Pallas kernels for 0% -> 16%
where the time goes in v1:
time: 319 us; the launch traced here: 316 us
  waiting for transfers between devices  161 us (50%)
  starting transfers between devices  86.8 us (27%)
  Pallas kernels  59.9 us (19%)
  local copies, waits for them, and re-layouts  4.15 us (1%)
    ppermute x69, waiting for transfers between devices, permute(): return lax.ppermute(value, axis, pairs)  161 us
    ppermute x69, starting transfers between devices, permute(): return lax.ppermute(value, axis, pairs)  86.8 us
    pallas_call x3, Pallas kernels, ladder_chunk(): pl.pallas_call(functools.partial(ladder_kernel, blocks), grid_spec=pltpu....  50.8 us
  transfers between devices with their start and end apart: 69, of which 25 were waited for; matrix products, arithmetic and copies ran while one was open for 1% of the time, Pallas kernels for 16%

profile of v1, /device:TPU:38, one launch (start us, length us, event | category | flops | bytes accessed | tf_op | source)
XLA Modules:
  0.0 315.8 jit_solution(15382056402536634582)
XLA Ops:
  0.0 4.4 %split_rows.1 = (bf16[288,1024]{1,0:T(8,128)(2,1)}, bf16[144,1024]{1,0:T(8,128)(2,1)}, bf16[144,1024]{1,0:T(8,128)(2,1)}, bf16[288,1024]{1,0:T(8,128)(2,1)}, bf1...) custom-call(bf16[1152,1024]{1,0:T(8,128)(2,1)} %a_ref.1), custom_call_target="tpu_custom_call" | custom-call | tf_op jit(solution)/shard_map/split_rows/pallas_call | solution.py:93
  6.5 1.9 collective-permute-start.39
  9.2 4.2 %collective-permute-done.far = s32[16]{0:T(128)S(1)} collective-permute-done((s32[16]{0:T(128)S(1)}, s32[16]{0:T(128)S(1)}, u32[]{:S(2)}, u32[]{:S(2)}) %collective-permute-start) | collective-permute-done | bytes 96 | tf_op jit(solution)/shard_map/ppermute | solution.py:28
  15.5 2.1 collective-permute-start.50
  20.3 3.3 %collective-permute-done.47.refs_1_ = bf16[144,1024]{1,0:T(8,128)(2,1)S(1)} collective-permute-done((bf16[144,1024]{1,0:T(8,128)(2,1)}, bf16[144,1024]{1,0:T(8,128)(2,1)S(1)}, u32[]{:S(2)}, u32[]{:S(2)}) %collective-permute-start.47) | collective-permute-done | bytes 294944 | tf_op jit(solution)/shard_map/ppermute | solution.py:28
  23.6 2.0 collective-permute-done.48.refs_2_
  25.6 1.9 collective-permute-start.8
  29.2 13.8 %collective-permute-done.54.refs_12_ = bf16[144,1024]{1,0:T(8,128)(2,1)S(1)} collective-permute-done((bf16[144,1024]{1,0:T(8,128)(2,1)}, bf16[144,1024]{1,0:T(8,128)(2,1)S(1)}, u32[]{:S(2)}, u32[]{:S(2)}) %collective-permute-start.54) | collective-permute-done | bytes 294944 | tf_op jit(solution)/shard_map/ppermute | solution.py:28
  44.0 2.9 collective-permute-start.36
  46.9 1.8 dynamic-slice_bitcast_fusion
  49.8 2.0 collective-permute-start.40
  54.4 2.7 collective-permute-done.37.refs_6_
  57.0 1.7 collective-permute-start.49
  60.6 2.1 collective-permute-done.44.refs_13_
  64.2 4.7 %collective-permute-done.45.refs_14_ = bf16[144,1024]{1,0:T(8,128)(2,1)S(1)} collective-permute-done((bf16[144,1024]{1,0:T(8,128)(2,1)S(1)}, bf16[144,1024]{1,0:T(8,128)(2,1)S(1)}, u32[]{:S(2)}, u32[]{:S(2)}) %collective-permute-start.45) | collective-permute-done | bytes 294944 | tf_op jit(solution)/shard_map/ppermute | solution.py:28
  69.2 2.2 collective-permute-start.55
  71.4 2.0 collective-permute-start.59
  73.3 3.8 %collective-permute-done.52.refs_6_ = bf16[144,1024]{1,0:T(8,128)(2,1)S(1)} collective-permute-done((bf16[144,1024]{1,0:T(8,128)(2,1)S(1)}, bf16[144,1024]{1,0:T(8,128)(2,1)S(1)}, u32[]{:S(2)}, u32[]{:S(2)}) %collective-permute-start.52) | collective-permute-done | bytes 294944 | tf_op jit(solution)/shard_map/ppermute | solution.py:28
  77.1 2.4 collective-permute-start.60
  79.5 2.7 collective-permute-start.3
  83.7 5.0 %collective-permute-done.60.refs_14_ = bf16[144,1024]{1,0:T(8,128)(2,1)S(1)} collective-permute-done((bf16[144,1024]{1,0:T(8,128)(2,1)S(1)}, bf16[144,1024]{1,0:T(8,128)(2,1)S(1)}, u32[]{:S(2)}, u32[]{:S(2)}) %collective-permute-start.60) | collective-permute-done | bytes 294944 | tf_op jit(solution)/shard_map/ppermute | solution.py:28
  93.0 5.6 %collective-permute-done.5.refs_5_ = bf16[288,1024]{1,0:T(8,128)(2,1)S(1)} collective-permute-done((bf16[288,1024]{1,0:T(8,128)(2,1)S(1)}, bf16[288,1024]{1,0:T(8,128)(2,1)S(1)}, u32[]{:S(2)}, u32[]{:S(2)}) %collective-permute-start.5) | collective-permute-done | bytes 589856 | tf_op jit(solution)/shard_map/ppermute | solution.py:28
  99.9 11.4 %collective-permute-done.6.refs_6_ = bf16[288,1024]{1,0:T(8,128)(2,1)S(1)} collective-permute-done((bf16[288,1024]{1,0:T(8,128)(2,1)S(1)}, bf16[288,1024]{1,0:T(8,128)(2,1)S(1)}, u32[]{:S(2)}, u32[]{:S(2)}) %collective-permute-start.6) | collective-permute-done | bytes 589856 | tf_op jit(solution)/shard_map/ppermute | solution.py:28
  112.5 2.5 collective-permute-start.11
  115.0 4.0 %collective-permute-done.13.refs_13_ = bf16[288,1024]{1,0:T(8,128)(2,1)S(1)} collective-permute-done((bf16[288,1024]{1,0:T(8,128)(2,1)S(1)}, bf16[288,1024]{1,0:T(8,128)(2,1)S(1)}, u32[]{:S(2)}, u32[]{:S(2)}) %collective-permute-start.13) | collective-permute-done | bytes 589856 | tf_op jit(solution)/shard_map/ppermute | solution.py:28
  119.8 9.3 %collective-permute-done.14.refs_14_ = bf16[288,1024]{1,0:T(8,128)(2,1)} collective-permute-done((bf16[288,1024]{1,0:T(8,128)(2,1)S(1)}, bf16[288,1024]{1,0:T(8,128)(2,1)}, u32[]{:S(2)}, u32[]{:S(2)}) %collective-permute-start.14) | collective-permute-done | bytes 589856 | tf_op jit(solution)/shard_map/ppermute | solution.py:28
  129.1 3.0 collective-permute-start.18
  132.2 3.2 %collective-permute-start.26 = (bf16[512,1024]{1,0:T(8,128)(2,1)S(1)}, bf16[512,1024]{1,0:T(8,128)(2,1)S(1)}, u32[]{:S(2)}, u32[]{:S(2)}) collective-permute-start(bf16[512,1024]{1,0:T(8,128)(2,1)S(1)} %collective-permute-done.24.refs_25_), channel_id=1, source_target_pairs={{0,96},{16,112},{32,0},{48,16},{64,32},{80,48},{96,64},{112,80},{1... | collective-permute-start | bytes 3145736 | tf_op jit(solution)/shard_map/ppermute | solution.py:28
  137.1 18.6 %collective-permute-done.18.refs_19_ = bf16[512,1024]{1,0:T(8,128)(2,1)S(1)} collective-permute-done((bf16[512,1024]{1,0:T(8,128)(2,1)S(1)}, bf16[512,1024]{1,0:T(8,128)(2,1)S(1)}, u32[]{:S(2)}, u32[]{:S(2)}) %collective-permute-start.18) | collective-permute-done | bytes 1048608 | tf_op jit(solution)/shard_map/ppermute | solution.py:28
  155.7 3.7 %collective-permute-done.20.refs_23_ = bf16[512,1024]{1,0:T(8,128)(2,1)S(1)} collective-permute-done((bf16[512,1024]{1,0:T(8,128)(2,1)S(1)}, bf16[512,1024]{1,0:T(8,128)(2,1)S(1)}, u32[]{:S(2)}, u32[]{:S(2)}) %collective-permute-start.20) | collective-permute-done | bytes 1048608 | tf_op jit(solution)/shard_map/ppermute | solution.py:28
  159.4 18.3 %collective-permute-done.26.refs_27_ = bf16[512,1024]{1,0:T(8,128)(2,1)S(1)} collective-permute-done((bf16[512,1024]{1,0:T(8,128)(2,1)S(1)}, bf16[512,1024]{1,0:T(8,128)(2,1)S(1)}, u32[]{:S(2)}, u32[]{:S(2)}) %collective-permute-start.26) | collective-permute-done | bytes 1048608 | tf_op jit(solution)/shard_map/ppermute | solution.py:28
  177.7 3.7 %collective-permute-start.28 = (bf16[512,1024]{1,0:T(8,128)(2,1)S(1)}, bf16[512,1024]{1,0:T(8,128)(2,1)S(1)}, u32[]{:S(2)}, u32[]{:S(2)}) collective-permute-start(bf16[512,1024]{1,0:T(8,128)(2,1)S(1)} %collective-permute-done.26.refs_27_), channel_id=1, source_target_pairs={{0,96},{16,112},{32,0},{48,16},{64,32},{80,48},{96,64},{112,80},{1... | collective-permute-start | bytes 3145736 | tf_op jit(solution)/shard_map/ppermute | solution.py:28
  181.4 1.7 collective-permute-start.12
  183.2 14.0 %collective-permute-done.12.refs_11_ = bf16[288,1024]{1,0:T(8,128)(2,1)S(1)} collective-permute-done((bf16[288,1024]{1,0:T(8,128)(2,1)S(1)}, bf16[288,1024]{1,0:T(8,128)(2,1)S(1)}, u32[]{:S(2)}, u32[]{:S(2)}) %collective-permute-start.12) | collective-permute-done | bytes 589856 | tf_op jit(solution)/shard_map/ppermute | solution.py:28
  197.7 5.9 %collective-permute-done.21.refs_21_ = bf16[512,1024]{1,0:T(8,128)(2,1)S(1)} collective-permute-done((bf16[512,1024]{1,0:T(8,128)(2,1)S(1)}, bf16[512,1024]{1,0:T(8,128)(2,1)S(1)}, u32[]{:S(2)}, u32[]{:S(2)}) %collective-permute-start.21) | collective-permute-done | bytes 1048608 | tf_op jit(solution)/shard_map/ppermute | solution.py:28
  204.2 2.2 fusion.refs_33_
  210.1 1.8 collective-permute-start.42
  212.0 2.3 collective-permute-start.53
  214.5 18.6 %shard_map.46 = (bf16[2,288,1024]{2,1,0:T(8,128)(2,1)}, bf16[2,144,1024]{2,1,0:T(8,128)(2,1)S(1)}, bf16[2,144,1024]{2,1,0:T(8,128)(2,1)S(1)}) custom-call(s32[8]{0:T(128)S(1)} %bitcast.15, s32[1]{0:T(128)S(6)} %copy.5.own_count, s32[16]{0:T(128)S(1)} %collective-permute-done.far, bf16[288,1024]{1,0:T(8,128)(2,1)S(1)} %copy-done.2, ...), custom_call_target="tpu_custom_call" | custom-call | tf_op jit(solution)/shard_map/pallas_call | solution.py:224
  234.9 3.2 %collective-permute-start.62 = (bf16[2,144,1024]{2,1,0:T(8,128)(2,1)S(1)}, bf16[2,144,1024]{2,1,0:T(8,128)(2,1)S(1)}, u32[]{:S(2)}, u32[]{:S(2)}) collective-permute-start(bf16[2,144,1024]{2,1,0:T(8,128)(2,1)S(1)} %get-tuple-element.27), channel_id=1, source_target_pairs={{0,96},{1,33},{2,34},{3,99},{4,100},{5,37},{6,38},{7,103},{8,104},... | collective-permute-start | bytes 1769480 | tf_op jit(solution)/shard_map/ppermute | solution.py:28
  238.1 2.3 collective-permute-start.57
  243.6 16.3 %shard_map.47 = (bf16[2,144,1024]{2,1,0:T(8,128)(2,1)S(1)}, bf16[2,144,1024]{2,1,0:T(8,128)(2,1)S(1)}) custom-call(s32[8]{0:T(128)S(1)} %bitcast.16, s32[1]{0:T(128)S(6)} %copy.5.own_count, s32[16]{0:T(128)S(1)} %collective-permute-done.far, bf16[144,1024]{1,0:T(8,128)(2,1)S(1)} %copy-done.4, bf16[144,1024]{1,0:T(8,128)(2,1)S(1)} %collective-permute-done.32.refs_1_, ...), custom_call_target="tpu_custom_call" | custom-call | tf_op jit(solution)/shard_map/pallas_call | solution.py:224
  260.1 15.9 %shard_map.48 = (bf16[2,144,1024]{2,1,0:T(8,128)(2,1)S(1)}, bf16[2,144,1024]{2,1,0:T(8,128)(2,1)S(1)}) custom-call(s32[8]{0:T(128)S(1)} %bitcast.17, s32[1]{0:T(128)S(6)} %copy.5.own_count, s32[16]{0:T(128)S(1)} %collective-permute-done.far, bf16[144,1024]{1,0:T(8,128)(2,1)S(1)} %copy-done.3, bf16[144,1024]{1,0:T(8,128)(2,1)S(1)} %collective-permute-done.47.refs_1_, ...), custom_call_target="tpu_custom_call" | custom-call | tf_op jit(solution)/shard_map/pallas_call | solution.py:224
  276.0 5.2 %collective-permute-start.65 = (bf16[2,144,1024]{2,1,0:T(8,128)(2,1)S(1)}, bf16[2,144,1024]{2,1,0:T(8,128)(2,1)S(1)}, u32[]{:S(2)}, u32[]{:S(2)}) collective-permute-start(bf16[2,144,1024]{2,1,0:T(8,128)(2,1)S(1)} %get-tuple-element.30), channel_id=1, source_target_pairs={{0,16},{1,1},{2,2},{3,19},{4,20},{5,5},{6,6},{7,23},{8,24},{9,9},{... | collective-permute-start | bytes 1769480 | tf_op jit(solution)/shard_map/ppermute | solution.py:28
  281.7 2.1 collective-permute-start.67
  284.0 20.1 %collective-permute-done.67.refs_8_ = bf16[144,1024]{1,0:T(8,128)(2,1)S(1)} collective-permute-done((bf16[144,1024]{1,0:T(8,128)(2,1)S(1)}, bf16[144,1024]{1,0:T(8,128)(2,1)S(1)}, u32[]{:S(2)}, u32[]{:S(2)}) %collective-permute-start.67) | collective-permute-done | bytes 294944 | tf_op jit(solution)/shard_map/ppermute | solution.py:28
  304.1 5.4 %collective-permute-done.68.refs_9_ = bf16[144,1024]{1,0:T(8,128)(2,1)S(1)} collective-permute-done((bf16[144,1024]{1,0:T(8,128)(2,1)S(1)}, bf16[144,1024]{1,0:T(8,128)(2,1)S(1)}, u32[]{:S(2)}, u32[]{:S(2)}) %collective-permute-start.68) | collective-permute-done | bytes 294944 | tf_op jit(solution)/shard_map/ppermute | solution.py:28
  311.0 4.8 %join_rows.1 = bf16[1152,1024]{1,0:T(8,128)(2,1)} custom-call(bf16[2,288,1024]{2,1,0:T(8,128)(2,1)} %get-tuple-element.20.refs_0_, bf16[2,144,1024]{2,1,0:T(8,128)(2,1)} %copy-done, bf16[2,144,1024]{2,1,0:T(8,128)(2,1)} %copy-done.1, bf16[2,144,1024]{2,1,0:T(8,128)(2,1)} %copy-done.27, bf16[2,144,1024]{2,1,0:T(8,128)(2,1)} %copy-done.28, ...), custom_call_target="tpu_custom_call" | custom-call | tf_op jit(solution)/shard_map/join_rows/pallas_call | solution.py:129
  (184 shorter events, 40.2 us)
Async XLA Ops:
  6.5 11.9 %collective-permute-start.39 = (bf16[144,1024]{1,0:T(8,128)(2,1)}, bf16[144,1024]{1,0:T(8,128)(2,1)S(1)}, u32[]{:S(2)}, u32[]{:S(2)}) collective-permute-start(bf16[144,1024]{1,0:T(8,128)(2,1)} %get-tuple-element.21.refs_0_), channel_id=1, source_target_pairs={{0,4},{1,5},{2,6},{3,7},{4,8},{5,9},{6,10},{7,11},{8,12},{9,13},{1... | collective-permute-start | bytes 884744 | tf_op jit(solution)/shard_map/ppermute | solution.py:28
  14.3 11.3 %collective-permute-start.48 = (bf16[144,1024]{1,0:T(8,128)(2,1)}, bf16[144,1024]{1,0:T(8,128)(2,1)S(1)}, u32[]{:S(2)}, u32[]{:S(2)}) collective-permute-start(bf16[144,1024]{1,0:T(8,128)(2,1)} %get-tuple-element.24.refs_0_), channel_id=1, source_target_pairs={{0,3},{1,2},{2,1},{3,0},{4,7},{5,6},{6,5},{7,4},{8,11},{9,10},{10,... | collective-permute-start | bytes 884744 | tf_op jit(solution)/shard_map/ppermute | solution.py:28
  15.5 12.1 %collective-permute-start.50 = (bf16[144,1024]{1,0:T(8,128)(2,1)}, bf16[144,1024]{1,0:T(8,128)(2,1)S(1)}, u32[]{:S(2)}, u32[]{:S(2)}) collective-permute-start(bf16[144,1024]{1,0:T(8,128)(2,1)} %get-tuple-element.24.refs_0_), channel_id=1, source_target_pairs={{0,12},{1,13},{2,14},{3,15},{4,0},{5,1},{6,2},{7,3},{8,4},{9,5},{1... | collective-permute-start | bytes 884744 | tf_op jit(solution)/shard_map/ppermute | solution.py:28
  17.6 26.4 %collective-permute-start.1 = (bf16[288,1024]{1,0:T(8,128)(2,1)}, bf16[288,1024]{1,0:T(8,128)(2,1)S(1)}, u32[]{:S(2)}, u32[]{:S(2)}) collective-permute-start(bf16[288,1024]{1,0:T(8,128)(2,1)} %get-tuple-element.19), channel_id=1, source_target_pairs={{0,1},{1,0},{2,3},{3,2},{4,5},{5,4},{6,7},{7,6},{8,9},{9,8},{10,11... | collective-permute-start | bytes 1769480 | tf_op jit(solution)/shard_map/ppermute | solution.py:28
  19.1 29.6 %collective-permute-start.2 = (bf16[288,1024]{1,0:T(8,128)(2,1)}, bf16[288,1024]{1,0:T(8,128)(2,1)S(1)}, u32[]{:S(2)}, u32[]{:S(2)}) collective-permute-start(bf16[288,1024]{1,0:T(8,128)(2,1)} %get-tuple-element.18.refs_0_), channel_id=1, source_target_pairs={{0,3},{1,2},{2,1},{3,0},{4,7},{5,6},{6,5},{7,4},{8,11},{9,10},{10,... | collective-permute-start | bytes 1769480 | tf_op jit(solution)/shard_map/ppermute | solution.py:28
  23.6 26.2 %collective-permute-start.4 = (bf16[288,1024]{1,0:T(8,128)(2,1)}, bf16[288,1024]{1,0:T(8,128)(2,1)S(1)}, u32[]{:S(2)}, u32[]{:S(2)}) collective-permute-start(bf16[288,1024]{1,0:T(8,128)(2,1)} %get-tuple-element.18.refs_0_), channel_id=1, source_target_pairs={{0,12},{1,13},{2,14},{3,15},{4,0},{5,1},{6,2},{7,3},{8,4},{9,5},{1... | collective-permute-start | bytes 1769480 | tf_op jit(solution)/shard_map/ppermute | solution.py:28
  25.6 24.2 %collective-permute-start.8 = (bf16[288,1024]{1,0:T(8,128)(2,1)}, bf16[288,1024]{1,0:T(8,128)(2,1)}, u32[]{:S(2)}, u32[]{:S(2)}) collective-permute-start(bf16[288,1024]{1,0:T(8,128)(2,1)} %get-tuple-element.18.refs_0_), channel_id=1, source_target_pairs={{0,4},{1,5},{2,6},{3,7},{4,8},{5,9},{6,10},{7,11},{8,12},{9,13},{1... | collective-permute-start | bytes 1769480 | tf_op jit(solution)/shard_map/ppermute | solution.py:28
  27.5 15.4 %collective-permute-start.54 = (bf16[144,1024]{1,0:T(8,128)(2,1)}, bf16[144,1024]{1,0:T(8,128)(2,1)S(1)}, u32[]{:S(2)}, u32[]{:S(2)}) collective-permute-start(bf16[144,1024]{1,0:T(8,128)(2,1)} %get-tuple-element.24.refs_0_), channel_id=1, source_target_pairs={{0,4},{1,5},{2,6},{3,7},{4,8},{5,9},{6,10},{7,11},{8,12},{9,13},{1... | collective-permute-start | bytes 884744 | tf_op jit(solution)/shard_map/ppermute | solution.py:28
  48.7 41.3 %collective-permute-start.16 = (bf16[512,1024]{1,0:T(8,128)(2,1)S(1)}, bf16[512,1024]{1,0:T(8,128)(2,1)S(1)}, u32[]{:S(2)}, u32[]{:S(2)}) collective-permute-start(bf16[512,1024]{1,0:T(8,128)(2,1)S(1)} %get-tuple-element.32), channel_id=1, source_target_pairs={{0,1},{1,0},{2,3},{3,2},{4,5},{5,4},{6,7},{7,6},{8,9},{9,8},{10,11... | collective-permute-start | bytes 3145736 | tf_op jit(solution)/shard_map/ppermute | solution.py:28
  53.2 15.6 %collective-permute-start.45 = (bf16[144,1024]{1,0:T(8,128)(2,1)S(1)}, bf16[144,1024]{1,0:T(8,128)(2,1)S(1)}, u32[]{:S(2)}, u32[]{:S(2)}) collective-permute-start(bf16[144,1024]{1,0:T(8,128)(2,1)S(1)} %collective-permute-done.33.refs_2_), channel_id=1, source_target_pairs={{0,4},{1,5},{2,6},{3,7},{4,8},{5,9},{6,10},{7,11},{8,12},{9,13},{1... | collective-permute-start | bytes 884744 | tf_op jit(solution)/shard_map/ppermute | solution.py:28
  57.0 12.2 %collective-permute-start.49 = (bf16[144,1024]{1,0:T(8,128)(2,1)S(1)}, bf16[144,1024]{1,0:T(8,128)(2,1)S(1)}, u32[]{:S(2)}, u32[]{:S(2)}) collective-permute-start(bf16[144,1024]{1,0:T(8,128)(2,1)S(1)} %collective-permute-done.47.refs_1_), channel_id=1, source_target_pairs={{0,3},{1,2},{2,1},{3,0},{4,7},{5,6},{6,5},{7,4},{8,11},{9,10},{10,... | collective-permute-start | bytes 884744 | tf_op jit(solution)/shard_map/ppermute | solution.py:28
  59.5 31.3 %collective-permute-start.24 = (bf16[512,1024]{1,0:T(8,128)(2,1)S(1)}, bf16[512,1024]{1,0:T(8,128)(2,1)S(1)}, u32[]{:S(2)}, u32[]{:S(2)}) collective-permute-start(bf16[512,1024]{1,0:T(8,128)(2,1)S(1)} %get-tuple-element.31), channel_id=1, source_target_pairs={{0,1},{1,0},{2,3},{3,2},{4,5},{5,4},{6,7},{7,6},{8,9},{9,8},{10,11... | collective-permute-start | bytes 3145736 | tf_op jit(solution)/shard_map/ppermute | solution.py:28
  77.1 11.6 %collective-permute-start.60 = (bf16[144,1024]{1,0:T(8,128)(2,1)S(1)}, bf16[144,1024]{1,0:T(8,128)(2,1)S(1)}, u32[]{:S(2)}, u32[]{:S(2)}) collective-permute-start(bf16[144,1024]{1,0:T(8,128)(2,1)S(1)} %collective-permute-done.48.refs_2_), channel_id=1, source_target_pairs={{0,4},{1,5},{2,6},{3,7},{4,8},{5,9},{6,10},{7,11},{8,12},{9,13},{1... | collective-permute-start | bytes 884744 | tf_op jit(solution)/shard_map/ppermute | solution.py:28
  79.5 12.9 %collective-permute-start.3 = (bf16[288,1024]{1,0:T(8,128)(2,1)S(1)}, bf16[288,1024]{1,0:T(8,128)(2,1)S(1)}, u32[]{:S(2)}, u32[]{:S(2)}) collective-permute-start(bf16[288,1024]{1,0:T(8,128)(2,1)S(1)} %collective-permute-done.1.refs_1_), channel_id=1, source_target_pairs={{0,3},{1,2},{2,1},{3,0},{4,7},{5,6},{6,5},{7,4},{8,11},{9,10},{10,... | collective-permute-start | bytes 1769480 | tf_op jit(solution)/shard_map/ppermute | solution.py:28
  82.4 16.2 %collective-permute-start.5 = (bf16[288,1024]{1,0:T(8,128)(2,1)S(1)}, bf16[288,1024]{1,0:T(8,128)(2,1)S(1)}, u32[]{:S(2)}, u32[]{:S(2)}) collective-permute-start(bf16[288,1024]{1,0:T(8,128)(2,1)S(1)} %collective-permute-done.1.refs_1_), channel_id=1, source_target_pairs={{0,12},{1,13},{2,14},{3,15},{4,0},{5,1},{6,2},{7,3},{8,4},{9,5},{1... | collective-permute-start | bytes 1769480 | tf_op jit(solution)/shard_map/ppermute | solution.py:28
  88.7 22.5 %collective-permute-start.6 = (bf16[288,1024]{1,0:T(8,128)(2,1)S(1)}, bf16[288,1024]{1,0:T(8,128)(2,1)S(1)}, u32[]{:S(2)}, u32[]{:S(2)}) collective-permute-start(bf16[288,1024]{1,0:T(8,128)(2,1)S(1)} %collective-permute-done.2.refs_2_), channel_id=1, source_target_pairs={{0,12},{1,13},{2,14},{3,15},{4,0},{5,1},{6,2},{7,3},{8,4},{9,5},{1... | collective-permute-start | bytes 1769480 | tf_op jit(solution)/shard_map/ppermute | solution.py:28
  90.0 22.5 %collective-permute-start.9 = (bf16[288,1024]{1,0:T(8,128)(2,1)}, bf16[288,1024]{1,0:T(8,128)(2,1)S(1)}, u32[]{:S(2)}, u32[]{:S(2)}) collective-permute-start(bf16[288,1024]{1,0:T(8,128)(2,1)} %collective-permute-done.8.refs_12_), channel_id=1, source_target_pairs={{0,4},{1,5},{2,6},{3,7},{4,8},{5,9},{6,10},{7,11},{8,12},{9,13},{1... | collective-permute-start | bytes 1769480 | tf_op jit(solution)/shard_map/ppermute | solution.py:28
  90.8 28.3 %collective-permute-start.13 = (bf16[288,1024]{1,0:T(8,128)(2,1)S(1)}, bf16[288,1024]{1,0:T(8,128)(2,1)S(1)}, u32[]{:S(2)}, u32[]{:S(2)}) collective-permute-start(bf16[288,1024]{1,0:T(8,128)(2,1)S(1)} %collective-permute-done.1.refs_1_), channel_id=1, source_target_pairs={{0,4},{1,5},{2,6},{3,7},{4,8},{5,9},{6,10},{7,11},{8,12},{9,13},{1... | collective-permute-start | bytes 1769480 | tf_op jit(solution)/shard_map/ppermute | solution.py:28
  92.4 36.7 %collective-permute-start.14 = (bf16[288,1024]{1,0:T(8,128)(2,1)S(1)}, bf16[288,1024]{1,0:T(8,128)(2,1)}, u32[]{:S(2)}, u32[]{:S(2)}) collective-permute-start(bf16[288,1024]{1,0:T(8,128)(2,1)S(1)} %collective-permute-done.2.refs_2_), channel_id=1, source_target_pairs={{0,4},{1,5},{2,6},{3,7},{4,8},{5,9},{6,10},{7,11},{8,12},{9,13},{1... | collective-permute-start | bytes 1769480 | tf_op jit(solution)/shard_map/ppermute | solution.py:28
  98.6 30.5 %collective-permute-start.7 = (bf16[288,1024]{1,0:T(8,128)(2,1)S(1)}, bf16[288,1024]{1,0:T(8,128)(2,1)S(1)}, u32[]{:S(2)}, u32[]{:S(2)}) collective-permute-start(bf16[288,1024]{1,0:T(8,128)(2,1)S(1)} %collective-permute-done.3.refs_3_), channel_id=1, source_target_pairs={{0,12},{1,13},{2,14},{3,15},{4,0},{5,1},{6,2},{7,3},{8,4},{9,5},{1... | collective-permute-start | bytes 1769480 | tf_op jit(solution)/shard_map/ppermute | solution.py:28
  111.3 20.9 %collective-permute-start.10 = (bf16[288,1024]{1,0:T(8,128)(2,1)S(1)}, bf16[288,1024]{1,0:T(8,128)(2,1)S(1)}, u32[]{:S(2)}, u32[]{:S(2)}) collective-permute-start(bf16[288,1024]{1,0:T(8,128)(2,1)S(1)} %collective-permute-done.5.refs_5_), channel_id=1, source_target_pairs={{0,12},{1,13},{2,14},{3,15},{4,0},{5,1},{6,2},{7,3},{8,4},{9,5},{1... | collective-permute-start | bytes 1769480 | tf_op jit(solution)/shard_map/ppermute | solution.py:28
  112.5 19.6 %collective-permute-start.11 = (bf16[288,1024]{1,0:T(8,128)(2,1)S(1)}, bf16[288,1024]{1,0:T(8,128)(2,1)S(1)}, u32[]{:S(2)}, u32[]{:S(2)}) collective-permute-start(bf16[288,1024]{1,0:T(8,128)(2,1)S(1)} %collective-permute-done.9.refs_8_), channel_id=1, source_target_pairs={{0,3},{1,2},{2,1},{3,0},{4,7},{5,6},{6,5},{7,4},{8,11},{9,10},{10,... | collective-permute-start | bytes 1769480 | tf_op jit(solution)/shard_map/ppermute | solution.py:28
  119.1 16.4 %collective-permute-start.15 = (bf16[288,1024]{1,0:T(8,128)(2,1)S(1)}, bf16[288,1024]{1,0:T(8,128)(2,1)}, u32[]{:S(2)}, u32[]{:S(2)}) collective-permute-start(bf16[288,1024]{1,0:T(8,128)(2,1)S(1)} %collective-permute-done.3.refs_3_), channel_id=1, source_target_pairs={{0,4},{1,5},{2,6},{3,7},{4,8},{5,9},{6,10},{7,11},{8,12},{9,13},{1... | collective-permute-start | bytes 1769480 | tf_op jit(solution)/shard_map/ppermute | solution.py:28
  129.1 26.6 %collective-permute-start.18 = (bf16[512,1024]{1,0:T(8,128)(2,1)S(1)}, bf16[512,1024]{1,0:T(8,128)(2,1)S(1)}, u32[]{:S(2)}, u32[]{:S(2)}) collective-permute-start(bf16[512,1024]{1,0:T(8,128)(2,1)S(1)} %collective-permute-done.16.refs_17_), channel_id=1, source_target_pairs={{0,96},{16,112},{32,0},{48,16},{64,32},{80,48},{96,64},{112,80},{1... | collective-permute-start | bytes 3145736 | tf_op jit(solution)/shard_map/ppermute | solution.py:28
  132.1 27.2 %collective-permute-start.20 = (bf16[512,1024]{1,0:T(8,128)(2,1)S(1)}, bf16[512,1024]{1,0:T(8,128)(2,1)S(1)}, u32[]{:S(2)}, u32[]{:S(2)}) collective-permute-start(bf16[512,1024]{1,0:T(8,128)(2,1)S(1)} %collective-permute-done.16.refs_17_), channel_id=1, source_target_pairs={{0,32},{16,48},{32,64},{48,80},{64,96},{80,112},{96,0},{112,16},{1... | collective-permute-start | bytes 3145736 | tf_op jit(solution)/shard_map/ppermute | solution.py:28
  132.2 45.5 %collective-permute-start.26 = (bf16[512,1024]{1,0:T(8,128)(2,1)S(1)}, bf16[512,1024]{1,0:T(8,128)(2,1)S(1)}, u32[]{:S(2)}, u32[]{:S(2)}) collective-permute-start(bf16[512,1024]{1,0:T(8,128)(2,1)S(1)} %collective-permute-done.24.refs_25_), channel_id=1, source_target_pairs={{0,96},{16,112},{32,0},{48,16},{64,32},{80,48},{96,64},{112,80},{1... | collective-permute-start | bytes 3145736 | tf_op jit(solution)/shard_map/ppermute | solution.py:28
  135.4 46.0 %collective-permute-start.25 = (bf16[512,1024]{1,0:T(8,128)(2,1)S(1)}, bf16[512,1024]{1,0:T(8,128)(2,1)S(1)}, u32[]{:S(2)}, u32[]{:S(2)}) collective-permute-start(bf16[512,1024]{1,0:T(8,128)(2,1)S(1)} %collective-permute-done.24.refs_25_), channel_id=1, source_target_pairs={{0,16},{16,0},{32,48},{48,32},{64,80},{80,64},{96,112},{112,96},{1... | collective-permute-start | bytes 3145736 | tf_op jit(solution)/shard_map/ppermute | solution.py:28
  135.5 47.7 %collective-permute-start.30 = (bf16[512,1024]{1,0:T(8,128)(2,1)S(1)}, bf16[512,1024]{1,0:T(8,128)(2,1)S(1)}, u32[]{:S(2)}, u32[]{:S(2)}) collective-permute-start(bf16[512,1024]{1,0:T(8,128)(2,1)S(1)} %collective-permute-done.24.refs_25_), channel_id=1, source_target_pairs={{0,32},{16,48},{32,64},{48,80},{64,96},{80,112},{96,0},{112,16},{1... | collective-permute-start | bytes 3145736 | tf_op jit(solution)/shard_map/ppermute | solution.py:28
  155.7 41.5 %collective-permute-start.19 = (bf16[512,1024]{1,0:T(8,128)(2,1)S(1)}, bf16[512,1024]{1,0:T(8,128)(2,1)S(1)}, u32[]{:S(2)}, u32[]{:S(2)}) collective-permute-start(bf16[512,1024]{1,0:T(8,128)(2,1)S(1)} %collective-permute-done.18.refs_19_), channel_id=1, source_target_pairs={{0,16},{16,0},{32,48},{48,32},{64,80},{80,64},{96,112},{112,96},{1... | collective-permute-start | bytes 3145736 | tf_op jit(solution)/shard_map/ppermute | solution.py:28
  159.4 44.2 %collective-permute-start.21 = (bf16[512,1024]{1,0:T(8,128)(2,1)S(1)}, bf16[512,1024]{1,0:T(8,128)(2,1)S(1)}, u32[]{:S(2)}, u32[]{:S(2)}) collective-permute-start(bf16[512,1024]{1,0:T(8,128)(2,1)S(1)} %collective-permute-done.20.refs_23_), channel_id=1, source_target_pairs={{0,32},{16,48},{32,64},{48,80},{64,96},{80,112},{96,0},{112,16},{1... | collective-permute-start | bytes 3145736 | tf_op jit(solution)/shard_map/ppermute | solution.py:28
  177.7 25.9 %collective-permute-start.28 = (bf16[512,1024]{1,0:T(8,128)(2,1)S(1)}, bf16[512,1024]{1,0:T(8,128)(2,1)S(1)}, u32[]{:S(2)}, u32[]{:S(2)}) collective-permute-start(bf16[512,1024]{1,0:T(8,128)(2,1)S(1)} %collective-permute-done.26.refs_27_), channel_id=1, source_target_pairs={{0,96},{16,112},{32,0},{48,16},{64,32},{80,48},{96,64},{112,80},{1... | collective-permute-start | bytes 3145736 | tf_op jit(solution)/shard_map/ppermute | solution.py:28
  181.4 15.8 %collective-permute-start.12 = (bf16[288,1024]{1,0:T(8,128)(2,1)S(1)}, bf16[288,1024]{1,0:T(8,128)(2,1)S(1)}, u32[]{:S(2)}, u32[]{:S(2)}) collective-permute-start(bf16[288,1024]{1,0:T(8,128)(2,1)S(1)} %collective-permute-done.10.refs_9_), channel_id=1, source_target_pairs={{0,3},{1,2},{2,1},{3,0},{4,7},{5,6},{6,5},{7,4},{8,11},{9,10},{10,... | collective-permute-start | bytes 1769480 | tf_op jit(solution)/shard_map/ppermute | solution.py:28
  183.1 23.3 %collective-permute-start.23 = (bf16[512,1024]{1,0:T(8,128)(2,1)S(1)}, bf16[512,1024]{1,0:T(8,128)(2,1)S(1)}, u32[]{:S(2)}, u32[]{:S(2)}) collective-permute-start(bf16[512,1024]{1,0:T(8,128)(2,1)S(1)} %collective-permute-done.20.refs_23_), channel_id=1, source_target_pairs={{0,16},{16,0},{32,48},{48,32},{64,80},{80,64},{96,112},{112,96},{1... | collective-permute-start | bytes 3145736 | tf_op jit(solution)/shard_map/ppermute | solution.py:28
  197.2 11.3 %collective-permute-start.31 = (bf16[512,1024]{1,0:T(8,128)(2,1)S(1)}, bf16[512,1024]{1,0:T(8,128)(2,1)S(1)}, u32[]{:S(2)}, u32[]{:S(2)}) collective-permute-start(bf16[512,1024]{1,0:T(8,128)(2,1)S(1)} %collective-permute-done.30.refs_31_), channel_id=1, source_target_pairs={{0,16},{16,0},{32,48},{48,32},{64,80},{80,64},{96,112},{112,96},{1... | collective-permute-start | bytes 3145736 | tf_op jit(solution)/shard_map/ppermute | solution.py:28
  206.4 26.6 %collective-permute-start.38 = (bf16[144,1024]{1,0:T(8,128)(2,1)}, bf16[144,1024]{1,0:T(8,128)(2,1)S(1)}, u32[]{:S(2)}, u32[]{:S(2)}) collective-permute-start(bf16[144,1024]{1,0:T(8,128)(2,1)} %collective-permute-done.34.refs_3_), channel_id=1, source_target_pairs={{0,12},{1,13},{2,14},{3,15},{4,0},{5,1},{6,2},{7,3},{8,4},{9,5},{1... | collective-permute-start | bytes 884744 | tf_op jit(solution)/shard_map/ppermute | solution.py:28
  208.0 30.1 %collective-permute-start.46 = (bf16[144,1024]{1,0:T(8,128)(2,1)}, bf16[144,1024]{1,0:T(8,128)(2,1)S(1)}, u32[]{:S(2)}, u32[]{:S(2)}) collective-permute-start(bf16[144,1024]{1,0:T(8,128)(2,1)} %collective-permute-done.34.refs_3_), channel_id=1, source_target_pairs={{0,4},{1,5},{2,6},{3,7},{4,8},{5,9},{6,10},{7,11},{8,12},{9,13},{1... | collective-permute-start | bytes 884744 | tf_op jit(solution)/shard_map/ppermute | solution.py:28
  208.5 25.3 %collective-permute-start.41 = (bf16[144,1024]{1,0:T(8,128)(2,1)}, bf16[144,1024]{1,0:T(8,128)(2,1)S(1)}, u32[]{:S(2)}, u32[]{:S(2)}) collective-permute-start(bf16[144,1024]{1,0:T(8,128)(2,1)} %collective-permute-done.36.refs_5_), channel_id=1, source_target_pairs={{0,12},{1,13},{2,14},{3,15},{4,0},{5,1},{6,2},{7,3},{8,4},{9,5},{1... | collective-permute-start | bytes 884744 | tf_op jit(solution)/shard_map/ppermute | solution.py:28
  210.1 24.8 %collective-permute-start.42 = (bf16[144,1024]{1,0:T(8,128)(2,1)S(1)}, bf16[144,1024]{1,0:T(8,128)(2,1)S(1)}, u32[]{:S(2)}, u32[]{:S(2)}) collective-permute-start(bf16[144,1024]{1,0:T(8,128)(2,1)S(1)} %collective-permute-done.40.refs_8_), channel_id=1, source_target_pairs={{0,3},{1,2},{2,1},{3,0},{4,7},{5,6},{6,5},{7,4},{8,11},{9,10},{10,... | collective-permute-start | bytes 884744 | tf_op jit(solution)/shard_map/ppermute | solution.py:28
  212.0 26.1 %collective-permute-start.53 = (bf16[144,1024]{1,0:T(8,128)(2,1)S(1)}, bf16[144,1024]{1,0:T(8,128)(2,1)S(1)}, u32[]{:S(2)}, u32[]{:S(2)}) collective-permute-start(bf16[144,1024]{1,0:T(8,128)(2,1)S(1)} %collective-permute-done.49.refs_3_), channel_id=1, source_target_pairs={{0,12},{1,13},{2,14},{3,15},{4,0},{5,1},{6,2},{7,3},{8,4},{9,5},{1... | collective-permute-start | bytes 884744 | tf_op jit(solution)/shard_map/ppermute | solution.py:28
  234.9 46.3 %collective-permute-start.62 = (bf16[2,144,1024]{2,1,0:T(8,128)(2,1)S(1)}, bf16[2,144,1024]{2,1,0:T(8,128)(2,1)S(1)}, u32[]{:S(2)}, u32[]{:S(2)}) collective-permute-start(bf16[2,144,1024]{2,1,0:T(8,128)(2,1)S(1)} %get-tuple-element.27), channel_id=1, source_target_pairs={{0,96},{1,33},{2,34},{3,99},{4,100},{5,37},{6,38},{7,103},{8,104},... | collective-permute-start | bytes 1769480 | tf_op jit(solution)/shard_map/ppermute | solution.py:28
  238.1 43.1 %collective-permute-start.63 = (bf16[2,144,1024]{2,1,0:T(8,128)(2,1)S(1)}, bf16[2,144,1024]{2,1,0:T(8,128)(2,1)S(1)}, u32[]{:S(2)}, u32[]{:S(2)}) collective-permute-start(bf16[2,144,1024]{2,1,0:T(8,128)(2,1)S(1)} %get-tuple-element.28), channel_id=1, source_target_pairs={{0,112},{1,49},{2,50},{3,115},{4,116},{5,53},{6,54},{7,119},{8,120... | collective-permute-start | bytes 1769480 | tf_op jit(solution)/shard_map/ppermute | solution.py:28
  238.1 21.9 %collective-permute-start.57 = (bf16[144,1024]{1,0:T(8,128)(2,1)S(1)}, bf16[144,1024]{1,0:T(8,128)(2,1)S(1)}, u32[]{:S(2)}, u32[]{:S(2)}) collective-permute-start(bf16[144,1024]{1,0:T(8,128)(2,1)S(1)} %collective-permute-done.55.refs_8_), channel_id=1, source_target_pairs={{0,3},{1,2},{2,1},{3,0},{4,7},{5,6},{6,5},{7,4},{8,11},{9,10},{10,... | collective-permute-start | bytes 884744 | tf_op jit(solution)/shard_map/ppermute | solution.py:28
  240.6 19.4 %collective-permute-start.61 = (bf16[144,1024]{1,0:T(8,128)(2,1)S(1)}, bf16[144,1024]{1,0:T(8,128)(2,1)S(1)}, u32[]{:S(2)}, u32[]{:S(2)}) collective-permute-start(bf16[144,1024]{1,0:T(8,128)(2,1)S(1)} %collective-permute-done.49.refs_3_), channel_id=1, source_target_pairs={{0,4},{1,5},{2,6},{3,7},{4,8},{5,9},{6,10},{7,11},{8,12},{9,13},{1... | collective-permute-start | bytes 884744 | tf_op jit(solution)/shard_map/ppermute | solution.py:28
  243.1 17.0 %collective-permute-start.58 = (bf16[144,1024]{1,0:T(8,128)(2,1)S(1)}, bf16[144,1024]{1,0:T(8,128)(2,1)S(1)}, u32[]{:S(2)}, u32[]{:S(2)}) collective-permute-start(bf16[144,1024]{1,0:T(8,128)(2,1)S(1)} %collective-permute-done.56.refs_9_), channel_id=1, source_target_pairs={{0,3},{1,2},{2,1},{3,0},{4,7},{5,6},{6,5},{7,4},{8,11},{9,10},{10,... | collective-permute-start | bytes 884744 | tf_op jit(solution)/shard_map/ppermute | solution.py:28
  260.0 21.6 %collective-permute-start.64 = (bf16[2,144,1024]{2,1,0:T(8,128)(2,1)S(1)}, bf16[2,144,1024]{2,1,0:T(8,128)(2,1)S(1)}, u32[]{:S(2)}, u32[]{:S(2)}) collective-permute-start(bf16[2,144,1024]{2,1,0:T(8,128)(2,1)S(1)} %get-tuple-element.29), channel_id=1, source_target_pairs={{0,80},{1,65},{2,66},{3,83},{4,84},{5,69},{6,70},{7,87},{8,88},{9,... | collective-permute-start | bytes 1769480 | tf_op jit(solution)/shard_map/ppermute | solution.py:28
  281.5 28.0 %collective-permute-start.66 = (bf16[288,1024]{1,0:T(8,128)(2,1)S(1)}, bf16[288,1024]{1,0:T(8,128)(2,1)S(1)}, u32[]{:S(2)}, u32[]{:S(2)}) collective-permute-start(bf16[288,1024]{1,0:T(8,128)(2,1)S(1)} %pad_maximum_fusion), channel_id=1, source_target_pairs={{0,1},{1,0},{2,3},{3,2},{4,5},{5,4},{6,7},{7,6},{8,9},{9,8},{10,11... | collective-permute-start | bytes 1769480 | tf_op jit(solution)/shard_map/ppermute | solution.py:28
  281.7 22.4 %collective-permute-start.67 = (bf16[144,1024]{1,0:T(8,128)(2,1)S(1)}, bf16[144,1024]{1,0:T(8,128)(2,1)S(1)}, u32[]{:S(2)}, u32[]{:S(2)}) collective-permute-start(bf16[144,1024]{1,0:T(8,128)(2,1)S(1)} %fusion.3), channel_id=1, source_target_pairs={{0,1},{1,0},{2,3},{3,2},{4,5},{5,4},{6,7},{7,6},{8,9},{9,8},{10,11... | collective-permute-start | bytes 884744 | tf_op jit(solution)/shard_map/ppermute | solution.py:28
  283.9 25.6 %collective-permute-start.68 = (bf16[144,1024]{1,0:T(8,128)(2,1)S(1)}, bf16[144,1024]{1,0:T(8,128)(2,1)S(1)}, u32[]{:S(2)}, u32[]{:S(2)}) collective-permute-start(bf16[144,1024]{1,0:T(8,128)(2,1)S(1)} %fusion.4), channel_id=1, source_target_pairs={{0,1},{1,0},{2,3},{3,2},{4,5},{5,4},{6,7},{7,6},{8,9},{9,8},{10,11... | collective-permute-start | bytes 884744 | tf_op jit(solution)/shard_map/ppermute | solution.py:28
  (60 other events, 1385.4 us)

commit v2 on v1

v2 whole, which is shorter than its diff:
```python
import functools

import jax
import jax.numpy as jnp
from jax import lax
from jax.experimental import pallas as pl
from jax.experimental.pallas import tpu as pltpu
from jax.sharding import PartitionSpec as P

TW = 32
K = 1024
CD_MAX = 8
OCC = 8
OI = 12
BLK = OI * OI
NO = OCC * OI
BF = jnp.bfloat16
F32 = jnp.float32

HALF = ((2, 7, 5, 0), (3, 6, 4, 1))
CHUNKS = ((0, 1), (2, 3))
NCH = len(CHUNKS)


def half_of(v):
    return 0 if v % 4 in (1, 2) else 1


def permute(value, pairs, axis):
    return lax.ppermute(value, axis, pairs)


def pair_perm(value):
    return permute(value, [(v, v ^ 1) for v in range(16)], "vir")


def group_perm(value):
    return permute(value, [(v, v ^ 3) for v in range(16)], "vir")


def z_perm(value, step):
    return permute(value, [(v, (v + 4 * step) % 16) for v in range(16)], "vir")


def y_perm(value, step):
    return permute(value, [(o, (o + 2 * step) % 8) for o in range(8)], "occ")


def core_perm(value):
    return permute(value, [(o, o ^ 1) for o in range(8)], "occ")


def mirror_perm(value, pos):
    pairs = [(o * 16 + v, (o ^ HALF[half_of(v)][pos]) * 16 + v) for o in range(8) for v in range(16)]
    return permute(value, pairs, ("occ", "vir"))


def my_half():
    x = lax.rem(lax.axis_index("vir"), 4)
    return jnp.where((x == 1) | (x == 2), 0, 1)


def any_spec():
    return pl.BlockSpec(memory_space=pl.ANY)


LANES = 256


def split_kernel(a_ref, *refs):
    outs, wide, cut = refs[:-2], refs[-2], refs[-1]
    me = lax.axis_index("occ")
    half = my_half()
    wide[...] = a_ref[...].astype(F32)
    for owner in range(OCC):
        kk = owner ^ me
        for ii in range(OI):
            cut[kk, ii * OI:(ii + 1) * OI, :] = wide[ii * NO + owner * OI:ii * NO + (owner + 1) * OI, :]
    for hh in range(2):
        for chunk, members in enumerate(CHUNKS):
            for slot, pos in enumerate(members):
                rows = cut[HALF[hh][pos]].astype(BF)

                @pl.when(half == hh)
                def _():
                    outs[chunk][slot * BLK:(slot + 1) * BLK, :] = rows

                @pl.when(half != hh)
                def _():
                    outs[NCH + chunk][slot * BLK:(slot + 1) * BLK, :] = rows


def split_rows(amplitudes):
    sizes = [len(members) * BLK for members in CHUNKS] * 2
    return pl.pallas_call(
        split_kernel,
        grid=(K // LANES,),
        in_specs=[pl.BlockSpec((OI * NO, LANES), lambda g: (0, g))],
        out_specs=[pl.BlockSpec((n, LANES), lambda g: (0, g)) for n in sizes],
        out_shape=[jax.ShapeDtypeStruct((n, K), BF) for n in sizes],
        scratch_shapes=[pltpu.VMEM((OI * NO, LANES), F32), pltpu.VMEM((OCC, BLK, LANES), F32)],
        name="split_rows",
    )(amplitudes)


def join_kernel(*refs):
    mine, mirror, other = refs[0:NCH], refs[NCH:NCH + 4], refs[NCH + 4:NCH + 8]
    out, cut, wide = refs[NCH + 8:]
    me = lax.axis_index("occ")
    half = my_half()
    for chunk, members in enumerate(CHUNKS):
        for slot, pos in enumerate(members):
            own = mine[chunk][slot * BLK:(slot + 1) * BLK, :].astype(F32) + mirror[pos][...].astype(F32)
            got = other[pos][...].astype(F32)
            for hh in range(2):
                cut[HALF[hh][pos]] = jnp.where(half == hh, own, got)
    for owner in range(OCC):
        kk = owner ^ me
        for ii in range(OI):
            wide[ii * NO + owner * OI:ii * NO + (owner + 1) * OI, :] = cut[kk, ii * OI:(ii + 1) * OI, :]
    out[...] = wide[...].astype(BF)


def join_rows(mine, mirror, other):
    def lead(n):
        return pl.BlockSpec((None, n, LANES), lambda g: (0, 0, g))

    def part(at):
        return pl.BlockSpec((BLK, LANES), lambda g: (at, g))

    sizes = [len(members) * BLK for members in CHUNKS]
    return pl.pallas_call(
        join_kernel,
        grid=(K // LANES,),
        in_specs=[lead(n) for n in sizes] + [lead(BLK)] * 4 + [part(at) for _, at in other],
        out_specs=pl.BlockSpec((OI * NO, LANES), lambda g: (0, g)),
        out_shape=jax.ShapeDtypeStruct((OI * NO, K), BF),
        scratch_shapes=[pltpu.VMEM((OCC, BLK, LANES), F32), pltpu.VMEM((OI * NO, LANES), F32)],
        name="join_rows",
    )(*mine, *mirror, *[t for t, _ in other])


NBUF = 3


PLACE = tuple((k, 0) for k in range(4)) + ((4, 0), (5, 0), (6, 0), (6, 1)) + tuple((k, 0) for k in (7, 8, 9, 10)) + (
    (11, 0), (12, 0), (13, 0), (13, 1))
ARRAYS = 14


FULL = (1 << 16) - 1
LATE = 1 << 6 | 1 << 7 | 1 << 14 | 1 << 15


def ladder_kernel(blocks, mask, sides, resumed, final, apart, own_list, own_count, far, *refs):
    arrays, refs = refs[:ARRAYS], refs[ARRAYS:]
    far_n = 16 if sides[1] == 2 else 0
    own_int, far_int, refs = refs[0], refs[1:1 + far_n], refs[1 + far_n:]
    if resumed:
        before, refs = refs[0], refs[1:]
    if final:
        swap_cols, swap_rows, ladder, refs = refs[0], refs[1], refs[2], refs[3:]
        mirrors, refs = refs[:blocks + apart], refs[blocks + apart:]
        acc, cols, col_sem, refs = refs[0], refs[1], refs[2], refs[3:]
    else:
        acc, refs = refs[0], refs[1:]
    held, ints, piece_sem, int_sem, work, here = refs
    rows = blocks * BLK
    v, o = lax.axis_index("vir"), lax.axis_index("occ")
    x, z = lax.rem(v, 4), lax.div(v, 4)
    y, c = lax.div(o, 2), lax.rem(o, 2)
    count0, count1 = own_count[0], far[8]
    used = [q for q in range(16) if mask >> q & 1]

    def note(t, n):
        near = t < CD_MAX
        s = t & (CD_MAX - 1)
        tile = jnp.where(near, own_list[s], far[s])
        flip = lax.rem(tile, 4) ^ x
        q = ((lax.div(tile, 4) - z) & 3) * 4 + (flip ^ lax.div(flip, 2))
        live = (s < jnp.where(near, count0, count1)) & ((lax.shift_right_logical(mask, q) & 1) == 1)

        @pl.when(live)
        def _():
            work[n] = t * 16 + q

        return n + jnp.where(live, 1, 0)

    total = lax.fori_loop(sides[0] * CD_MAX, sides[1] * CD_MAX, note, jnp.int32(0))

    def fetch(item):
        t = lax.div(work[item], 16)
        slot = lax.rem(item, NBUF)
        near = t < CD_MAX

        @pl.when(near)
        def _():
            pltpu.make_async_copy(own_int.at[t], ints.at[slot], int_sem.at[slot]).start()

        s = t - CD_MAX
        dy = (lax.div(s, 2) - y) & 3
        dc = (s & 1) ^ c
        for rel in range(far_n // 2):
            @pl.when(jnp.logical_not(near) & (dy * 2 + dc == rel))
            def _():
                for part in range(2):
                    pltpu.make_async_copy(
                        far_int[part * 8 + rel],
                        ints.at[slot, pl.ds(part * (K // 2), K // 2), :],
                        int_sem.at[slot]).start()

    for ahead in range(NBUF - 1):
        @pl.when(ahead < total)
        def _():
            fetch(jnp.int32(ahead))
    for q in used:
        k, at = PLACE[q]
        pltpu.make_async_copy(arrays[k].at[pl.ds(at * rows, rows), :], held.at[q], piece_sem.at[q]).start()
        here[q] = 0
    if final:
        col_copy = pltpu.make_async_copy(swap_cols, cols, col_sem)
        col_copy.start()
    acc[...] = before[...] if resumed else jnp.zeros_like(acc)

    def arrive(q):
        @pl.when(here[q] == 0)
        def _():
            pltpu.make_async_copy(held.at[q], held.at[q], piece_sem.at[q]).wait()
            here[q] = 1

    def step(item, carry):
        @pl.when(item + NBUF - 1 < total)
        def _():
            fetch(item + NBUF - 1)

        t, q = lax.div(work[item], 16), work[item] & 15
        slot = lax.rem(item, NBUF)
        arrive(q)
        pltpu.make_async_copy(ints.at[slot], ints.at[slot], int_sem.at[slot]).wait()
        acc[lax.div(t, CD_MAX)] += lax.dot_general(
            held[q], ints[slot], (((1,), (1,)), ((), ())), preferred_element_type=F32)
        return carry

    lax.fori_loop(0, total, step, 0)
    for q in used:
        arrive(q)
    if not final:
        return
    col_copy.wait()
    for side in range(2):
        rounded = acc[side].astype(BF)
        ladder[side] = rounded
        turned = jnp.dot(rounded, cols[...], preferred_element_type=F32).astype(BF)
        for b in range(blocks):
            image = jnp.dot(
                swap_rows[...], turned[b * BLK:(b + 1) * BLK, :], preferred_element_type=F32).astype(BF)
            if apart and b == 0:
                mirrors[1 - side][...] = image
            else:
                mirrors[b + apart][1 - side] = image


def ladder_chunk(blocks, own_list, own_count, far, arrays, own_int, far_int, swaps=(), before=None, mask=FULL, apart=0,
                 sides=(0, 2)):
    rows = blocks * BLK
    final = bool(swaps)
    vmem = pl.BlockSpec(memory_space=pltpu.VMEM)
    sums = jax.ShapeDtypeStruct((2, rows, K), F32)
    if final:
        shapes = [jax.ShapeDtypeStruct((2, rows, K), BF)] + [jax.ShapeDtypeStruct((BLK, K), BF)] * (2 * apart)
        shapes += [jax.ShapeDtypeStruct((2, BLK, K), BF)] * (blocks - apart)
        scratch = [pltpu.VMEM((2, rows, K), F32), pltpu.VMEM((K, K), BF), pltpu.SemaphoreType.DMA]
    else:
        shapes, scratch = [sums], []
    extra = ([] if before is None else [before]) + list(swaps)
    extra_specs = ([] if before is None else [vmem]) + ([any_spec(), vmem] if final else [])
    outs = pl.pallas_call(
        functools.partial(ladder_kernel, blocks, mask, sides, before is not None, final, apart),
        grid_spec=pltpu.PrefetchScalarGridSpec(
            num_scalar_prefetch=3,
            grid=(),
            in_specs=[any_spec()] * (ARRAYS + 1 + len(far_int)) + extra_specs,
            out_specs=[vmem] * len(shapes),
            scratch_shapes=scratch + [
                pltpu.VMEM((16, rows, K), BF),
                pltpu.VMEM((NBUF, K, K), BF),
                pltpu.SemaphoreType.DMA((16,)),
                pltpu.SemaphoreType.DMA((NBUF,)),
                pltpu.SMEM((2 * CD_MAX,), jnp.int32),
                pltpu.SMEM((16,), jnp.int32),
            ],
        ),
        out_shape=shapes,
        compiler_params=pltpu.CompilerParams(vmem_limit_bytes=48 << 20),
    )(own_list, own_count, far, *arrays, own_int, *far_int, *extra)
    return outs


def gather_chunk(own, sent, way):
    um, dm = z_perm(own, 1), z_perm(own, -1)
    mg = group_perm(own)
    n = pair_perm(sent)
    un, dn = z_perm(n, 1), z_perm(n, -1)
    ng = group_perm(n)
    g = jnp.concatenate([mg, ng], 0)
    ug, dg = z_perm(g, 1), z_perm(g, -1)
    m2 = z_perm(um if way == 1 else dm, way)
    n2 = z_perm(dn if way == 1 else un, -way)
    mg2, ng2 = group_perm(m2), group_perm(n2)
    return [own, n, mg, ng, dm, dn, dg, m2, n2, mg2, ng2, um, un, ug]


def gather_integrals(blocks):
    me = lax.axis_index("occ")
    halves = []
    for part in range(2):
        mine = lax.dynamic_slice(blocks, (me, part * (K // 2), 0), (1, K // 2, K))[0]
        b = pair_perm(mine)
        up = y_perm(b, 1)
        down = y_perm(b, -1)
        far = y_perm(up, 1) if part == 0 else y_perm(down, -1)
        for t in (b, down, far, up):
            halves += [t, core_perm(t)]
    return halves


def on_device(amplitudes, integrals, cd_tiles, cd_count):
    listed = cd_tiles[0]
    blocks = integrals[0]
    far = pair_perm(jnp.concatenate([listed, cd_count, jnp.zeros((7,), jnp.int32)]))
    col = jnp.arange(K, dtype=jnp.int32)
    swap_cols = (col[:, None] == ((col % TW) * TW + col // TW)[None, :]).astype(BF)
    row = jnp.arange(BLK, dtype=jnp.int32)
    swap_rows = (row[:, None] == ((row % OI) * OI + row // OI)[None, :]).astype(BF)
    split = split_rows(amplitudes)
    far_int = gather_integrals(blocks)
    swaps = (swap_cols, swap_rows)

    def join(near, mirrored):
        return (near.astype(F32) + mirrored.astype(F32)).astype(BF)

    a_in = gather_chunk(split[0], split[NCH], 1)
    sums, = ladder_chunk(2, listed, cd_count, far, a_in, blocks, (), sides=(0, 1))
    a_lad, a_first, a_second = ladder_chunk(
        2, listed, cd_count, far, a_in, blocks, far_int, swaps, sums, sides=(1, 2))
    a_got = [mirror_perm(a_first, 0), mirror_perm(a_second, 1)]
    a_there = jnp.concatenate([join(a_lad[1, :BLK], a_got[0][1]), join(a_lad[1, BLK:], a_got[1][1])], 0)
    a_out = pair_perm(a_there)

    b_in = gather_chunk(split[1], split[NCH + 1], -1)
    sums, = ladder_chunk(2, listed, cd_count, far, b_in, blocks, far_int, mask=FULL & ~LATE)
    b_lad, b_near, b_far, b_second = ladder_chunk(
        2, listed, cd_count, far, b_in, blocks, far_int, swaps, sums, LATE, 1)
    b_got3 = mirror_perm(b_second, 3)
    b_far = mirror_perm(b_far, 2)
    b_near = mirror_perm(b_near, 2)
    there3 = join(b_lad[1, BLK:], b_got3[1])
    there2 = join(b_lad[1, :BLK], b_far)
    b_out3, b_out2 = pair_perm(there3), pair_perm(there2)
    mine, mirror = [a_lad, b_lad], [a_got[0], a_got[1], b_near[None], b_got3]
    other = [(a_out, 0), (a_out, 1), (b_out2, 0), (b_out3, 0)]
    return join_rows(mine, mirror, other)


def solution(mesh):
    placed = (P("occ", "vir"), P("vir", None, None, None), P("vir", None), P("vir"))
    return jax.shard_map(
        on_device, mesh=mesh, in_specs=placed, out_specs=P("occ", "vir"), check_vma=False
    )
```

time: 319 us -> 286 us (0.90)
  starting transfers between devices: 86.8 us -> 60.6 us
  waiting for transfers between devices: 161 us -> 154 us
    ppermute x69 -> x51, starting transfers between devices: 86.8 us -> 60.6 us  [permute(): return lax.ppermute(value, axis, pairs)]
    ppermute x69 -> x51, waiting for transfers between devices: 161 us -> 154 us  [permute(): return lax.ppermute(value, axis, pairs)]
    pallas_call x4 -> x5, Pallas kernels: 55.5 us -> 52.4 us  [the longest x4 47.7 us: ladder_chunk(): pl.pallas_call(functools.partial(ladder_kernel, blocks, mask, sides, befo...]
  transfers between devices with their start and end apart: 69 -> 51, of which waited for: 25 -> 19; matrix products, arithmetic and copies ran while one was open for 1% -> 2% of each run, Pallas kernels for 16% -> 17%
where the time goes in v2:
time: 286 us; the launch traced here: 282 us
  waiting for transfers between devices  154 us (54%)
  starting transfers between devices  60.6 us (21%)
  Pallas kernels  56.9 us (20%)
  local copies, waits for them, and re-layouts  6.78 us (2%)
    ppermute x51, waiting for transfers between devices, permute(): return lax.ppermute(value, axis, pairs)  154 us
    ppermute x51, starting transfers between devices, permute(): return lax.ppermute(value, axis, pairs)  60.6 us
    pallas_call x4, Pallas kernels, ladder_chunk(): pl.pallas_call(functools.partial(ladder_kernel, blocks, mask, sides, befo...  47.7 us
  transfers between devices with their start and end apart: 51, of which 19 were waited for; matrix products, arithmetic and copies ran while one was open for 2% of the time, Pallas kernels for 17%

profile of v2, /device:TPU:38, one launch (start us, length us, event | category | flops | bytes accessed | tf_op | source)
XLA Modules:
  0.0 281.6 jit_solution(12730715397108099111)
XLA Ops:
  0.0 4.4 %split_rows.1 = (bf16[288,1024]{1,0:T(8,128)(2,1)}, bf16[288,1024]{1,0:T(8,128)(2,1)}, bf16[288,1024]{1,0:T(8,128)(2,1)}, bf16[288,1024]{1,0:T(8,128)(2,1)}) custom-call(bf16[1152,1024]{1,0:T(8,128)(2,1)} %a_ref.1), custom_call_target="tpu_custom_call" | custom-call | tf_op jit(solution)/shard_map/split_rows/pallas_call | solution.py:95
  6.5 1.9 collective-permute-start.7
  9.3 10.5 %collective-permute-done.far = s32[16]{0:T(128)S(1)} collective-permute-done((s32[16]{0:T(128)S(1)}, s32[16]{0:T(128)S(1)}, u32[]{:S(2)}, u32[]{:S(2)}) %collective-permute-start) | collective-permute-done | bytes 96 | tf_op jit(solution)/shard_map/ppermute | solution.py:30
  20.6 1.7 dynamic-slice_bitcast_fusion
  25.1 11.1 %collective-permute-done.30.refs_1_ = bf16[288,1024]{1,0:T(8,128)(2,1)S(1)} collective-permute-done((bf16[288,1024]{1,0:T(8,128)(2,1)}, bf16[288,1024]{1,0:T(8,128)(2,1)S(1)}, u32[]{:S(2)}, u32[]{:S(2)}) %collective-permute-start.30) | collective-permute-done | bytes 589856 | tf_op jit(solution)/shard_map/ppermute | solution.py:30
  36.2 1.9 collective-permute-start.41
  39.1 10.1 %collective-permute-done.41.refs_11_ = bf16[288,1024]{1,0:T(8,128)(2,1)S(1)} collective-permute-done((bf16[288,1024]{1,0:T(8,128)(2,1)S(1)}, bf16[288,1024]{1,0:T(8,128)(2,1)S(1)}, u32[]{:S(2)}, u32[]{:S(2)}) %collective-permute-start.41) | collective-permute-done | bytes 589856 | tf_op jit(solution)/shard_map/ppermute | solution.py:30
  49.2 2.5 collective-permute-start.8
  51.6 7.1 %collective-permute-done.14.refs_15_ = bf16[512,1024]{1,0:T(8,128)(2,1)S(1)} collective-permute-done((bf16[512,1024]{1,0:T(8,128)(2,1)S(1)}, bf16[512,1024]{1,0:T(8,128)(2,1)S(1)}, u32[]{:S(2)}, u32[]{:S(2)}) %collective-permute-start.14) | collective-permute-done | bytes 1048608 | tf_op jit(solution)/shard_map/ppermute | solution.py:30
  58.7 1.9 collective-permute-start.12
  60.6 18.5 %collective-permute-done.22.refs_23_ = bf16[512,1024]{1,0:T(8,128)(2,1)S(1)} collective-permute-done((bf16[512,1024]{1,0:T(8,128)(2,1)S(1)}, bf16[512,1024]{1,0:T(8,128)(2,1)S(1)}, u32[]{:S(2)}, u32[]{:S(2)}) %collective-permute-start.22) | collective-permute-done | bytes 1048608 | tf_op jit(solution)/shard_map/ppermute | solution.py:30
  79.6 2.0 collective-permute-start.37
  81.6 2.3 collective-permute-start.9
  83.9 9.7 %collective-permute-done.32.refs_3_ = bf16[288,1024]{1,0:T(8,128)(2,1)S(1)} collective-permute-done((bf16[288,1024]{1,0:T(8,128)(2,1)S(1)}, bf16[288,1024]{1,0:T(8,128)(2,1)S(1)}, u32[]{:S(2)}, u32[]{:S(2)}) %collective-permute-start.32) | collective-permute-done | bytes 589856 | tf_op jit(solution)/shard_map/ppermute | solution.py:30
  93.6 3.0 %collective-permute-start.16 = (bf16[512,1024]{1,0:T(8,128)(2,1)S(1)}, bf16[512,1024]{1,0:T(8,128)(2,1)S(1)}, u32[]{:S(2)}, u32[]{:S(2)}) collective-permute-start(bf16[512,1024]{1,0:T(8,128)(2,1)S(1)} %collective-permute-done.14.refs_15_), channel_id=1, source_target_pairs={{0,96},{16,112},{32,0},{48,16},{64,32},{80,48},{96,64},{112,80},{1... | collective-permute-start | bytes 3145736 | tf_op jit(solution)/shard_map/ppermute | solution.py:30
  96.6 1.9 collective-permute-start.10
  98.5 1.9 collective-permute-start.38
  100.5 4.9 %collective-permute-done.9.refs_8_ = bf16[288,1024]{1,0:T(8,128)(2,1)S(1)} collective-permute-done((bf16[288,1024]{1,0:T(8,128)(2,1)S(1)}, bf16[288,1024]{1,0:T(8,128)(2,1)S(1)}, u32[]{:S(2)}, u32[]{:S(2)}) %collective-permute-start.9) | collective-permute-done | bytes 589856 | tf_op jit(solution)/shard_map/ppermute | solution.py:30
  105.4 1.6 collective-permute-start.18
  107.0 3.0 %collective-permute-done.10.refs_9_ = bf16[288,1024]{1,0:T(8,128)(2,1)S(1)} collective-permute-done((bf16[288,1024]{1,0:T(8,128)(2,1)S(1)}, bf16[288,1024]{1,0:T(8,128)(2,1)S(1)}, u32[]{:S(2)}, u32[]{:S(2)}) %collective-permute-start.10) | collective-permute-done | bytes 589856 | tf_op jit(solution)/shard_map/ppermute | solution.py:30
  110.0 1.5 collective-permute-start.24
  111.6 3.4 %collective-permute-start.6 = (bf16[576,1024]{1,0:T(8,128)(2,1)S(1)}, bf16[576,1024]{1,0:T(8,128)(2,1)S(1)}, u32[]{:S(2)}, u32[]{:S(2)}) collective-permute-start(bf16[576,1024]{1,0:T(8,128)(2,1)S(1)} %constant_dynamic-update-slice_fusion), channel_id=1, source_target_pairs={{0,12},{1,13},{2,14},{3,15},{4,0},{5,1},{6,2},{7,3},{8,4},{9,5},{1... | collective-permute-start | bytes 3538952 | tf_op jit(solution)/shard_map/ppermute | solution.py:30
  115.0 5.2 %collective-permute-done.16.refs_17_ = bf16[512,1024]{1,0:T(8,128)(2,1)S(1)} collective-permute-done((bf16[512,1024]{1,0:T(8,128)(2,1)S(1)}, bf16[512,1024]{1,0:T(8,128)(2,1)S(1)}, u32[]{:S(2)}, u32[]{:S(2)}) %collective-permute-start.16) | collective-permute-done | bytes 1048608 | tf_op jit(solution)/shard_map/ppermute | solution.py:30
  121.2 11.4 %collective-permute-done.18.refs_21_ = bf16[512,1024]{1,0:T(8,128)(2,1)S(1)} collective-permute-done((bf16[512,1024]{1,0:T(8,128)(2,1)S(1)}, bf16[512,1024]{1,0:T(8,128)(2,1)S(1)}, u32[]{:S(2)}, u32[]{:S(2)}) %collective-permute-start.18) | collective-permute-done | bytes 1048608 | tf_op jit(solution)/shard_map/ppermute | solution.py:30
  132.6 1.7 collective-permute-start.13
  134.4 4.4 %collective-permute-done.24.refs_25_ = bf16[512,1024]{1,0:T(8,128)(2,1)S(1)} collective-permute-done((bf16[512,1024]{1,0:T(8,128)(2,1)S(1)}, bf16[512,1024]{1,0:T(8,128)(2,1)S(1)}, u32[]{:S(2)}, u32[]{:S(2)}) %collective-permute-start.24) | collective-permute-done | bytes 1048608 | tf_op jit(solution)/shard_map/ppermute | solution.py:30
  139.9 15.2 %collective-permute-done.28.refs_29_ = bf16[512,1024]{1,0:T(8,128)(2,1)S(1)} collective-permute-done((bf16[512,1024]{1,0:T(8,128)(2,1)S(1)}, bf16[512,1024]{1,0:T(8,128)(2,1)S(1)}, u32[]{:S(2)}, u32[]{:S(2)}) %collective-permute-start.28) | collective-permute-done | bytes 1048608 | tf_op jit(solution)/shard_map/ppermute | solution.py:30
  155.1 1.8 collective-permute-start.26
  156.9 2.8 %collective-permute-start.11 = (bf16[288,1024]{1,0:T(8,128)(2,1)S(1)}, bf16[288,1024]{1,0:T(8,128)(2,1)S(1)}, u32[]{:S(2)}, u32[]{:S(2)}) collective-permute-start(bf16[288,1024]{1,0:T(8,128)(2,1)S(1)} %collective-permute-done.9.refs_8_), channel_id=1, source_target_pairs={{0,3},{1,2},{2,1},{3,0},{4,7},{5,6},{6,5},{7,4},{8,11},{9,10},{10,... | collective-permute-start | bytes 1769480 | tf_op jit(solution)/shard_map/ppermute | solution.py:30
  159.7 8.3 %collective-permute-done.11.refs_10_ = bf16[288,1024]{1,0:T(8,128)(2,1)S(1)} collective-permute-done((bf16[288,1024]{1,0:T(8,128)(2,1)S(1)}, bf16[288,1024]{1,0:T(8,128)(2,1)S(1)}, u32[]{:S(2)}, u32[]{:S(2)}) %collective-permute-start.11) | collective-permute-done | bytes 589856 | tf_op jit(solution)/shard_map/ppermute | solution.py:30
  168.7 5.0 %collective-permute-done.19.refs_19_ = bf16[512,1024]{1,0:T(8,128)(2,1)S(1)} collective-permute-done((bf16[512,1024]{1,0:T(8,128)(2,1)S(1)}, bf16[512,1024]{1,0:T(8,128)(2,1)S(1)}, u32[]{:S(2)}, u32[]{:S(2)}) %collective-permute-start.19) | collective-permute-done | bytes 1048608 | tf_op jit(solution)/shard_map/ppermute | solution.py:30
  177.6 3.7 %collective-permute-start.35 = (bf16[576,1024]{1,0:T(8,128)(2,1)}, bf16[576,1024]{1,0:T(8,128)(2,1)S(1)}, u32[]{:S(2)}, u32[]{:S(2)}) collective-permute-start(bf16[576,1024]{1,0:T(8,128)(2,1)} %constant_dynamic-update-slice_fusion.2), channel_id=1, source_target_pairs={{0,12},{1,13},{2,14},{3,15},{4,0},{5,1},{6,2},{7,3},{8,4},{9,5},{1... | collective-permute-start | bytes 3538952 | tf_op jit(solution)/shard_map/ppermute | solution.py:30
  181.3 2.8 %collective-permute-start.39 = (bf16[288,1024]{1,0:T(8,128)(2,1)S(1)}, bf16[288,1024]{1,0:T(8,128)(2,1)S(1)}, u32[]{:S(2)}, u32[]{:S(2)}) collective-permute-start(bf16[288,1024]{1,0:T(8,128)(2,1)S(1)} %collective-permute-done.36.refs_7_), channel_id=1, source_target_pairs={{0,3},{1,2},{2,1},{3,0},{4,7},{5,6},{6,5},{7,4},{8,11},{9,10},{10,... | collective-permute-start | bytes 1769480 | tf_op jit(solution)/shard_map/ppermute | solution.py:30
  184.2 2.2 fusion.refs_32_
  187.4 9.8 %shard_map.46.refs_31_ = f32[2,288,1024]{2,1,0:T(8,128)} custom-call(s32[8]{0:T(128)S(1)} %bitcast.17, s32[1]{0:T(128)S(6)} %copy.7.own_count, s32[16]{0:T(128)S(1)} %collective-permute-done.far, bf16[288,1024]{1,0:T(8,128)(2,1)S(1)} %copy-done.1, bf16[288,1024]{1,0:T(8,128)(2,1)S(1)} %collective-permute-done.1.refs_1_, ...), custom_call_target="tpu_custom_call" | custom-call | tf_op jit(solution)/shard_map/pallas_call | solution.py:277
  197.2 14.7 %shard_map.47 = (bf16[2,288,1024]{2,1,0:T(8,128)(2,1)}, bf16[2,144,1024]{2,1,0:T(8,128)(2,1)S(1)}, bf16[2,144,1024]{2,1,0:T(8,128)(2,1)S(1)}) custom-call(s32[8]{0:T(128)S(1)} %bitcast.18, s32[1]{0:T(128)S(6)} %copy.7.own_count, s32[16]{0:T(128)S(1)} %collective-permute-done.far, bf16[288,1024]{1,0:T(8,128)(2,1)S(1)} %copy-done.1, ...), custom_call_target="tpu_custom_call" | custom-call | tf_op jit(solution)/shard_map/pallas_call | solution.py:277
  212.0 1.8 collective-permute-start.44
  213.8 3.1 %collective-permute-done.35.refs_6_ = bf16[576,1024]{1,0:T(8,128)(2,1)S(1)} collective-permute-done((bf16[576,1024]{1,0:T(8,128)(2,1)}, bf16[576,1024]{1,0:T(8,128)(2,1)S(1)}, u32[]{:S(2)}, u32[]{:S(2)}) %collective-permute-start.35) | collective-permute-done | bytes 1179680 | tf_op jit(solution)/shard_map/ppermute | solution.py:30
  217.9 13.6 %shard_map.48.refs_31_ = f32[2,288,1024]{2,1,0:T(8,128)} custom-call(s32[8]{0:T(128)S(1)} %bitcast.19, s32[1]{0:T(128)S(6)} %copy.7.own_count, s32[16]{0:T(128)S(1)} %collective-permute-done.far, bf16[288,1024]{1,0:T(8,128)(2,1)S(1)} %copy-done, bf16[288,1024]{1,0:T(8,128)(2,1)S(1)} %collective-permute-done.30.refs_1_, ...), custom_call_target="tpu_custom_call" | custom-call | tf_op jit(solution)/shard_map/pallas_call | solution.py:277
  231.6 9.6 %shard_map.49 = (bf16[2,288,1024]{2,1,0:T(8,128)(2,1)}, bf16[144,1024]{1,0:T(8,128)(2,1)S(1)}, bf16[144,1024]{1,0:T(8,128)(2,1)S(1)}, bf16[2,144,1024]{2,1,0:T(8,128)(2,1)S(1)}) custom-call(s32[8]{0:T(128)S(1)} %bitcast.20, s32[1]{0:T(128)S(6)} %copy.7.own_count, s32[16]{0:T(128)S(1)} %collective-permute-done.far, bf16[288,1024]{1,0:T(8,128)(2,1)S(1)} %copy-done, ...), custom_call_target="tpu_custom_call" | custom-call | tf_op jit(solution)/shard_map/pallas_call | solution.py:277
  241.2 2.0 collective-permute-start.45
  243.2 1.9 collective-permute-start.46
  245.1 1.7 collective-permute-start.48
  247.9 9.4 %collective-permute-done.48 = bf16[144,1024]{1,0:T(8,128)(2,1)S(1)} collective-permute-done((bf16[144,1024]{1,0:T(8,128)(2,1)S(1)}, bf16[144,1024]{1,0:T(8,128)(2,1)S(1)}, u32[]{:S(2)}, u32[]{:S(2)}) %collective-permute-start.48) | collective-permute-done | bytes 294944 | tf_op jit(solution)/shard_map/ppermute | solution.py:30
  257.4 1.6 collective-permute-start.49
  259.6 10.8 %collective-permute-done.49.refs_8_ = bf16[144,1024]{1,0:T(8,128)(2,1)S(1)} collective-permute-done((bf16[144,1024]{1,0:T(8,128)(2,1)S(1)}, bf16[144,1024]{1,0:T(8,128)(2,1)S(1)}, u32[]{:S(2)}, u32[]{:S(2)}) %collective-permute-start.49) | collective-permute-done | bytes 294944 | tf_op jit(solution)/shard_map/ppermute | solution.py:30
  270.4 5.6 %collective-permute-done.50.refs_9_ = bf16[144,1024]{1,0:T(8,128)(2,1)S(1)} collective-permute-done((bf16[144,1024]{1,0:T(8,128)(2,1)S(1)}, bf16[144,1024]{1,0:T(8,128)(2,1)S(1)}, u32[]{:S(2)}, u32[]{:S(2)}) %collective-permute-start.50) | collective-permute-done | bytes 294944 | tf_op jit(solution)/shard_map/ppermute | solution.py:30
  276.9 4.8 %join_rows.1 = bf16[1152,1024]{1,0:T(8,128)(2,1)} custom-call(bf16[2,288,1024]{2,1,0:T(8,128)(2,1)} %get-tuple-element.18.refs_0_, bf16[2,288,1024]{2,1,0:T(8,128)(2,1)} %get-tuple-element.21.refs_1_, bf16[2,144,1024]{2,1,0:T(8,128)(2,1)} %copy-done.32, bf16[2,144,1024]{2,1,0:T(8,128)(2,1)} %copy-done.33, bf16[1,144,1024]{2,1,0:T(8,128)(2,1)} %bitcast.25, ...), custom_call_target="tpu_custom_call" | custom-call | tf_op jit(solution)/shard_map/join_rows/pallas_call | solution.py:132
  (151 shorter events, 18.7 us)
Async XLA Ops:
  4.4 17.9 %collective-permute-start.1 = (bf16[288,1024]{1,0:T(8,128)(2,1)}, bf16[288,1024]{1,0:T(8,128)(2,1)S(1)}, u32[]{:S(2)}, u32[]{:S(2)}) collective-permute-start(bf16[288,1024]{1,0:T(8,128)(2,1)} %get-tuple-element.17), channel_id=1, source_target_pairs={{0,1},{1,0},{2,3},{3,2},{4,5},{5,4},{6,7},{7,6},{8,9},{9,8},{10,11... | collective-permute-start | bytes 1769480 | tf_op jit(solution)/shard_map/ppermute | solution.py:30
  5.3 18.4 %collective-permute-start.2 = (bf16[288,1024]{1,0:T(8,128)(2,1)}, bf16[288,1024]{1,0:T(8,128)(2,1)S(1)}, u32[]{:S(2)}, u32[]{:S(2)}) collective-permute-start(bf16[288,1024]{1,0:T(8,128)(2,1)} %get-tuple-element.16.refs_0_), channel_id=1, source_target_pairs={{0,3},{1,2},{2,1},{3,0},{4,7},{5,6},{6,5},{7,4},{8,11},{9,10},{10,... | collective-permute-start | bytes 1769480 | tf_op jit(solution)/shard_map/ppermute | solution.py:30
  6.4 17.7 %collective-permute-start.4 = (bf16[288,1024]{1,0:T(8,128)(2,1)}, bf16[288,1024]{1,0:T(8,128)(2,1)S(1)}, u32[]{:S(2)}, u32[]{:S(2)}) collective-permute-start(bf16[288,1024]{1,0:T(8,128)(2,1)} %get-tuple-element.16.refs_0_), channel_id=1, source_target_pairs={{0,12},{1,13},{2,14},{3,15},{4,0},{5,1},{6,2},{7,3},{8,4},{9,5},{1... | collective-permute-start | bytes 1769480 | tf_op jit(solution)/shard_map/ppermute | solution.py:30
  6.5 17.6 %collective-permute-start.7 = (bf16[288,1024]{1,0:T(8,128)(2,1)}, bf16[288,1024]{1,0:T(8,128)(2,1)S(1)}, u32[]{:S(2)}, u32[]{:S(2)}) collective-permute-start(bf16[288,1024]{1,0:T(8,128)(2,1)} %get-tuple-element.16.refs_0_), channel_id=1, source_target_pairs={{0,4},{1,5},{2,6},{3,7},{4,8},{5,9},{6,10},{7,11},{8,12},{9,13},{1... | collective-permute-start | bytes 1769480 | tf_op jit(solution)/shard_map/ppermute | solution.py:30
  9.2 10.6 %collective-permute-start = (s32[16]{0:T(128)S(1)}, s32[16]{0:T(128)S(1)}, u32[]{:S(2)}, u32[]{:S(2)}) collective-permute-start(s32[16]{0:T(128)S(1)} %pad_add_fusion), channel_id=1, source_target_pairs={{0,1},{1,0},{2,3},{3,2},{4,5},{5,4},{6,7},{7,6},{8,9},{9,8},{10,11... | collective-permute-start | bytes 200 | tf_op jit(solution)/shard_map/ppermute | solution.py:30
  19.8 16.4 %collective-permute-start.30 = (bf16[288,1024]{1,0:T(8,128)(2,1)}, bf16[288,1024]{1,0:T(8,128)(2,1)S(1)}, u32[]{:S(2)}, u32[]{:S(2)}) collective-permute-start(bf16[288,1024]{1,0:T(8,128)(2,1)} %get-tuple-element.20), channel_id=1, source_target_pairs={{0,1},{1,0},{2,3},{3,2},{4,5},{5,4},{6,7},{7,6},{8,9},{9,8},{10,11... | collective-permute-start | bytes 1769480 | tf_op jit(solution)/shard_map/ppermute | solution.py:30
  22.4 36.3 %collective-permute-start.14 = (bf16[512,1024]{1,0:T(8,128)(2,1)S(1)}, bf16[512,1024]{1,0:T(8,128)(2,1)S(1)}, u32[]{:S(2)}, u32[]{:S(2)}) collective-permute-start(bf16[512,1024]{1,0:T(8,128)(2,1)S(1)} %get-tuple-element.28), channel_id=1, source_target_pairs={{0,1},{1,0},{2,3},{3,2},{4,5},{5,4},{6,7},{7,6},{8,9},{9,8},{10,11... | collective-permute-start | bytes 3145736 | tf_op jit(solution)/shard_map/ppermute | solution.py:30
  23.6 14.8 %collective-permute-start.31 = (bf16[288,1024]{1,0:T(8,128)(2,1)S(1)}, bf16[288,1024]{1,0:T(8,128)(2,1)S(1)}, u32[]{:S(2)}, u32[]{:S(2)}) collective-permute-start(bf16[288,1024]{1,0:T(8,128)(2,1)S(1)} %copy-done), channel_id=1, source_target_pairs={{0,3},{1,2},{2,1},{3,0},{4,7},{5,6},{6,5},{7,4},{8,11},{9,10},{10,... | collective-permute-start | bytes 1769480 | tf_op jit(solution)/shard_map/ppermute | solution.py:30
  24.1 14.8 %collective-permute-start.33 = (bf16[288,1024]{1,0:T(8,128)(2,1)S(1)}, bf16[288,1024]{1,0:T(8,128)(2,1)S(1)}, u32[]{:S(2)}, u32[]{:S(2)}) collective-permute-start(bf16[288,1024]{1,0:T(8,128)(2,1)S(1)} %copy-done), channel_id=1, source_target_pairs={{0,12},{1,13},{2,14},{3,15},{4,0},{5,1},{6,2},{7,3},{8,4},{9,5},{1... | collective-permute-start | bytes 1769480 | tf_op jit(solution)/shard_map/ppermute | solution.py:30
  24.2 54.9 %collective-permute-start.22 = (bf16[512,1024]{1,0:T(8,128)(2,1)S(1)}, bf16[512,1024]{1,0:T(8,128)(2,1)S(1)}, u32[]{:S(2)}, u32[]{:S(2)}) collective-permute-start(bf16[512,1024]{1,0:T(8,128)(2,1)S(1)} %get-tuple-element.27), channel_id=1, source_target_pairs={{0,1},{1,0},{2,3},{3,2},{4,5},{5,4},{6,7},{7,6},{8,9},{9,8},{10,11... | collective-permute-start | bytes 3145736 | tf_op jit(solution)/shard_map/ppermute | solution.py:30
  36.2 12.9 %collective-permute-start.41 = (bf16[288,1024]{1,0:T(8,128)(2,1)S(1)}, bf16[288,1024]{1,0:T(8,128)(2,1)S(1)}, u32[]{:S(2)}, u32[]{:S(2)}) collective-permute-start(bf16[288,1024]{1,0:T(8,128)(2,1)S(1)} %copy-done), channel_id=1, source_target_pairs={{0,4},{1,5},{2,6},{3,7},{4,8},{5,9},{6,10},{7,11},{8,12},{9,13},{1... | collective-permute-start | bytes 1769480 | tf_op jit(solution)/shard_map/ppermute | solution.py:30
  38.4 41.1 %collective-permute-start.3 = (bf16[288,1024]{1,0:T(8,128)(2,1)S(1)}, bf16[288,1024]{1,0:T(8,128)(2,1)S(1)}, u32[]{:S(2)}, u32[]{:S(2)}) collective-permute-start(bf16[288,1024]{1,0:T(8,128)(2,1)S(1)} %collective-permute-done.1.refs_1_), channel_id=1, source_target_pairs={{0,3},{1,2},{2,1},{3,0},{4,7},{5,6},{6,5},{7,4},{8,11},{9,10},{10,... | collective-permute-start | bytes 1769480 | tf_op jit(solution)/shard_map/ppermute | solution.py:30
  38.9 40.7 %collective-permute-start.5 = (bf16[288,1024]{1,0:T(8,128)(2,1)S(1)}, bf16[288,1024]{1,0:T(8,128)(2,1)S(1)}, u32[]{:S(2)}, u32[]{:S(2)}) collective-permute-start(bf16[288,1024]{1,0:T(8,128)(2,1)S(1)} %collective-permute-done.1.refs_1_), channel_id=1, source_target_pairs={{0,12},{1,13},{2,14},{3,15},{4,0},{5,1},{6,2},{7,3},{8,4},{9,5},{1... | collective-permute-start | bytes 1769480 | tf_op jit(solution)/shard_map/ppermute | solution.py:30
  49.2 32.5 %collective-permute-start.8 = (bf16[288,1024]{1,0:T(8,128)(2,1)S(1)}, bf16[288,1024]{1,0:T(8,128)(2,1)S(1)}, u32[]{:S(2)}, u32[]{:S(2)}) collective-permute-start(bf16[288,1024]{1,0:T(8,128)(2,1)S(1)} %collective-permute-done.7.refs_11_), channel_id=1, source_target_pairs={{0,4},{1,5},{2,6},{3,7},{4,8},{5,9},{6,10},{7,11},{8,12},{9,13},{1... | collective-permute-start | bytes 1769480 | tf_op jit(solution)/shard_map/ppermute | solution.py:30
  58.7 22.9 %collective-permute-start.12 = (bf16[288,1024]{1,0:T(8,128)(2,1)S(1)}, bf16[288,1024]{1,0:T(8,128)(2,1)}, u32[]{:S(2)}, u32[]{:S(2)}) collective-permute-start(bf16[288,1024]{1,0:T(8,128)(2,1)S(1)} %collective-permute-done.1.refs_1_), channel_id=1, source_target_pairs={{0,4},{1,5},{2,6},{3,7},{4,8},{5,9},{6,10},{7,11},{8,12},{9,13},{1... | collective-permute-start | bytes 1769480 | tf_op jit(solution)/shard_map/ppermute | solution.py:30
  79.1 14.5 %collective-permute-start.32 = (bf16[288,1024]{1,0:T(8,128)(2,1)S(1)}, bf16[288,1024]{1,0:T(8,128)(2,1)S(1)}, u32[]{:S(2)}, u32[]{:S(2)}) collective-permute-start(bf16[288,1024]{1,0:T(8,128)(2,1)S(1)} %collective-permute-done.30.refs_1_), channel_id=1, source_target_pairs={{0,3},{1,2},{2,1},{3,0},{4,7},{5,6},{6,5},{7,4},{8,11},{9,10},{10,... | collective-permute-start | bytes 1769480 | tf_op jit(solution)/shard_map/ppermute | solution.py:30
  79.6 17.0 %collective-permute-start.36 = (bf16[288,1024]{1,0:T(8,128)(2,1)S(1)}, bf16[288,1024]{1,0:T(8,128)(2,1)S(1)}, u32[]{:S(2)}, u32[]{:S(2)}) collective-permute-start(bf16[288,1024]{1,0:T(8,128)(2,1)S(1)} %collective-permute-done.33.refs_4_), channel_id=1, source_target_pairs={{0,12},{1,13},{2,14},{3,15},{4,0},{5,1},{6,2},{7,3},{8,4},{9,5},{1... | collective-permute-start | bytes 1769480 | tf_op jit(solution)/shard_map/ppermute | solution.py:30
  79.6 19.0 %collective-permute-start.37 = (bf16[288,1024]{1,0:T(8,128)(2,1)S(1)}, bf16[288,1024]{1,0:T(8,128)(2,1)S(1)}, u32[]{:S(2)}, u32[]{:S(2)}) collective-permute-start(bf16[288,1024]{1,0:T(8,128)(2,1)S(1)} %collective-permute-done.30.refs_1_), channel_id=1, source_target_pairs={{0,4},{1,5},{2,6},{3,7},{4,8},{5,9},{6,10},{7,11},{8,12},{9,13},{1... | collective-permute-start | bytes 1769480 | tf_op jit(solution)/shard_map/ppermute | solution.py:30
  81.6 29.9 %collective-permute-start.15 = (bf16[512,1024]{1,0:T(8,128)(2,1)S(1)}, bf16[512,1024]{1,0:T(8,128)(2,1)S(1)}, u32[]{:S(2)}, u32[]{:S(2)}) collective-permute-start(bf16[512,1024]{1,0:T(8,128)(2,1)S(1)} %collective-permute-done.14.refs_15_), channel_id=1, source_target_pairs={{0,16},{16,0},{32,48},{48,32},{64,80},{80,64},{96,112},{112,96},{1... | collective-permute-start | bytes 3145736 | tf_op jit(solution)/shard_map/ppermute | solution.py:30
  81.6 23.8 %collective-permute-start.9 = (bf16[288,1024]{1,0:T(8,128)(2,1)S(1)}, bf16[288,1024]{1,0:T(8,128)(2,1)S(1)}, u32[]{:S(2)}, u32[]{:S(2)}) collective-permute-start(bf16[288,1024]{1,0:T(8,128)(2,1)S(1)} %collective-permute-done.5.refs_5_), channel_id=1, source_target_pairs={{0,12},{1,13},{2,14},{3,15},{4,0},{5,1},{6,2},{7,3},{8,4},{9,5},{1... | collective-permute-start | bytes 1769480 | tf_op jit(solution)/shard_map/ppermute | solution.py:30
  93.6 26.6 %collective-permute-start.16 = (bf16[512,1024]{1,0:T(8,128)(2,1)S(1)}, bf16[512,1024]{1,0:T(8,128)(2,1)S(1)}, u32[]{:S(2)}, u32[]{:S(2)}) collective-permute-start(bf16[512,1024]{1,0:T(8,128)(2,1)S(1)} %collective-permute-done.14.refs_15_), channel_id=1, source_target_pairs={{0,96},{16,112},{32,0},{48,16},{64,32},{80,48},{96,64},{112,80},{1... | collective-permute-start | bytes 3145736 | tf_op jit(solution)/shard_map/ppermute | solution.py:30
  96.6 13.3 %collective-permute-start.10 = (bf16[288,1024]{1,0:T(8,128)(2,1)S(1)}, bf16[288,1024]{1,0:T(8,128)(2,1)S(1)}, u32[]{:S(2)}, u32[]{:S(2)}) collective-permute-start(bf16[288,1024]{1,0:T(8,128)(2,1)S(1)} %collective-permute-done.8.refs_7_), channel_id=1, source_target_pairs={{0,3},{1,2},{2,1},{3,0},{4,7},{5,6},{6,5},{7,4},{8,11},{9,10},{10,... | collective-permute-start | bytes 1769480 | tf_op jit(solution)/shard_map/ppermute | solution.py:30
  98.5 11.4 %collective-permute-start.38 = (bf16[288,1024]{1,0:T(8,128)(2,1)S(1)}, bf16[288,1024]{1,0:T(8,128)(2,1)S(1)}, u32[]{:S(2)}, u32[]{:S(2)}) collective-permute-start(bf16[288,1024]{1,0:T(8,128)(2,1)S(1)} %collective-permute-done.37.refs_12_), channel_id=1, source_target_pairs={{0,4},{1,5},{2,6},{3,7},{4,8},{5,9},{6,10},{7,11},{8,12},{9,13},{1... | collective-permute-start | bytes 1769480 | tf_op jit(solution)/shard_map/ppermute | solution.py:30
  105.4 27.2 %collective-permute-start.18 = (bf16[512,1024]{1,0:T(8,128)(2,1)S(1)}, bf16[512,1024]{1,0:T(8,128)(2,1)S(1)}, u32[]{:S(2)}, u32[]{:S(2)}) collective-permute-start(bf16[512,1024]{1,0:T(8,128)(2,1)S(1)} %collective-permute-done.14.refs_15_), channel_id=1, source_target_pairs={{0,32},{16,48},{32,64},{48,80},{64,96},{80,112},{96,0},{112,16},{1... | collective-permute-start | bytes 3145736 | tf_op jit(solution)/shard_map/ppermute | solution.py:30
  109.9 24.4 %collective-permute-start.23 = (bf16[512,1024]{1,0:T(8,128)(2,1)S(1)}, bf16[512,1024]{1,0:T(8,128)(2,1)S(1)}, u32[]{:S(2)}, u32[]{:S(2)}) collective-permute-start(bf16[512,1024]{1,0:T(8,128)(2,1)S(1)} %collective-permute-done.22.refs_23_), channel_id=1, source_target_pairs={{0,16},{16,0},{32,48},{48,32},{64,80},{80,64},{96,112},{112,96},{1... | collective-permute-start | bytes 3145736 | tf_op jit(solution)/shard_map/ppermute | solution.py:30
  110.0 28.9 %collective-permute-start.24 = (bf16[512,1024]{1,0:T(8,128)(2,1)S(1)}, bf16[512,1024]{1,0:T(8,128)(2,1)S(1)}, u32[]{:S(2)}, u32[]{:S(2)}) collective-permute-start(bf16[512,1024]{1,0:T(8,128)(2,1)S(1)} %collective-permute-done.22.refs_23_), channel_id=1, source_target_pairs={{0,96},{16,112},{32,0},{48,16},{64,32},{80,48},{96,64},{112,80},{1... | collective-permute-start | bytes 3145736 | tf_op jit(solution)/shard_map/ppermute | solution.py:30
  111.6 45.3 %collective-permute-start.6 = (bf16[576,1024]{1,0:T(8,128)(2,1)S(1)}, bf16[576,1024]{1,0:T(8,128)(2,1)S(1)}, u32[]{:S(2)}, u32[]{:S(2)}) collective-permute-start(bf16[576,1024]{1,0:T(8,128)(2,1)S(1)} %constant_dynamic-update-slice_fusion), channel_id=1, source_target_pairs={{0,12},{1,13},{2,14},{3,15},{4,0},{5,1},{6,2},{7,3},{8,4},{9,5},{1... | collective-permute-start | bytes 3538952 | tf_op jit(solution)/shard_map/ppermute | solution.py:30
  120.1 34.9 %collective-permute-start.28 = (bf16[512,1024]{1,0:T(8,128)(2,1)S(1)}, bf16[512,1024]{1,0:T(8,128)(2,1)S(1)}, u32[]{:S(2)}, u32[]{:S(2)}) collective-permute-start(bf16[512,1024]{1,0:T(8,128)(2,1)S(1)} %collective-permute-done.22.refs_23_), channel_id=1, source_target_pairs={{0,32},{16,48},{32,64},{48,80},{64,96},{80,112},{96,0},{112,16},{1... | collective-permute-start | bytes 3145736 | tf_op jit(solution)/shard_map/ppermute | solution.py:30
  132.6 35.5 %collective-permute-start.13 = (bf16[576,1024]{1,0:T(8,128)(2,1)S(1)}, bf16[576,1024]{1,0:T(8,128)(2,1)S(1)}, u32[]{:S(2)}, u32[]{:S(2)}) collective-permute-start(bf16[576,1024]{1,0:T(8,128)(2,1)S(1)} %constant_dynamic-update-slice_fusion), channel_id=1, source_target_pairs={{0,4},{1,5},{2,6},{3,7},{4,8},{5,9},{6,10},{7,11},{8,12},{9,13},{1... | collective-permute-start | bytes 3538952 | tf_op jit(solution)/shard_map/ppermute | solution.py:30
  134.4 34.2 %collective-permute-start.17 = (bf16[512,1024]{1,0:T(8,128)(2,1)S(1)}, bf16[512,1024]{1,0:T(8,128)(2,1)S(1)}, u32[]{:S(2)}, u32[]{:S(2)}) collective-permute-start(bf16[512,1024]{1,0:T(8,128)(2,1)S(1)} %collective-permute-done.16.refs_17_), channel_id=1, source_target_pairs={{0,16},{16,0},{32,48},{48,32},{64,80},{80,64},{96,112},{112,96},{1... | collective-permute-start | bytes 3145736 | tf_op jit(solution)/shard_map/ppermute | solution.py:30
  138.8 34.9 %collective-permute-start.19 = (bf16[512,1024]{1,0:T(8,128)(2,1)S(1)}, bf16[512,1024]{1,0:T(8,128)(2,1)S(1)}, u32[]{:S(2)}, u32[]{:S(2)}) collective-permute-start(bf16[512,1024]{1,0:T(8,128)(2,1)S(1)} %collective-permute-done.18.refs_21_), channel_id=1, source_target_pairs={{0,32},{16,48},{32,64},{48,80},{64,96},{80,112},{96,0},{112,16},{1... | collective-permute-start | bytes 3145736 | tf_op jit(solution)/shard_map/ppermute | solution.py:30
  155.1 18.6 %collective-permute-start.26 = (bf16[512,1024]{1,0:T(8,128)(2,1)S(1)}, bf16[512,1024]{1,0:T(8,128)(2,1)S(1)}, u32[]{:S(2)}, u32[]{:S(2)}) collective-permute-start(bf16[512,1024]{1,0:T(8,128)(2,1)S(1)} %collective-permute-done.24.refs_25_), channel_id=1, source_target_pairs={{0,96},{16,112},{32,0},{48,16},{64,32},{80,48},{96,64},{112,80},{1... | collective-permute-start | bytes 3145736 | tf_op jit(solution)/shard_map/ppermute | solution.py:30
  156.9 11.2 %collective-permute-start.11 = (bf16[288,1024]{1,0:T(8,128)(2,1)S(1)}, bf16[288,1024]{1,0:T(8,128)(2,1)S(1)}, u32[]{:S(2)}, u32[]{:S(2)}) collective-permute-start(bf16[288,1024]{1,0:T(8,128)(2,1)S(1)} %collective-permute-done.9.refs_8_), channel_id=1, source_target_pairs={{0,3},{1,2},{2,1},{3,0},{4,7},{5,6},{6,5},{7,4},{8,11},{9,10},{10,... | collective-permute-start | bytes 1769480 | tf_op jit(solution)/shard_map/ppermute | solution.py:30
  168.6 12.7 %collective-permute-start.29 = (bf16[512,1024]{1,0:T(8,128)(2,1)S(1)}, bf16[512,1024]{1,0:T(8,128)(2,1)S(1)}, u32[]{:S(2)}, u32[]{:S(2)}) collective-permute-start(bf16[512,1024]{1,0:T(8,128)(2,1)S(1)} %collective-permute-done.28.refs_29_), channel_id=1, source_target_pairs={{0,16},{16,0},{32,48},{48,32},{64,80},{80,64},{96,112},{112,96},{1... | collective-permute-start | bytes 3145736 | tf_op jit(solution)/shard_map/ppermute | solution.py:30
  173.8 12.6 %collective-permute-start.27 = (bf16[512,1024]{1,0:T(8,128)(2,1)S(1)}, bf16[512,1024]{1,0:T(8,128)(2,1)S(1)}, u32[]{:S(2)}, u32[]{:S(2)}) collective-permute-start(bf16[512,1024]{1,0:T(8,128)(2,1)S(1)} %collective-permute-done.26.refs_27_), channel_id=1, source_target_pairs={{0,16},{16,0},{32,48},{48,32},{64,80},{80,64},{96,112},{112,96},{1... | collective-permute-start | bytes 3145736 | tf_op jit(solution)/shard_map/ppermute | solution.py:30
  176.2 35.7 %collective-permute-start.34 = (bf16[288,1024]{1,0:T(8,128)(2,1)S(1)}, bf16[288,1024]{1,0:T(8,128)(2,1)S(1)}, u32[]{:S(2)}, u32[]{:S(2)}) collective-permute-start(bf16[288,1024]{1,0:T(8,128)(2,1)S(1)} %collective-permute-done.30.refs_1_), channel_id=1, source_target_pairs={{0,12},{1,13},{2,14},{3,15},{4,0},{5,1},{6,2},{7,3},{8,4},{9,5},{1... | collective-permute-start | bytes 1769480 | tf_op jit(solution)/shard_map/ppermute | solution.py:30
  177.6 39.3 %collective-permute-start.35 = (bf16[576,1024]{1,0:T(8,128)(2,1)}, bf16[576,1024]{1,0:T(8,128)(2,1)S(1)}, u32[]{:S(2)}, u32[]{:S(2)}) collective-permute-start(bf16[576,1024]{1,0:T(8,128)(2,1)} %constant_dynamic-update-slice_fusion.2), channel_id=1, source_target_pairs={{0,12},{1,13},{2,14},{3,15},{4,0},{5,1},{6,2},{7,3},{8,4},{9,5},{1... | collective-permute-start | bytes 3538952 | tf_op jit(solution)/shard_map/ppermute | solution.py:30
  181.3 35.6 %collective-permute-start.42 = (bf16[576,1024]{1,0:T(8,128)(2,1)}, bf16[576,1024]{1,0:T(8,128)(2,1)}, u32[]{:S(2)}, u32[]{:S(2)}) collective-permute-start(bf16[576,1024]{1,0:T(8,128)(2,1)} %constant_dynamic-update-slice_fusion.2), channel_id=1, source_target_pairs={{0,4},{1,5},{2,6},{3,7},{4,8},{5,9},{6,10},{7,11},{8,12},{9,13},{1... | collective-permute-start | bytes 3538952 | tf_op jit(solution)/shard_map/ppermute | solution.py:30
  181.3 30.7 %collective-permute-start.39 = (bf16[288,1024]{1,0:T(8,128)(2,1)S(1)}, bf16[288,1024]{1,0:T(8,128)(2,1)S(1)}, u32[]{:S(2)}, u32[]{:S(2)}) collective-permute-start(bf16[288,1024]{1,0:T(8,128)(2,1)S(1)} %collective-permute-done.36.refs_7_), channel_id=1, source_target_pairs={{0,3},{1,2},{2,1},{3,0},{4,7},{5,6},{6,5},{7,4},{8,11},{9,10},{10,... | collective-permute-start | bytes 1769480 | tf_op jit(solution)/shard_map/ppermute | solution.py:30
  186.4 30.5 %collective-permute-start.40 = (bf16[288,1024]{1,0:T(8,128)(2,1)S(1)}, bf16[288,1024]{1,0:T(8,128)(2,1)S(1)}, u32[]{:S(2)}, u32[]{:S(2)}) collective-permute-start(bf16[288,1024]{1,0:T(8,128)(2,1)S(1)} %collective-permute-done.38.refs_8_), channel_id=1, source_target_pairs={{0,3},{1,2},{2,1},{3,0},{4,7},{5,6},{6,5},{7,4},{8,11},{9,10},{10,... | collective-permute-start | bytes 1769480 | tf_op jit(solution)/shard_map/ppermute | solution.py:30
  211.9 34.9 %collective-permute-start.43 = (bf16[2,144,1024]{2,1,0:T(8,128)(2,1)S(1)}, bf16[2,144,1024]{2,1,0:T(8,128)(2,1)S(1)}, u32[]{:S(2)}, u32[]{:S(2)}) collective-permute-start(bf16[2,144,1024]{2,1,0:T(8,128)(2,1)S(1)} %get-tuple-element.22), channel_id=1, source_target_pairs={{0,48},{1,33},{2,34},{3,51},{4,52},{5,37},{6,38},{7,55},{8,56},{9,... | collective-permute-start | bytes 1769480 | tf_op jit(solution)/shard_map/ppermute | solution.py:30
  212.0 34.8 %collective-permute-start.44 = (bf16[2,144,1024]{2,1,0:T(8,128)(2,1)S(1)}, bf16[2,144,1024]{2,1,0:T(8,128)(2,1)S(1)}, u32[]{:S(2)}, u32[]{:S(2)}) collective-permute-start(bf16[2,144,1024]{2,1,0:T(8,128)(2,1)S(1)} %get-tuple-element.23), channel_id=1, source_target_pairs={{0,96},{1,113},{2,114},{3,99},{4,100},{5,117},{6,118},{7,103},{8,1... | collective-permute-start | bytes 1769480 | tf_op jit(solution)/shard_map/ppermute | solution.py:30
  241.2 18.4 %collective-permute-start.45 = (bf16[144,1024]{1,0:T(8,128)(2,1)S(1)}, bf16[144,1024]{1,0:T(8,128)(2,1)S(1)}, u32[]{:S(2)}, u32[]{:S(2)}) collective-permute-start(bf16[144,1024]{1,0:T(8,128)(2,1)S(1)} %get-tuple-element.24), channel_id=1, source_target_pairs={{0,64},{1,81},{2,82},{3,67},{4,68},{5,85},{6,86},{7,71},{8,72},{9,... | collective-permute-start | bytes 884744 | tf_op jit(solution)/shard_map/ppermute | solution.py:30
  243.2 15.8 %collective-permute-start.46 = (bf16[2,144,1024]{2,1,0:T(8,128)(2,1)S(1)}, bf16[2,144,1024]{2,1,0:T(8,128)(2,1)S(1)}, u32[]{:S(2)}, u32[]{:S(2)}) collective-permute-start(bf16[2,144,1024]{2,1,0:T(8,128)(2,1)S(1)} %get-tuple-element.25), channel_id=1, source_target_pairs={{0,16},{1,1},{2,2},{3,19},{4,20},{5,5},{6,6},{7,23},{8,24},{9,9},{... | collective-permute-start | bytes 1769480 | tf_op jit(solution)/shard_map/ppermute | solution.py:30
  245.1 12.2 %collective-permute-start.48 = (bf16[144,1024]{1,0:T(8,128)(2,1)S(1)}, bf16[144,1024]{1,0:T(8,128)(2,1)S(1)}, u32[]{:S(2)}, u32[]{:S(2)}) collective-permute-start(bf16[144,1024]{1,0:T(8,128)(2,1)S(1)} %get-tuple-element.26), channel_id=1, source_target_pairs={{0,64},{1,81},{2,82},{3,67},{4,68},{5,85},{6,86},{7,71},{8,72},{9,... | collective-permute-start | bytes 884744 | tf_op jit(solution)/shard_map/ppermute | solution.py:30
  247.9 28.1 %collective-permute-start.47 = (bf16[288,1024]{1,0:T(8,128)(2,1)S(1)}, bf16[288,1024]{1,0:T(8,128)(2,1)S(1)}, u32[]{:S(2)}, u32[]{:S(2)}) collective-permute-start(bf16[288,1024]{1,0:T(8,128)(2,1)S(1)} %pad_maximum_fusion), channel_id=1, source_target_pairs={{0,1},{1,0},{2,3},{3,2},{4,5},{5,4},{6,7},{7,6},{8,9},{9,8},{10,11... | collective-permute-start | bytes 1769480 | tf_op jit(solution)/shard_map/ppermute | solution.py:30
  257.4 13.0 %collective-permute-start.49 = (bf16[144,1024]{1,0:T(8,128)(2,1)S(1)}, bf16[144,1024]{1,0:T(8,128)(2,1)S(1)}, u32[]{:S(2)}, u32[]{:S(2)}) collective-permute-start(bf16[144,1024]{1,0:T(8,128)(2,1)S(1)} %fusion.1), channel_id=1, source_target_pairs={{0,1},{1,0},{2,3},{3,2},{4,5},{5,4},{6,7},{7,6},{8,9},{9,8},{10,11... | collective-permute-start | bytes 884744 | tf_op jit(solution)/shard_map/ppermute | solution.py:30
  259.0 17.0 %collective-permute-start.50 = (bf16[144,1024]{1,0:T(8,128)(2,1)S(1)}, bf16[144,1024]{1,0:T(8,128)(2,1)S(1)}, u32[]{:S(2)}, u32[]{:S(2)}) collective-permute-start(bf16[144,1024]{1,0:T(8,128)(2,1)S(1)} %fusion.4), channel_id=1, source_target_pairs={{0,1},{1,0},{2,3},{3,2},{4,5},{5,4},{6,7},{7,6},{8,9},{9,8},{10,11... | collective-permute-start | bytes 884744 | tf_op jit(solution)/shard_map/ppermute | solution.py:30
  (41 other events, 1116.8 us)

commit v3 on v2

--- a/solution.py
+++ b/solution.py
@@ -61,10 +61,10 @@
 
 
 def any_spec():
-    return pl.BlockSpec(memory_space=pl.ANY)
-
-
-LANES = 256
+    return pl.BlockSpec(memory_space=pltpu.HBM)
+
+
+LANES = 512
 
 
 def split_kernel(a_ref, *refs):
@@ -141,6 +141,7 @@
 
 
 NBUF = 3
+PARTS = ((0, 576), (576, 448))
 
 
 PLACE = tuple((k, 0) for k in range(4)) + ((4, 0), (5, 0), (6, 0), (6, 1)) + tuple((k, 0) for k in (7, 8, 9, 10)) + (
@@ -149,12 +150,13 @@
 
 
 FULL = (1 << 16) - 1
-LATE = 1 << 6 | 1 << 7 | 1 << 14 | 1 << 15
-
-
-def ladder_kernel(blocks, mask, sides, resumed, final, apart, own_list, own_count, far, *refs):
+LATE_A = 1 << 6 | 1 << 7 | 1 << 11
+LATE_B = LATE_A | 1 << 14 | 1 << 15
+
+
+def ladder_kernel(blocks, masks, resumed, final, apart, own_list, own_count, far, *refs):
     arrays, refs = refs[:ARRAYS], refs[ARRAYS:]
-    far_n = 16 if sides[1] == 2 else 0
+    far_n = 16 if masks[1] else 0
     own_int, far_int, refs = refs[0], refs[1:1 + far_n], refs[1 + far_n:]
     if resumed:
         before, refs = refs[0], refs[1:]
@@ -170,7 +172,7 @@
     x, z = lax.rem(v, 4), lax.div(v, 4)
     y, c = lax.div(o, 2), lax.rem(o, 2)
     count0, count1 = own_count[0], far[8]
-    used = [q for q in range(16) if mask >> q & 1]
+    used = [q for q in range(16) if (masks[0] | masks[1]) >> q & 1]
 
     def note(t, n):
         near = t < CD_MAX
@@ -178,6 +180,7 @@
         tile = jnp.where(near, own_list[s], far[s])
         flip = lax.rem(tile, 4) ^ x
         q = ((lax.div(tile, 4) - z) & 3) * 4 + (flip ^ lax.div(flip, 2))
+        mask = jnp.where(near, masks[0], masks[1])
         live = (s < jnp.where(near, count0, count1)) & ((lax.shift_right_logical(mask, q) & 1) == 1)
 
         @pl.when(live)
@@ -186,7 +189,8 @@
 
         return n + jnp.where(live, 1, 0)
 
-    total = lax.fori_loop(sides[0] * CD_MAX, sides[1] * CD_MAX, note, jnp.int32(0))
+    total = lax.fori_loop(
+        0 if masks[0] else CD_MAX, 2 * CD_MAX if masks[1] else CD_MAX, note, jnp.int32(0))
 
     def fetch(item):
         t = lax.div(work[item], 16)
@@ -203,10 +207,10 @@
         for rel in range(far_n // 2):
             @pl.when(jnp.logical_not(near) & (dy * 2 + dc == rel))
             def _():
-                for part in range(2):
+                for part, (at, size) in enumerate(PARTS):
                     pltpu.make_async_copy(
                         far_int[part * 8 + rel],
-                        ints.at[slot, pl.ds(part * (K // 2), K // 2), :],
+                        ints.at[slot, pl.ds(at, size), :],
                         int_sem.at[slot]).start()
 
     for ahead in range(NBUF - 1):
@@ -260,10 +264,12 @@
                 mirrors[b + apart][1 - side] = image
 
 
-def ladder_chunk(blocks, own_list, own_count, far, arrays, own_int, far_int, swaps=(), before=None, mask=FULL, apart=0,
-                 sides=(0, 2)):
+def ladder_chunk(blocks, own_list, own_count, far, arrays, own_int, far_int, swaps=(), before=None, masks=(FULL, FULL),
+                 apart=0):
     rows = blocks * BLK
     final = bool(swaps)
+    needed = {k for q, (k, _) in enumerate(PLACE) if (masks[0] | masks[1]) >> q & 1}
+    arrays = [t if k in needed else arrays[0] for k, t in enumerate(arrays)]
     vmem = pl.BlockSpec(memory_space=pltpu.VMEM)
     sums = jax.ShapeDtypeStruct((2, rows, K), F32)
     if final:
@@ -275,7 +281,7 @@
     extra = ([] if before is None else [before]) + list(swaps)
     extra_specs = ([] if before is None else [vmem]) + ([any_spec(), vmem] if final else [])
     outs = pl.pallas_call(
-        functools.partial(ladder_kernel, blocks, mask, sides, before is not None, final, apart),
+        functools.partial(ladder_kernel, blocks, masks, before is not None, final, apart),
         grid_spec=pltpu.PrefetchScalarGridSpec(
             num_scalar_prefetch=3,
             grid=(),
@@ -296,6 +302,12 @@
     return outs
 
 
+def swap_matrix(n):
+    row = lax.broadcasted_iota(jnp.int32, (n * n, n * n), 0)
+    col = lax.broadcasted_iota(jnp.int32, (n * n, n * n), 1)
+    return (row == (col % n) * n + col // n).astype(BF)
+
+
 def gather_chunk(own, sent, way):
     um, dm = z_perm(own, 1), z_perm(own, -1)
     mg = group_perm(own)
@@ -313,8 +325,8 @@
 def gather_integrals(blocks):
     me = lax.axis_index("occ")
     halves = []
-    for part in range(2):
-        mine = lax.dynamic_slice(blocks, (me, part * (K // 2), 0), (1, K // 2, K))[0]
+    for part, (at, size) in enumerate(PARTS):
+        mine = lax.dynamic_slice(blocks, (me, at, 0), (1, size, K))[0]
         b = pair_perm(mine)
         up = y_perm(b, 1)
         down = y_perm(b, -1)
@@ -328,10 +340,7 @@
     listed = cd_tiles[0]
     blocks = integrals[0]
     far = pair_perm(jnp.concatenate([listed, cd_count, jnp.zeros((7,), jnp.int32)]))
-    col = jnp.arange(K, dtype=jnp.int32)
-    swap_cols = (col[:, None] == ((col % TW) * TW + col // TW)[None, :]).astype(BF)
-    row = jnp.arange(BLK, dtype=jnp.int32)
-    swap_rows = (row[:, None] == ((row % OI) * OI + row // OI)[None, :]).astype(BF)
+    swap_cols, swap_rows = swap_matrix(TW), swap_matrix(OI)
     split = split_rows(amplitudes)
     far_int = gather_integrals(blocks)
     swaps = (swap_cols, swap_rows)
@@ -340,17 +349,18 @@
         return (near.astype(F32) + mirrored.astype(F32)).astype(BF)
 
     a_in = gather_chunk(split[0], split[NCH], 1)
-    sums, = ladder_chunk(2, listed, cd_count, far, a_in, blocks, (), sides=(0, 1))
+    sums, = ladder_chunk(2, listed, cd_count, far, a_in, blocks, (), masks=(FULL & ~LATE_A, 0))
     a_lad, a_first, a_second = ladder_chunk(
-        2, listed, cd_count, far, a_in, blocks, far_int, swaps, sums, sides=(1, 2))
+        2, listed, cd_count, far, a_in, blocks, far_int, swaps, sums, (LATE_A, FULL))
     a_got = [mirror_perm(a_first, 0), mirror_perm(a_second, 1)]
     a_there = jnp.concatenate([join(a_lad[1, :BLK], a_got[0][1]), join(a_lad[1, BLK:], a_got[1][1])], 0)
     a_out = pair_perm(a_there)
 
     b_in = gather_chunk(split[1], split[NCH + 1], -1)
-    sums, = ladder_chunk(2, listed, cd_count, far, b_in, blocks, far_int, mask=FULL & ~LATE)
+    sums, = ladder_chunk(2, listed, cd_count, far, b_in, blocks, far_int,
+                         masks=(FULL & ~LATE_B, FULL & ~LATE_B))
     b_lad, b_near, b_far, b_second = ladder_chunk(
-        2, listed, cd_count, far, b_in, blocks, far_int, swaps, sums, LATE, 1)
+        2, listed, cd_count, far, b_in, blocks, far_int, swaps, sums, (LATE_B, LATE_B), 1)
     b_got3 = mirror_perm(b_second, 3)
     b_far = mirror_perm(b_far, 2)
     b_near = mirror_perm(b_near, 2)

time: 286 us -> 277 us (0.969)
  waiting for transfers between devices: 154 us -> 149 us
  starting transfers between devices: 60.6 us -> 57.6 us
  local copies, waits for them, and re-layouts: 6.78 us -> 9.7 us
    ppermute x51, waiting for transfers between devices: 154 us -> 149 us  [permute(): return lax.ppermute(value, axis, pairs)]
    ppermute x51, starting transfers between devices: 60.6 us -> 57.6 us  [permute(): return lax.ppermute(value, axis, pairs)]
    unnamed x78 -> x84, local copies, waits for them, and re-layouts: 4.13 us -> 6.21 us
  transfers between devices with their start and end apart: 51 -> 51, of which waited for: 19 -> 17; matrix products, arithmetic and copies ran while one was open for 2% -> 3% of each run, Pallas kernels for 17% -> 17%
where the time goes in v3:
time: 277 us; the launch traced here: 274 us
  waiting for transfers between devices  149 us (54%)
  starting transfers between devices  57.6 us (21%)
  Pallas kernels  54.5 us (20%)
  local copies, waits for them, and re-layouts  9.7 us (4%)
    ppermute x51, waiting for transfers between devices, permute(): return lax.ppermute(value, axis, pairs)  149 us
    ppermute x51, starting transfers between devices, permute(): return lax.ppermute(value, axis, pairs)  57.6 us
    pallas_call x4, Pallas kernels, ladder_chunk(): pl.pallas_call(functools.partial(ladder_kernel, blocks, masks, before is...  47.2 us
    unnamed x84, local copies, waits for them, and re-layouts  6.21 us
  transfers between devices with their start and end apart: 51, of which 17 were waited for; matrix products, arithmetic and copies ran while one was open for 3% of the time, Pallas kernels for 17%

profile of v3, /device:TPU:38, one launch (start us, length us, event | category | flops | bytes accessed | tf_op | source)
XLA Modules:
  0.0 274.3 jit_solution(1017185114170112473)
XLA Ops:
  0.0 3.4 %split_rows.1 = (bf16[288,1024]{1,0:T(8,128)(2,1)}, bf16[288,1024]{1,0:T(8,128)(2,1)}, bf16[288,1024]{1,0:T(8,128)(2,1)}, bf16[288,1024]{1,0:T(8,128)(2,1)}) custom-call(bf16[1152,1024]{1,0:T(8,128)(2,1)} %a_ref.1), custom_call_target="tpu_custom_call" | custom-call | tf_op jit(solution)/shard_map/split_rows/pallas_call | solution.py:95
  4.3 1.1 collective-permute-start.2
  5.5 1.9 collective-permute-start.7
  8.3 10.5 %collective-permute-done.far = s32[16]{0:T(128)S(1)} collective-permute-done((s32[16]{0:T(128)S(1)}, s32[16]{0:T(128)S(1)}, u32[]{:S(2)}, u32[]{:S(2)}) %collective-permute-start) | collective-permute-done | bytes 96 | tf_op jit(solution)/shard_map/ppermute | solution.py:30
  20.6 1.2 dynamic-slice_bitcast_fusion.1
  22.7 2.1 collective-permute-start.42
  24.7 1.4 dynamic-slice_bitcast_fusion
  26.1 8.3 %collective-permute-done.30.refs_2_ = bf16[288,1024]{1,0:T(8,128)(2,1)S(1)} collective-permute-done((bf16[288,1024]{1,0:T(8,128)(2,1)}, bf16[288,1024]{1,0:T(8,128)(2,1)S(1)}, u32[]{:S(2)}, u32[]{:S(2)}) %collective-permute-start.30) | collective-permute-done | bytes 589856 | tf_op jit(solution)/shard_map/ppermute | solution.py:30
  34.4 1.4 collective-permute-done.31.refs_1_
  35.8 2.8 %collective-permute-start.3 = (bf16[288,1024]{1,0:T(8,128)(2,1)S(1)}, bf16[288,1024]{1,0:T(8,128)(2,1)S(1)}, u32[]{:S(2)}, u32[]{:S(2)}) collective-permute-start(bf16[288,1024]{1,0:T(8,128)(2,1)S(1)} %collective-permute-done.1.refs_1_), channel_id=1, source_target_pairs={{0,3},{1,2},{2,1},{3,0},{4,7},{5,6},{6,5},{7,4},{8,11},{9,10},{10,... | collective-permute-start | bytes 1769480 | tf_op jit(solution)/shard_map/ppermute | solution.py:30
  38.7 1.9 collective-permute-start.8
  40.6 14.8 %collective-permute-done.22.refs_23_ = bf16[448,1024]{1,0:T(8,128)(2,1)S(1)} collective-permute-done((bf16[448,1024]{1,0:T(8,128)(2,1)S(1)}, bf16[448,1024]{1,0:T(8,128)(2,1)S(1)}, u32[]{:S(2)}, u32[]{:S(2)}) %collective-permute-start.22) | collective-permute-done | bytes 917536 | tf_op jit(solution)/shard_map/ppermute | solution.py:30
  55.4 1.9 collective-permute-start.12
  57.3 2.8 %collective-permute-start.32 = (bf16[288,1024]{1,0:T(8,128)(2,1)}, bf16[288,1024]{1,0:T(8,128)(2,1)S(1)}, u32[]{:S(2)}, u32[]{:S(2)}) collective-permute-start(bf16[288,1024]{1,0:T(8,128)(2,1)} %collective-permute-done.31.refs_1_), channel_id=1, source_target_pairs={{0,3},{1,2},{2,1},{3,0},{4,7},{5,6},{6,5},{7,4},{8,11},{9,10},{10,... | collective-permute-start | bytes 1769480 | tf_op jit(solution)/shard_map/ppermute | solution.py:30
  60.0 1.6 collective-permute-start.34
  62.1 9.5 %collective-permute-done.12.refs_12_ = bf16[288,1024]{1,0:T(8,128)(2,1)S(1)} collective-permute-done((bf16[288,1024]{1,0:T(8,128)(2,1)S(1)}, bf16[288,1024]{1,0:T(8,128)(2,1)S(1)}, u32[]{:S(2)}, u32[]{:S(2)}) %collective-permute-start.12) | collective-permute-done | bytes 589856 | tf_op jit(solution)/shard_map/ppermute | solution.py:30
  71.6 2.1 collective-permute-start.9
  73.7 4.6 %collective-permute-done.14.refs_15_ = bf16[576,1024]{1,0:T(8,128)(2,1)S(1)} collective-permute-done((bf16[576,1024]{1,0:T(8,128)(2,1)S(1)}, bf16[576,1024]{1,0:T(8,128)(2,1)S(1)}, u32[]{:S(2)}, u32[]{:S(2)}) %collective-permute-start.14) | collective-permute-done | bytes 1179680 | tf_op jit(solution)/shard_map/ppermute | solution.py:30
  78.3 2.8 %collective-permute-start.10 = (bf16[288,1024]{1,0:T(8,128)(2,1)S(1)}, bf16[288,1024]{1,0:T(8,128)(2,1)S(1)}, u32[]{:S(2)}, u32[]{:S(2)}) collective-permute-start(bf16[288,1024]{1,0:T(8,128)(2,1)S(1)} %collective-permute-done.8.refs_7_), channel_id=1, source_target_pairs={{0,3},{1,2},{2,1},{3,0},{4,7},{5,6},{6,5},{7,4},{8,11},{9,10},{10,... | collective-permute-start | bytes 1769480 | tf_op jit(solution)/shard_map/ppermute | solution.py:30
  81.1 1.9 collective-permute-start.35
  84.1 3.0 %collective-permute-start.24 = (bf16[448,1024]{1,0:T(8,128)(2,1)S(1)}, bf16[448,1024]{1,0:T(8,128)(2,1)S(1)}, u32[]{:S(2)}, u32[]{:S(2)}) collective-permute-start(bf16[448,1024]{1,0:T(8,128)(2,1)S(1)} %collective-permute-done.22.refs_23_), channel_id=1, source_target_pairs={{0,96},{16,112},{32,0},{48,16},{64,32},{80,48},{96,64},{112,80},{1... | collective-permute-start | bytes 2752520 | tf_op jit(solution)/shard_map/ppermute | solution.py:30
  87.1 8.1 %collective-permute-done.10.refs_9_ = bf16[288,1024]{1,0:T(8,128)(2,1)S(1)} collective-permute-done((bf16[288,1024]{1,0:T(8,128)(2,1)S(1)}, bf16[288,1024]{1,0:T(8,128)(2,1)S(1)}, u32[]{:S(2)}, u32[]{:S(2)}) %collective-permute-start.10) | collective-permute-done | bytes 589856 | tf_op jit(solution)/shard_map/ppermute | solution.py:30
  95.2 1.6 collective-permute-start.28
  96.8 1.6 collective-permute-start.18
  98.4 1.9 collective-permute-start.13
  100.3 5.6 %collective-permute-done.24.refs_25_ = bf16[448,1024]{1,0:T(8,128)(2,1)S(1)} collective-permute-done((bf16[448,1024]{1,0:T(8,128)(2,1)S(1)}, bf16[448,1024]{1,0:T(8,128)(2,1)S(1)}, u32[]{:S(2)}, u32[]{:S(2)}) %collective-permute-start.24) | collective-permute-done | bytes 917536 | tf_op jit(solution)/shard_map/ppermute | solution.py:30
  106.5 13.2 %collective-permute-done.28.refs_29_ = bf16[448,1024]{1,0:T(8,128)(2,1)S(1)} collective-permute-done((bf16[448,1024]{1,0:T(8,128)(2,1)S(1)}, bf16[448,1024]{1,0:T(8,128)(2,1)S(1)}, u32[]{:S(2)}, u32[]{:S(2)}) %collective-permute-start.28) | collective-permute-done | bytes 917536 | tf_op jit(solution)/shard_map/ppermute | solution.py:30
  119.7 1.8 collective-permute-start.16
  121.6 22.0 %collective-permute-done.18.refs_21_ = bf16[576,1024]{1,0:T(8,128)(2,1)S(1)} collective-permute-done((bf16[576,1024]{1,0:T(8,128)(2,1)S(1)}, bf16[576,1024]{1,0:T(8,128)(2,1)S(1)}, u32[]{:S(2)}, u32[]{:S(2)}) %collective-permute-start.18) | collective-permute-done | bytes 1179680 | tf_op jit(solution)/shard_map/ppermute | solution.py:30
  144.0 3.2 %collective-permute-start.26 = (bf16[448,1024]{1,0:T(8,128)(2,1)S(1)}, bf16[448,1024]{1,0:T(8,128)(2,1)S(1)}, u32[]{:S(2)}, u32[]{:S(2)}) collective-permute-start(bf16[448,1024]{1,0:T(8,128)(2,1)S(1)} %collective-permute-done.24.refs_25_), channel_id=1, source_target_pairs={{0,96},{16,112},{32,0},{48,16},{64,32},{80,48},{96,64},{112,80},{1... | collective-permute-start | bytes 2752520 | tf_op jit(solution)/shard_map/ppermute | solution.py:30
  147.9 19.3 %collective-permute-done.26.refs_27_ = bf16[448,1024]{1,0:T(8,128)(2,1)S(1)} collective-permute-done((bf16[448,1024]{1,0:T(8,128)(2,1)S(1)}, bf16[448,1024]{1,0:T(8,128)(2,1)S(1)}, u32[]{:S(2)}, u32[]{:S(2)}) %collective-permute-start.26) | collective-permute-done | bytes 917536 | tf_op jit(solution)/shard_map/ppermute | solution.py:30
  167.2 4.3 %collective-permute-done.19.refs_19_ = bf16[576,1024]{1,0:T(8,128)(2,1)S(1)} collective-permute-done((bf16[576,1024]{1,0:T(8,128)(2,1)S(1)}, bf16[576,1024]{1,0:T(8,128)(2,1)S(1)}, u32[]{:S(2)}, u32[]{:S(2)}) %collective-permute-start.19) | collective-permute-done | bytes 1179680 | tf_op jit(solution)/shard_map/ppermute | solution.py:30
  171.5 1.0 constant_dynamic-update-slice_fusion.3
  173.8 3.8 %collective-permute-start.33 = (bf16[576,1024]{1,0:T(8,128)(2,1)}, bf16[576,1024]{1,0:T(8,128)(2,1)}, u32[]{:S(2)}, u32[]{:S(2)}) collective-permute-start(bf16[576,1024]{1,0:T(8,128)(2,1)} %constant_dynamic-update-slice_fusion.2), channel_id=1, source_target_pairs={{0,12},{1,13},{2,14},{3,15},{4,0},{5,1},{6,2},{7,3},{8,4},{9,5},{1... | collective-permute-start | bytes 3538952 | tf_op jit(solution)/shard_map/ppermute | solution.py:30
  177.7 2.8 %collective-permute-start.41 = (bf16[288,1024]{1,0:T(8,128)(2,1)S(1)}, bf16[288,1024]{1,0:T(8,128)(2,1)S(1)}, u32[]{:S(2)}, u32[]{:S(2)}) collective-permute-start(bf16[288,1024]{1,0:T(8,128)(2,1)S(1)} %collective-permute-done.40.refs_7_), channel_id=1, source_target_pairs={{0,3},{1,2},{2,1},{3,0},{4,7},{5,6},{6,5},{7,4},{8,11},{9,10},{10,... | collective-permute-start | bytes 1769480 | tf_op jit(solution)/shard_map/ppermute | solution.py:30
  180.6 2.0 fusion.refs_32_
  183.7 8.4 %shard_map.46.refs_31_ = f32[2,288,1024]{2,1,0:T(8,128)} custom-call(s32[8]{0:T(128)S(1)} %bitcast.17, s32[1]{0:T(128)S(6)} %copy.7.own_count, s32[16]{0:T(128)S(1)} %collective-permute-done.far, bf16[288,1024]{1,0:T(8,128)(2,1)S(1)} %copy-done.1, bf16[288,1024]{1,0:T(8,128)(2,1)S(1)} %collective-permute-done.1.refs_1_, ...), custom_call_target="tpu_custom_call" | custom-call | tf_op jit(solution)/shard_map/pallas_call | solution.py:283
  193.0 15.5 %shard_map.47 = (bf16[2,288,1024]{2,1,0:T(8,128)(2,1)}, bf16[2,144,1024]{2,1,0:T(8,128)(2,1)S(1)}, bf16[2,144,1024]{2,1,0:T(8,128)(2,1)S(1)}) custom-call(s32[8]{0:T(128)S(1)} %bitcast.18, s32[1]{0:T(128)S(6)} %copy.7.own_count, s32[16]{0:T(128)S(1)} %collective-permute-done.far, bf16[288,1024]{1,0:T(8,128)(2,1)S(1)} %copy-done.1, ...), custom_call_target="tpu_custom_call" | custom-call | tf_op jit(solution)/shard_map/pallas_call | solution.py:283
  210.0 1.3 copy-done.13
  211.3 13.5 %shard_map.48.refs_31_ = f32[2,288,1024]{2,1,0:T(8,128)} custom-call(s32[8]{0:T(128)S(1)} %bitcast.19, s32[1]{0:T(128)S(6)} %copy.7.own_count, s32[16]{0:T(128)S(1)} %collective-permute-done.far, bf16[288,1024]{1,0:T(8,128)(2,1)S(1)} %copy-done, bf16[288,1024]{1,0:T(8,128)(2,1)} %collective-permute-done.31.refs_1_, ...), custom_call_target="tpu_custom_call" | custom-call | tf_op jit(solution)/shard_map/pallas_call | solution.py:283
  224.9 9.8 %shard_map.49 = (bf16[2,288,1024]{2,1,0:T(8,128)(2,1)}, bf16[144,1024]{1,0:T(8,128)(2,1)S(1)}, bf16[144,1024]{1,0:T(8,128)(2,1)S(1)}, bf16[2,144,1024]{2,1,0:T(8,128)(2,1)S(1)}) custom-call(s32[8]{0:T(128)S(1)} %bitcast.20, s32[1]{0:T(128)S(6)} %copy.7.own_count, s32[16]{0:T(128)S(1)} %collective-permute-done.far, bf16[288,1024]{1,0:T(8,128)(2,1)S(1)} %copy-done, ...), custom_call_target="tpu_custom_call" | custom-call | tf_op jit(solution)/shard_map/pallas_call | solution.py:283
  234.7 2.6 collective-permute-start.45
  237.3 2.3 collective-permute-start.46
  241.3 10.5 %collective-permute-done.48 = bf16[144,1024]{1,0:T(8,128)(2,1)S(1)} collective-permute-done((bf16[144,1024]{1,0:T(8,128)(2,1)S(1)}, bf16[144,1024]{1,0:T(8,128)(2,1)S(1)}, u32[]{:S(2)}, u32[]{:S(2)}) %collective-permute-start.48) | collective-permute-done | bytes 294944 | tf_op jit(solution)/shard_map/ppermute | solution.py:30
  252.1 2.1 collective-permute-start.50
  254.2 9.7 %collective-permute-done.49.refs_8_ = bf16[144,1024]{1,0:T(8,128)(2,1)S(1)} collective-permute-done((bf16[144,1024]{1,0:T(8,128)(2,1)S(1)}, bf16[144,1024]{1,0:T(8,128)(2,1)S(1)}, u32[]{:S(2)}, u32[]{:S(2)}) %collective-permute-start.49) | collective-permute-done | bytes 294944 | tf_op jit(solution)/shard_map/ppermute | solution.py:30
  263.9 5.6 %collective-permute-done.50.refs_9_ = bf16[144,1024]{1,0:T(8,128)(2,1)S(1)} collective-permute-done((bf16[144,1024]{1,0:T(8,128)(2,1)S(1)}, bf16[144,1024]{1,0:T(8,128)(2,1)S(1)}, u32[]{:S(2)}, u32[]{:S(2)}) %collective-permute-start.50) | collective-permute-done | bytes 294944 | tf_op jit(solution)/shard_map/ppermute | solution.py:30
  270.3 3.9 %join_rows.1 = bf16[1152,1024]{1,0:T(8,128)(2,1)} custom-call(bf16[2,288,1024]{2,1,0:T(8,128)(2,1)} %get-tuple-element.18.refs_0_, bf16[2,288,1024]{2,1,0:T(8,128)(2,1)} %get-tuple-element.21.refs_1_, bf16[2,144,1024]{2,1,0:T(8,128)(2,1)} %copy-done.32, bf16[2,144,1024]{2,1,0:T(8,128)(2,1)} %copy-done.33, bf16[1,144,1024]{2,1,0:T(8,128)(2,1)} %bitcast.25, ...), custom_call_target="tpu_custom_call" | custom-call | tf_op jit(solution)/shard_map/join_rows/pallas_call | solution.py:132
  (162 shorter events, 14.4 us)
Async XLA Ops:
  3.4 15.9 %collective-permute-start.1 = (bf16[288,1024]{1,0:T(8,128)(2,1)}, bf16[288,1024]{1,0:T(8,128)(2,1)S(1)}, u32[]{:S(2)}, u32[]{:S(2)}) collective-permute-start(bf16[288,1024]{1,0:T(8,128)(2,1)} %get-tuple-element.17), channel_id=1, source_target_pairs={{0,1},{1,0},{2,3},{3,2},{4,5},{5,4},{6,7},{7,6},{8,9},{9,8},{10,11... | collective-permute-start | bytes 1769480 | tf_op jit(solution)/shard_map/ppermute | solution.py:30
  4.3 16.2 %collective-permute-start.2 = (bf16[288,1024]{1,0:T(8,128)(2,1)}, bf16[288,1024]{1,0:T(8,128)(2,1)S(1)}, u32[]{:S(2)}, u32[]{:S(2)}) collective-permute-start(bf16[288,1024]{1,0:T(8,128)(2,1)} %get-tuple-element.16.refs_0_.refs_6_.refs_10_), channel_id=1, source_target_pairs={{0,3},{1,2},{2,1},{3,0},{4,7},{5,6},{6,5},{7,4},{8,11},{9,10},{10,... | collective-permute-start | bytes 1769480 | tf_op jit(solution)/shard_map/ppermute | solution.py:30
  5.4 16.4 %collective-permute-start.4 = (bf16[288,1024]{1,0:T(8,128)(2,1)}, bf16[288,1024]{1,0:T(8,128)(2,1)S(1)}, u32[]{:S(2)}, u32[]{:S(2)}) collective-permute-start(bf16[288,1024]{1,0:T(8,128)(2,1)} %get-tuple-element.16.refs_0_.refs_6_.refs_10_), channel_id=1, source_target_pairs={{0,12},{1,13},{2,14},{3,15},{4,0},{5,1},{6,2},{7,3},{8,4},{9,5},{1... | collective-permute-start | bytes 1769480 | tf_op jit(solution)/shard_map/ppermute | solution.py:30
  5.5 17.1 %collective-permute-start.7 = (bf16[288,1024]{1,0:T(8,128)(2,1)}, bf16[288,1024]{1,0:T(8,128)(2,1)S(1)}, u32[]{:S(2)}, u32[]{:S(2)}) collective-permute-start(bf16[288,1024]{1,0:T(8,128)(2,1)} %get-tuple-element.16.refs_0_.refs_6_.refs_10_), channel_id=1, source_target_pairs={{0,4},{1,5},{2,6},{3,7},{4,8},{5,9},{6,10},{7,11},{8,12},{9,13},{1... | collective-permute-start | bytes 1769480 | tf_op jit(solution)/shard_map/ppermute | solution.py:30
  18.8 15.5 %collective-permute-start.30 = (bf16[288,1024]{1,0:T(8,128)(2,1)}, bf16[288,1024]{1,0:T(8,128)(2,1)S(1)}, u32[]{:S(2)}, u32[]{:S(2)}) collective-permute-start(bf16[288,1024]{1,0:T(8,128)(2,1)} %get-tuple-element.19.refs_0_.refs_6_.refs_10_.refs_13_.refs_1_.refs_2_.refs_3_.refs_4_.refs_5_.refs_7_.refs_8_.refs, ...), channel_id=1, source_target_pairs={{0,3},{1,2},{2,1},{3,0},{4,7},{5,6},{6,5},{7,4},{8,11},{9,10},{10,... | collective-permute-start | bytes 1769480 | tf_op jit(solution)/shard_map/ppermute | solution.py:30
  19.3 16.5 %collective-permute-start.31 = (bf16[288,1024]{1,0:T(8,128)(2,1)}, bf16[288,1024]{1,0:T(8,128)(2,1)}, u32[]{:S(2)}, u32[]{:S(2)}) collective-permute-start(bf16[288,1024]{1,0:T(8,128)(2,1)} %get-tuple-element.20), channel_id=1, source_target_pairs={{0,1},{1,0},{2,3},{3,2},{4,5},{5,4},{6,7},{7,6},{8,9},{9,8},{10,11... | collective-permute-start | bytes 1769480 | tf_op jit(solution)/shard_map/ppermute | solution.py:30
  20.5 18.1 %collective-permute-start.38 = (bf16[288,1024]{1,0:T(8,128)(2,1)}, bf16[288,1024]{1,0:T(8,128)(2,1)S(1)}, u32[]{:S(2)}, u32[]{:S(2)}) collective-permute-start(bf16[288,1024]{1,0:T(8,128)(2,1)} %get-tuple-element.19.refs_0_.refs_6_.refs_10_.refs_13_.refs_1_.refs_2_.refs_3_.refs_4_.refs_5_.refs_7_.refs_8_.refs, ...), channel_id=1, source_target_pairs={{0,12},{1,13},{2,14},{3,15},{4,0},{5,1},{6,2},{7,3},{8,4},{9,5},{1... | collective-permute-start | bytes 1769480 | tf_op jit(solution)/shard_map/ppermute | solution.py:30
  21.8 33.5 %collective-permute-start.22 = (bf16[448,1024]{1,0:T(8,128)(2,1)S(1)}, bf16[448,1024]{1,0:T(8,128)(2,1)S(1)}, u32[]{:S(2)}, u32[]{:S(2)}) collective-permute-start(bf16[448,1024]{1,0:T(8,128)(2,1)S(1)} %dynamic-slice_bitcast_fusion.1), channel_id=1, source_target_pairs={{0,1},{1,0},{2,3},{3,2},{4,5},{5,4},{6,7},{7,6},{8,9},{9,8},{10,11... | collective-permute-start | bytes 2752520 | tf_op jit(solution)/shard_map/ppermute | solution.py:30
  22.7 16.0 %collective-permute-start.42 = (bf16[288,1024]{1,0:T(8,128)(2,1)S(1)}, bf16[288,1024]{1,0:T(8,128)(2,1)S(1)}, u32[]{:S(2)}, u32[]{:S(2)}) collective-permute-start(bf16[288,1024]{1,0:T(8,128)(2,1)S(1)} %copy-done), channel_id=1, source_target_pairs={{0,4},{1,5},{2,6},{3,7},{4,8},{5,9},{6,10},{7,11},{8,12},{9,13},{1... | collective-permute-start | bytes 1769480 | tf_op jit(solution)/shard_map/ppermute | solution.py:30
  34.3 43.9 %collective-permute-start.14 = (bf16[576,1024]{1,0:T(8,128)(2,1)S(1)}, bf16[576,1024]{1,0:T(8,128)(2,1)S(1)}, u32[]{:S(2)}, u32[]{:S(2)}) collective-permute-start(bf16[576,1024]{1,0:T(8,128)(2,1)S(1)} %dynamic-slice_bitcast_fusion), channel_id=1, source_target_pairs={{0,1},{1,0},{2,3},{3,2},{4,5},{5,4},{6,7},{7,6},{8,9},{9,8},{10,11... | collective-permute-start | bytes 3538952 | tf_op jit(solution)/shard_map/ppermute | solution.py:30
  35.8 21.5 %collective-permute-start.3 = (bf16[288,1024]{1,0:T(8,128)(2,1)S(1)}, bf16[288,1024]{1,0:T(8,128)(2,1)S(1)}, u32[]{:S(2)}, u32[]{:S(2)}) collective-permute-start(bf16[288,1024]{1,0:T(8,128)(2,1)S(1)} %collective-permute-done.1.refs_1_), channel_id=1, source_target_pairs={{0,3},{1,2},{2,1},{3,0},{4,7},{5,6},{6,5},{7,4},{8,11},{9,10},{10,... | collective-permute-start | bytes 1769480 | tf_op jit(solution)/shard_map/ppermute | solution.py:30
  38.6 21.5 %collective-permute-start.5 = (bf16[288,1024]{1,0:T(8,128)(2,1)S(1)}, bf16[288,1024]{1,0:T(8,128)(2,1)S(1)}, u32[]{:S(2)}, u32[]{:S(2)}) collective-permute-start(bf16[288,1024]{1,0:T(8,128)(2,1)S(1)} %collective-permute-done.1.refs_1_), channel_id=1, source_target_pairs={{0,12},{1,13},{2,14},{3,15},{4,0},{5,1},{6,2},{7,3},{8,4},{9,5},{1... | collective-permute-start | bytes 1769480 | tf_op jit(solution)/shard_map/ppermute | solution.py:30
  38.7 23.0 %collective-permute-start.8 = (bf16[288,1024]{1,0:T(8,128)(2,1)S(1)}, bf16[288,1024]{1,0:T(8,128)(2,1)S(1)}, u32[]{:S(2)}, u32[]{:S(2)}) collective-permute-start(bf16[288,1024]{1,0:T(8,128)(2,1)S(1)} %collective-permute-done.7.refs_11_), channel_id=1, source_target_pairs={{0,4},{1,5},{2,6},{3,7},{4,8},{5,9},{6,10},{7,11},{8,12},{9,13},{1... | collective-permute-start | bytes 1769480 | tf_op jit(solution)/shard_map/ppermute | solution.py:30
  55.4 16.2 %collective-permute-start.12 = (bf16[288,1024]{1,0:T(8,128)(2,1)S(1)}, bf16[288,1024]{1,0:T(8,128)(2,1)S(1)}, u32[]{:S(2)}, u32[]{:S(2)}) collective-permute-start(bf16[288,1024]{1,0:T(8,128)(2,1)S(1)} %collective-permute-done.1.refs_1_), channel_id=1, source_target_pairs={{0,4},{1,5},{2,6},{3,7},{4,8},{5,9},{6,10},{7,11},{8,12},{9,13},{1... | collective-permute-start | bytes 1769480 | tf_op jit(solution)/shard_map/ppermute | solution.py:30
  57.3 21.0 %collective-permute-start.32 = (bf16[288,1024]{1,0:T(8,128)(2,1)}, bf16[288,1024]{1,0:T(8,128)(2,1)S(1)}, u32[]{:S(2)}, u32[]{:S(2)}) collective-permute-start(bf16[288,1024]{1,0:T(8,128)(2,1)} %collective-permute-done.31.refs_1_), channel_id=1, source_target_pairs={{0,3},{1,2},{2,1},{3,0},{4,7},{5,6},{6,5},{7,4},{8,11},{9,10},{10,... | collective-permute-start | bytes 1769480 | tf_op jit(solution)/shard_map/ppermute | solution.py:30
  60.0 21.1 %collective-permute-start.34 = (bf16[288,1024]{1,0:T(8,128)(2,1)}, bf16[288,1024]{1,0:T(8,128)(2,1)S(1)}, u32[]{:S(2)}, u32[]{:S(2)}) collective-permute-start(bf16[288,1024]{1,0:T(8,128)(2,1)} %collective-permute-done.31.refs_1_), channel_id=1, source_target_pairs={{0,4},{1,5},{2,6},{3,7},{4,8},{5,9},{6,10},{7,11},{8,12},{9,13},{1... | collective-permute-start | bytes 1769480 | tf_op jit(solution)/shard_map/ppermute | solution.py:30
  61.7 21.5 %collective-permute-start.40 = (bf16[288,1024]{1,0:T(8,128)(2,1)S(1)}, bf16[288,1024]{1,0:T(8,128)(2,1)S(1)}, u32[]{:S(2)}, u32[]{:S(2)}) collective-permute-start(bf16[288,1024]{1,0:T(8,128)(2,1)S(1)} %collective-permute-done.38.refs_4_), channel_id=1, source_target_pairs={{0,12},{1,13},{2,14},{3,15},{4,0},{5,1},{6,2},{7,3},{8,4},{9,5},{1... | collective-permute-start | bytes 1769480 | tf_op jit(solution)/shard_map/ppermute | solution.py:30
  71.6 12.5 %collective-permute-start.9 = (bf16[288,1024]{1,0:T(8,128)(2,1)S(1)}, bf16[288,1024]{1,0:T(8,128)(2,1)S(1)}, u32[]{:S(2)}, u32[]{:S(2)}) collective-permute-start(bf16[288,1024]{1,0:T(8,128)(2,1)S(1)} %collective-permute-done.5.refs_5_), channel_id=1, source_target_pairs={{0,12},{1,13},{2,14},{3,15},{4,0},{5,1},{6,2},{7,3},{8,4},{9,5},{1... | collective-permute-start | bytes 1769480 | tf_op jit(solution)/shard_map/ppermute | solution.py:30
  78.3 20.1 %collective-permute-start.23 = (bf16[448,1024]{1,0:T(8,128)(2,1)S(1)}, bf16[448,1024]{1,0:T(8,128)(2,1)S(1)}, u32[]{:S(2)}, u32[]{:S(2)}) collective-permute-start(bf16[448,1024]{1,0:T(8,128)(2,1)S(1)} %collective-permute-done.22.refs_23_), channel_id=1, source_target_pairs={{0,16},{16,0},{32,48},{48,32},{64,80},{80,64},{96,112},{112,96},{1... | collective-permute-start | bytes 2752520 | tf_op jit(solution)/shard_map/ppermute | solution.py:30
  78.3 16.9 %collective-permute-start.10 = (bf16[288,1024]{1,0:T(8,128)(2,1)S(1)}, bf16[288,1024]{1,0:T(8,128)(2,1)S(1)}, u32[]{:S(2)}, u32[]{:S(2)}) collective-permute-start(bf16[288,1024]{1,0:T(8,128)(2,1)S(1)} %collective-permute-done.8.refs_7_), channel_id=1, source_target_pairs={{0,3},{1,2},{2,1},{3,0},{4,7},{5,6},{6,5},{7,4},{8,11},{9,10},{10,... | collective-permute-start | bytes 1769480 | tf_op jit(solution)/shard_map/ppermute | solution.py:30
  81.1 15.7 %collective-permute-start.35 = (bf16[288,1024]{1,0:T(8,128)(2,1)S(1)}, bf16[288,1024]{1,0:T(8,128)(2,1)S(1)}, u32[]{:S(2)}, u32[]{:S(2)}) collective-permute-start(bf16[288,1024]{1,0:T(8,128)(2,1)S(1)} %collective-permute-done.34.refs_12_), channel_id=1, source_target_pairs={{0,4},{1,5},{2,6},{3,7},{4,8},{5,9},{6,10},{7,11},{8,12},{9,13},{1... | collective-permute-start | bytes 1769480 | tf_op jit(solution)/shard_map/ppermute | solution.py:30
  83.2 38.3 %collective-permute-start.6 = (bf16[576,1024]{1,0:T(8,128)(2,1)S(1)}, bf16[576,1024]{1,0:T(8,128)(2,1)S(1)}, u32[]{:S(2)}, u32[]{:S(2)}) collective-permute-start(bf16[576,1024]{1,0:T(8,128)(2,1)S(1)} %constant_dynamic-update-slice_fusion), channel_id=1, source_target_pairs={{0,12},{1,13},{2,14},{3,15},{4,0},{5,1},{6,2},{7,3},{8,4},{9,5},{1... | collective-permute-start | bytes 3538952 | tf_op jit(solution)/shard_map/ppermute | solution.py:30
  84.1 21.9 %collective-permute-start.24 = (bf16[448,1024]{1,0:T(8,128)(2,1)S(1)}, bf16[448,1024]{1,0:T(8,128)(2,1)S(1)}, u32[]{:S(2)}, u32[]{:S(2)}) collective-permute-start(bf16[448,1024]{1,0:T(8,128)(2,1)S(1)} %collective-permute-done.22.refs_23_), channel_id=1, source_target_pairs={{0,96},{16,112},{32,0},{48,16},{64,32},{80,48},{96,64},{112,80},{1... | collective-permute-start | bytes 2752520 | tf_op jit(solution)/shard_map/ppermute | solution.py:30
  95.2 24.4 %collective-permute-start.28 = (bf16[448,1024]{1,0:T(8,128)(2,1)S(1)}, bf16[448,1024]{1,0:T(8,128)(2,1)S(1)}, u32[]{:S(2)}, u32[]{:S(2)}) collective-permute-start(bf16[448,1024]{1,0:T(8,128)(2,1)S(1)} %collective-permute-done.22.refs_23_), channel_id=1, source_target_pairs={{0,32},{16,48},{32,64},{48,80},{64,96},{80,112},{96,0},{112,16},{1... | collective-permute-start | bytes 2752520 | tf_op jit(solution)/shard_map/ppermute | solution.py:30
  96.8 46.8 %collective-permute-start.18 = (bf16[576,1024]{1,0:T(8,128)(2,1)S(1)}, bf16[576,1024]{1,0:T(8,128)(2,1)S(1)}, u32[]{:S(2)}, u32[]{:S(2)}) collective-permute-start(bf16[576,1024]{1,0:T(8,128)(2,1)S(1)} %collective-permute-done.14.refs_15_), channel_id=1, source_target_pairs={{0,32},{16,48},{32,64},{48,80},{64,96},{80,112},{96,0},{112,16},{1... | collective-permute-start | bytes 3538952 | tf_op jit(solution)/shard_map/ppermute | solution.py:30
  98.4 45.5 %collective-permute-start.13 = (bf16[576,1024]{1,0:T(8,128)(2,1)S(1)}, bf16[576,1024]{1,0:T(8,128)(2,1)S(1)}, u32[]{:S(2)}, u32[]{:S(2)}) collective-permute-start(bf16[576,1024]{1,0:T(8,128)(2,1)S(1)} %constant_dynamic-update-slice_fusion), channel_id=1, source_target_pairs={{0,4},{1,5},{2,6},{3,7},{4,8},{5,9},{6,10},{7,11},{8,12},{9,13},{1... | collective-permute-start | bytes 3538952 | tf_op jit(solution)/shard_map/ppermute | solution.py:30
  106.0 38.0 %collective-permute-start.11 = (bf16[288,1024]{1,0:T(8,128)(2,1)S(1)}, bf16[288,1024]{1,0:T(8,128)(2,1)S(1)}, u32[]{:S(2)}, u32[]{:S(2)}) collective-permute-start(bf16[288,1024]{1,0:T(8,128)(2,1)S(1)} %collective-permute-done.9.refs_8_), channel_id=1, source_target_pairs={{0,3},{1,2},{2,1},{3,0},{4,7},{5,6},{6,5},{7,4},{8,11},{9,10},{10,... | collective-permute-start | bytes 1769480 | tf_op jit(solution)/shard_map/ppermute | solution.py:30
  119.7 27.5 %collective-permute-start.16 = (bf16[576,1024]{1,0:T(8,128)(2,1)S(1)}, bf16[576,1024]{1,0:T(8,128)(2,1)S(1)}, u32[]{:S(2)}, u32[]{:S(2)}) collective-permute-start(bf16[576,1024]{1,0:T(8,128)(2,1)S(1)} %collective-permute-done.14.refs_15_), channel_id=1, source_target_pairs={{0,96},{16,112},{32,0},{48,16},{64,32},{80,48},{96,64},{112,80},{1... | collective-permute-start | bytes 3538952 | tf_op jit(solution)/shard_map/ppermute | solution.py:30
  121.5 25.7 %collective-permute-start.15 = (bf16[576,1024]{1,0:T(8,128)(2,1)S(1)}, bf16[576,1024]{1,0:T(8,128)(2,1)S(1)}, u32[]{:S(2)}, u32[]{:S(2)}) collective-permute-start(bf16[576,1024]{1,0:T(8,128)(2,1)S(1)} %collective-permute-done.14.refs_15_), channel_id=1, source_target_pairs={{0,16},{16,0},{32,48},{48,32},{64,80},{80,64},{96,112},{112,96},{1... | collective-permute-start | bytes 3538952 | tf_op jit(solution)/shard_map/ppermute | solution.py:30
  143.6 27.9 %collective-permute-start.19 = (bf16[576,1024]{1,0:T(8,128)(2,1)S(1)}, bf16[576,1024]{1,0:T(8,128)(2,1)S(1)}, u32[]{:S(2)}, u32[]{:S(2)}) collective-permute-start(bf16[576,1024]{1,0:T(8,128)(2,1)S(1)} %collective-permute-done.18.refs_21_), channel_id=1, source_target_pairs={{0,32},{16,48},{32,64},{48,80},{64,96},{80,112},{96,0},{112,16},{1... | collective-permute-start | bytes 3538952 | tf_op jit(solution)/shard_map/ppermute | solution.py:30
  144.0 23.2 %collective-permute-start.26 = (bf16[448,1024]{1,0:T(8,128)(2,1)S(1)}, bf16[448,1024]{1,0:T(8,128)(2,1)S(1)}, u32[]{:S(2)}, u32[]{:S(2)}) collective-permute-start(bf16[448,1024]{1,0:T(8,128)(2,1)S(1)} %collective-permute-done.24.refs_25_), channel_id=1, source_target_pairs={{0,96},{16,112},{32,0},{48,16},{64,32},{80,48},{96,64},{112,80},{1... | collective-permute-start | bytes 2752520 | tf_op jit(solution)/shard_map/ppermute | solution.py:30
  147.1 26.6 %collective-permute-start.17 = (bf16[576,1024]{1,0:T(8,128)(2,1)S(1)}, bf16[576,1024]{1,0:T(8,128)(2,1)S(1)}, u32[]{:S(2)}, u32[]{:S(2)}) collective-permute-start(bf16[576,1024]{1,0:T(8,128)(2,1)S(1)} %collective-permute-done.16.refs_17_), channel_id=1, source_target_pairs={{0,16},{16,0},{32,48},{48,32},{64,80},{80,64},{96,112},{112,96},{1... | collective-permute-start | bytes 3538952 | tf_op jit(solution)/shard_map/ppermute | solution.py:30
  147.3 30.4 %collective-permute-start.21 = (bf16[576,1024]{1,0:T(8,128)(2,1)S(1)}, bf16[576,1024]{1,0:T(8,128)(2,1)S(1)}, u32[]{:S(2)}, u32[]{:S(2)}) collective-permute-start(bf16[576,1024]{1,0:T(8,128)(2,1)S(1)} %collective-permute-done.18.refs_21_), channel_id=1, source_target_pairs={{0,16},{16,0},{32,48},{48,32},{64,80},{80,64},{96,112},{112,96},{1... | collective-permute-start | bytes 3538952 | tf_op jit(solution)/shard_map/ppermute | solution.py:30
  147.7 25.7 %collective-permute-start.29 = (bf16[448,1024]{1,0:T(8,128)(2,1)S(1)}, bf16[448,1024]{1,0:T(8,128)(2,1)S(1)}, u32[]{:S(2)}, u32[]{:S(2)}) collective-permute-start(bf16[448,1024]{1,0:T(8,128)(2,1)S(1)} %collective-permute-done.28.refs_29_), channel_id=1, source_target_pairs={{0,16},{16,0},{32,48},{48,32},{64,80},{80,64},{96,112},{112,96},{1... | collective-permute-start | bytes 2752520 | tf_op jit(solution)/shard_map/ppermute | solution.py:30
  171.5 11.1 %collective-permute-start.20 = (bf16[576,1024]{1,0:T(8,128)(2,1)S(1)}, bf16[576,1024]{1,0:T(8,128)(2,1)S(1)}, u32[]{:S(2)}, u32[]{:S(2)}) collective-permute-start(bf16[576,1024]{1,0:T(8,128)(2,1)S(1)} %collective-permute-done.19.refs_19_), channel_id=1, source_target_pairs={{0,16},{16,0},{32,48},{48,32},{64,80},{80,64},{96,112},{112,96},{1... | collective-permute-start | bytes 3538952 | tf_op jit(solution)/shard_map/ppermute | solution.py:30
  173.4 35.1 %collective-permute-start.39 = (bf16[288,1024]{1,0:T(8,128)(2,1)}, bf16[288,1024]{1,0:T(8,128)(2,1)S(1)}, u32[]{:S(2)}, u32[]{:S(2)}) collective-permute-start(bf16[288,1024]{1,0:T(8,128)(2,1)} %collective-permute-done.31.refs_1_), channel_id=1, source_target_pairs={{0,12},{1,13},{2,14},{3,15},{4,0},{5,1},{6,2},{7,3},{8,4},{9,5},{1... | collective-permute-start | bytes 1769480 | tf_op jit(solution)/shard_map/ppermute | solution.py:30
  173.8 51.0 %collective-permute-start.33 = (bf16[576,1024]{1,0:T(8,128)(2,1)}, bf16[576,1024]{1,0:T(8,128)(2,1)}, u32[]{:S(2)}, u32[]{:S(2)}) collective-permute-start(bf16[576,1024]{1,0:T(8,128)(2,1)} %constant_dynamic-update-slice_fusion.2), channel_id=1, source_target_pairs={{0,12},{1,13},{2,14},{3,15},{4,0},{5,1},{6,2},{7,3},{8,4},{9,5},{1... | collective-permute-start | bytes 3538952 | tf_op jit(solution)/shard_map/ppermute | solution.py:30
  177.7 47.2 %collective-permute-start.37 = (bf16[576,1024]{1,0:T(8,128)(2,1)}, bf16[576,1024]{1,0:T(8,128)(2,1)}, u32[]{:S(2)}, u32[]{:S(2)}) collective-permute-start(bf16[576,1024]{1,0:T(8,128)(2,1)} %constant_dynamic-update-slice_fusion.2), channel_id=1, source_target_pairs={{0,4},{1,5},{2,6},{3,7},{4,8},{5,9},{6,10},{7,11},{8,12},{9,13},{1... | collective-permute-start | bytes 3538952 | tf_op jit(solution)/shard_map/ppermute | solution.py:30
  177.7 30.9 %collective-permute-start.41 = (bf16[288,1024]{1,0:T(8,128)(2,1)S(1)}, bf16[288,1024]{1,0:T(8,128)(2,1)S(1)}, u32[]{:S(2)}, u32[]{:S(2)}) collective-permute-start(bf16[288,1024]{1,0:T(8,128)(2,1)S(1)} %collective-permute-done.40.refs_7_), channel_id=1, source_target_pairs={{0,3},{1,2},{2,1},{3,0},{4,7},{5,6},{6,5},{7,4},{8,11},{9,10},{10,... | collective-permute-start | bytes 1769480 | tf_op jit(solution)/shard_map/ppermute | solution.py:30
  182.6 42.2 %collective-permute-start.36 = (bf16[288,1024]{1,0:T(8,128)(2,1)S(1)}, bf16[288,1024]{1,0:T(8,128)(2,1)S(1)}, u32[]{:S(2)}, u32[]{:S(2)}) collective-permute-start(bf16[288,1024]{1,0:T(8,128)(2,1)S(1)} %collective-permute-done.35.refs_8_), channel_id=1, source_target_pairs={{0,3},{1,2},{2,1},{3,0},{4,7},{5,6},{6,5},{7,4},{8,11},{9,10},{10,... | collective-permute-start | bytes 1769480 | tf_op jit(solution)/shard_map/ppermute | solution.py:30
  208.5 31.8 %collective-permute-start.43 = (bf16[2,144,1024]{2,1,0:T(8,128)(2,1)S(1)}, bf16[2,144,1024]{2,1,0:T(8,128)(2,1)S(1)}, u32[]{:S(2)}, u32[]{:S(2)}) collective-permute-start(bf16[2,144,1024]{2,1,0:T(8,128)(2,1)S(1)} %get-tuple-element.22), channel_id=1, source_target_pairs={{0,48},{1,33},{2,34},{3,51},{4,52},{5,37},{6,38},{7,55},{8,56},{9,... | collective-permute-start | bytes 1769480 | tf_op jit(solution)/shard_map/ppermute | solution.py:30
  209.5 30.9 %collective-permute-start.44 = (bf16[2,144,1024]{2,1,0:T(8,128)(2,1)S(1)}, bf16[2,144,1024]{2,1,0:T(8,128)(2,1)S(1)}, u32[]{:S(2)}, u32[]{:S(2)}) collective-permute-start(bf16[2,144,1024]{2,1,0:T(8,128)(2,1)S(1)} %get-tuple-element.23), channel_id=1, source_target_pairs={{0,96},{1,113},{2,114},{3,99},{4,100},{5,117},{6,118},{7,103},{8,1... | collective-permute-start | bytes 1769480 | tf_op jit(solution)/shard_map/ppermute | solution.py:30
  234.7 19.5 %collective-permute-start.45 = (bf16[144,1024]{1,0:T(8,128)(2,1)S(1)}, bf16[144,1024]{1,0:T(8,128)(2,1)S(1)}, u32[]{:S(2)}, u32[]{:S(2)}) collective-permute-start(bf16[144,1024]{1,0:T(8,128)(2,1)S(1)} %get-tuple-element.24), channel_id=1, source_target_pairs={{0,64},{1,81},{2,82},{3,67},{4,68},{5,85},{6,86},{7,71},{8,72},{9,... | collective-permute-start | bytes 884744 | tf_op jit(solution)/shard_map/ppermute | solution.py:30
  237.3 14.7 %collective-permute-start.46 = (bf16[2,144,1024]{2,1,0:T(8,128)(2,1)S(1)}, bf16[2,144,1024]{2,1,0:T(8,128)(2,1)S(1)}, u32[]{:S(2)}, u32[]{:S(2)}) collective-permute-start(bf16[2,144,1024]{2,1,0:T(8,128)(2,1)S(1)} %get-tuple-element.25), channel_id=1, source_target_pairs={{0,16},{1,1},{2,2},{3,19},{4,20},{5,5},{6,6},{7,23},{8,24},{9,9},{... | collective-permute-start | bytes 1769480 | tf_op jit(solution)/shard_map/ppermute | solution.py:30
  239.6 12.2 %collective-permute-start.48 = (bf16[144,1024]{1,0:T(8,128)(2,1)S(1)}, bf16[144,1024]{1,0:T(8,128)(2,1)S(1)}, u32[]{:S(2)}, u32[]{:S(2)}) collective-permute-start(bf16[144,1024]{1,0:T(8,128)(2,1)S(1)} %get-tuple-element.26), channel_id=1, source_target_pairs={{0,64},{1,81},{2,82},{3,67},{4,68},{5,85},{6,86},{7,71},{8,72},{9,... | collective-permute-start | bytes 884744 | tf_op jit(solution)/shard_map/ppermute | solution.py:30
  241.3 28.1 %collective-permute-start.47 = (bf16[288,1024]{1,0:T(8,128)(2,1)S(1)}, bf16[288,1024]{1,0:T(8,128)(2,1)S(1)}, u32[]{:S(2)}, u32[]{:S(2)}) collective-permute-start(bf16[288,1024]{1,0:T(8,128)(2,1)S(1)} %pad_maximum_fusion), channel_id=1, source_target_pairs={{0,1},{1,0},{2,3},{3,2},{4,5},{5,4},{6,7},{7,6},{8,9},{9,8},{10,11... | collective-permute-start | bytes 1769480 | tf_op jit(solution)/shard_map/ppermute | solution.py:30
  251.9 12.0 %collective-permute-start.49 = (bf16[144,1024]{1,0:T(8,128)(2,1)S(1)}, bf16[144,1024]{1,0:T(8,128)(2,1)S(1)}, u32[]{:S(2)}, u32[]{:S(2)}) collective-permute-start(bf16[144,1024]{1,0:T(8,128)(2,1)S(1)} %fusion.1), channel_id=1, source_target_pairs={{0,1},{1,0},{2,3},{3,2},{4,5},{5,4},{6,7},{7,6},{8,9},{9,8},{10,11... | collective-permute-start | bytes 884744 | tf_op jit(solution)/shard_map/ppermute | solution.py:30
  252.1 17.3 %collective-permute-start.50 = (bf16[144,1024]{1,0:T(8,128)(2,1)S(1)}, bf16[144,1024]{1,0:T(8,128)(2,1)S(1)}, u32[]{:S(2)}, u32[]{:S(2)}) collective-permute-start(bf16[144,1024]{1,0:T(8,128)(2,1)S(1)} %fusion.4), channel_id=1, source_target_pairs={{0,1},{1,0},{2,3},{3,2},{4,5},{5,4},{6,7},{7,6},{8,9},{9,8},{10,11... | collective-permute-start | bytes 884744 | tf_op jit(solution)/shard_map/ppermute | solution.py:30
  (44 other events, 1078.7 us)

commit v4 on v3

--- a/solution.py
+++ b/solution.py
@@ -172,14 +172,17 @@
     x, z = lax.rem(v, 4), lax.div(v, 4)
     y, c = lax.div(o, 2), lax.rem(o, 2)
     count0, count1 = own_count[0], far[8]
+    if resumed:
+        acc_copy = pltpu.make_async_copy(before, acc, col_sem.at[1])
+        acc_copy.start()
     used = [q for q in range(16) if (masks[0] | masks[1]) >> q & 1]
 
     def note(t, n):
         near = t < CD_MAX
         s = t & (CD_MAX - 1)
         tile = jnp.where(near, own_list[s], far[s])
-        flip = lax.rem(tile, 4) ^ x
-        q = ((lax.div(tile, 4) - z) & 3) * 4 + (flip ^ lax.div(flip, 2))
+        flip = (tile & 3) ^ x
+        q = (((tile >> 2) - z) & 3) * 4 + (flip ^ (flip >> 1))
         mask = jnp.where(near, masks[0], masks[1])
         live = (s < jnp.where(near, count0, count1)) & ((lax.shift_right_logical(mask, q) & 1) == 1)
 
@@ -222,9 +225,12 @@
         pltpu.make_async_copy(arrays[k].at[pl.ds(at * rows, rows), :], held.at[q], piece_sem.at[q]).start()
         here[q] = 0
     if final:
-        col_copy = pltpu.make_async_copy(swap_cols, cols, col_sem)
+        col_copy = pltpu.make_async_copy(swap_cols, cols, col_sem.at[0])
         col_copy.start()
-    acc[...] = before[...] if resumed else jnp.zeros_like(acc)
+    if resumed:
+        acc_copy.wait()
+    else:
+        acc[...] = jnp.zeros_like(acc)
 
     def arrive(q):
         @pl.when(here[q] == 0)
@@ -275,11 +281,11 @@
     if final:
         shapes = [jax.ShapeDtypeStruct((2, rows, K), BF)] + [jax.ShapeDtypeStruct((BLK, K), BF)] * (2 * apart)
         shapes += [jax.ShapeDtypeStruct((2, BLK, K), BF)] * (blocks - apart)
-        scratch = [pltpu.VMEM((2, rows, K), F32), pltpu.VMEM((K, K), BF), pltpu.SemaphoreType.DMA]
+        scratch = [pltpu.VMEM((2, rows, K), F32), pltpu.VMEM((K, K), BF), pltpu.SemaphoreType.DMA((2,))]
     else:
         shapes, scratch = [sums], []
     extra = ([] if before is None else [before]) + list(swaps)
-    extra_specs = ([] if before is None else [vmem]) + ([any_spec(), vmem] if final else [])
+    extra_specs = ([] if before is None else [any_spec()]) + ([any_spec(), vmem] if final else [])
     outs = pl.pallas_call(
         functools.partial(ladder_kernel, blocks, masks, before is not None, final, apart),
         grid_spec=pltpu.PrefetchScalarGridSpec(

time: 277 us -> 275 us (level)
  no operation moved by 1% of the time
where the time goes in v4:
time: 275 us; the launch traced here: 272 us
  waiting for transfers between devices  149 us (54%)
  starting transfers between devices  57.6 us (21%)
  Pallas kernels  52.5 us (19%)
  local copies, waits for them, and re-layouts  9.7 us (4%)
    ppermute x51, waiting for transfers between devices, permute(): return lax.ppermute(value, axis, pairs)  149 us
    ppermute x51, starting transfers between devices, permute(): return lax.ppermute(value, axis, pairs)  57.6 us
    pallas_call x4, Pallas kernels, ladder_chunk(): pl.pallas_call(functools.partial(ladder_kernel, blocks, masks, before is...  45.2 us
    unnamed x84, local copies, waits for them, and re-layouts  6.21 us
  transfers between devices with their start and end apart: 51, of which 17 were waited for; matrix products, arithmetic and copies ran while one was open for 3% of the time, Pallas kernels for 17%

profile of v4, /device:TPU:38, one launch (start us, length us, event | category | flops | bytes accessed | tf_op | source)
XLA Modules:
  0.0 272.3 jit_solution(9945148074712199678)
XLA Ops:
  0.0 3.4 %split_rows.1 = (bf16[288,1024]{1,0:T(8,128)(2,1)}, bf16[288,1024]{1,0:T(8,128)(2,1)}, bf16[288,1024]{1,0:T(8,128)(2,1)}, bf16[288,1024]{1,0:T(8,128)(2,1)}) custom-call(bf16[1152,1024]{1,0:T(8,128)(2,1)} %a_ref.1), custom_call_target="tpu_custom_call" | custom-call | tf_op jit(solution)/shard_map/split_rows/pallas_call | solution.py:95
  4.3 1.1 collective-permute-start.2
  5.5 1.9 collective-permute-start.7
  8.3 10.5 %collective-permute-done.far = s32[16]{0:T(128)S(1)} collective-permute-done((s32[16]{0:T(128)S(1)}, s32[16]{0:T(128)S(1)}, u32[]{:S(2)}, u32[]{:S(2)}) %collective-permute-start) | collective-permute-done | bytes 96 | tf_op jit(solution)/shard_map/ppermute | solution.py:30
  20.6 1.2 dynamic-slice_bitcast_fusion.1
  22.7 2.1 collective-permute-start.42
  24.7 1.4 dynamic-slice_bitcast_fusion
  26.1 8.3 %collective-permute-done.30.refs_2_ = bf16[288,1024]{1,0:T(8,128)(2,1)S(1)} collective-permute-done((bf16[288,1024]{1,0:T(8,128)(2,1)}, bf16[288,1024]{1,0:T(8,128)(2,1)S(1)}, u32[]{:S(2)}, u32[]{:S(2)}) %collective-permute-start.30) | collective-permute-done | bytes 589856 | tf_op jit(solution)/shard_map/ppermute | solution.py:30
  34.4 1.4 collective-permute-done.31.refs_1_
  35.8 2.8 %collective-permute-start.3 = (bf16[288,1024]{1,0:T(8,128)(2,1)S(1)}, bf16[288,1024]{1,0:T(8,128)(2,1)S(1)}, u32[]{:S(2)}, u32[]{:S(2)}) collective-permute-start(bf16[288,1024]{1,0:T(8,128)(2,1)S(1)} %collective-permute-done.1.refs_1_), channel_id=1, source_target_pairs={{0,3},{1,2},{2,1},{3,0},{4,7},{5,6},{6,5},{7,4},{8,11},{9,10},{10,... | collective-permute-start | bytes 1769480 | tf_op jit(solution)/shard_map/ppermute | solution.py:30
  38.7 1.9 collective-permute-start.8
  40.6 14.8 %collective-permute-done.22.refs_23_ = bf16[448,1024]{1,0:T(8,128)(2,1)S(1)} collective-permute-done((bf16[448,1024]{1,0:T(8,128)(2,1)S(1)}, bf16[448,1024]{1,0:T(8,128)(2,1)S(1)}, u32[]{:S(2)}, u32[]{:S(2)}) %collective-permute-start.22) | collective-permute-done | bytes 917536 | tf_op jit(solution)/shard_map/ppermute | solution.py:30
  55.4 1.9 collective-permute-start.12
  57.3 2.8 %collective-permute-start.32 = (bf16[288,1024]{1,0:T(8,128)(2,1)}, bf16[288,1024]{1,0:T(8,128)(2,1)S(1)}, u32[]{:S(2)}, u32[]{:S(2)}) collective-permute-start(bf16[288,1024]{1,0:T(8,128)(2,1)} %collective-permute-done.31.refs_1_), channel_id=1, source_target_pairs={{0,3},{1,2},{2,1},{3,0},{4,7},{5,6},{6,5},{7,4},{8,11},{9,10},{10,... | collective-permute-start | bytes 1769480 | tf_op jit(solution)/shard_map/ppermute | solution.py:30
  60.0 1.6 collective-permute-start.34
  62.1 9.5 %collective-permute-done.12.refs_12_ = bf16[288,1024]{1,0:T(8,128)(2,1)S(1)} collective-permute-done((bf16[288,1024]{1,0:T(8,128)(2,1)S(1)}, bf16[288,1024]{1,0:T(8,128)(2,1)S(1)}, u32[]{:S(2)}, u32[]{:S(2)}) %collective-permute-start.12) | collective-permute-done | bytes 589856 | tf_op jit(solution)/shard_map/ppermute | solution.py:30
  71.6 2.1 collective-permute-start.9
  73.7 4.6 %collective-permute-done.14.refs_15_ = bf16[576,1024]{1,0:T(8,128)(2,1)S(1)} collective-permute-done((bf16[576,1024]{1,0:T(8,128)(2,1)S(1)}, bf16[576,1024]{1,0:T(8,128)(2,1)S(1)}, u32[]{:S(2)}, u32[]{:S(2)}) %collective-permute-start.14) | collective-permute-done | bytes 1179680 | tf_op jit(solution)/shard_map/ppermute | solution.py:30
  78.3 2.8 %collective-permute-start.10 = (bf16[288,1024]{1,0:T(8,128)(2,1)S(1)}, bf16[288,1024]{1,0:T(8,128)(2,1)S(1)}, u32[]{:S(2)}, u32[]{:S(2)}) collective-permute-start(bf16[288,1024]{1,0:T(8,128)(2,1)S(1)} %collective-permute-done.8.refs_7_), channel_id=1, source_target_pairs={{0,3},{1,2},{2,1},{3,0},{4,7},{5,6},{6,5},{7,4},{8,11},{9,10},{10,... | collective-permute-start | bytes 1769480 | tf_op jit(solution)/shard_map/ppermute | solution.py:30
  81.1 1.9 collective-permute-start.35
  84.1 3.0 %collective-permute-start.24 = (bf16[448,1024]{1,0:T(8,128)(2,1)S(1)}, bf16[448,1024]{1,0:T(8,128)(2,1)S(1)}, u32[]{:S(2)}, u32[]{:S(2)}) collective-permute-start(bf16[448,1024]{1,0:T(8,128)(2,1)S(1)} %collective-permute-done.22.refs_23_), channel_id=1, source_target_pairs={{0,96},{16,112},{32,0},{48,16},{64,32},{80,48},{96,64},{112,80},{1... | collective-permute-start | bytes 2752520 | tf_op jit(solution)/shard_map/ppermute | solution.py:30
  87.1 8.1 %collective-permute-done.10.refs_9_ = bf16[288,1024]{1,0:T(8,128)(2,1)S(1)} collective-permute-done((bf16[288,1024]{1,0:T(8,128)(2,1)S(1)}, bf16[288,1024]{1,0:T(8,128)(2,1)S(1)}, u32[]{:S(2)}, u32[]{:S(2)}) %collective-permute-start.10) | collective-permute-done | bytes 589856 | tf_op jit(solution)/shard_map/ppermute | solution.py:30
  95.2 1.6 collective-permute-start.28
  96.8 1.6 collective-permute-start.18
  98.4 1.9 collective-permute-start.13
  100.3 5.6 %collective-permute-done.24.refs_25_ = bf16[448,1024]{1,0:T(8,128)(2,1)S(1)} collective-permute-done((bf16[448,1024]{1,0:T(8,128)(2,1)S(1)}, bf16[448,1024]{1,0:T(8,128)(2,1)S(1)}, u32[]{:S(2)}, u32[]{:S(2)}) %collective-permute-start.24) | collective-permute-done | bytes 917536 | tf_op jit(solution)/shard_map/ppermute | solution.py:30
  106.5 13.2 %collective-permute-done.28.refs_29_ = bf16[448,1024]{1,0:T(8,128)(2,1)S(1)} collective-permute-done((bf16[448,1024]{1,0:T(8,128)(2,1)S(1)}, bf16[448,1024]{1,0:T(8,128)(2,1)S(1)}, u32[]{:S(2)}, u32[]{:S(2)}) %collective-permute-start.28) | collective-permute-done | bytes 917536 | tf_op jit(solution)/shard_map/ppermute | solution.py:30
  119.7 1.8 collective-permute-start.16
  121.6 22.0 %collective-permute-done.18.refs_21_ = bf16[576,1024]{1,0:T(8,128)(2,1)S(1)} collective-permute-done((bf16[576,1024]{1,0:T(8,128)(2,1)S(1)}, bf16[576,1024]{1,0:T(8,128)(2,1)S(1)}, u32[]{:S(2)}, u32[]{:S(2)}) %collective-permute-start.18) | collective-permute-done | bytes 1179680 | tf_op jit(solution)/shard_map/ppermute | solution.py:30
  144.0 3.2 %collective-permute-start.26 = (bf16[448,1024]{1,0:T(8,128)(2,1)S(1)}, bf16[448,1024]{1,0:T(8,128)(2,1)S(1)}, u32[]{:S(2)}, u32[]{:S(2)}) collective-permute-start(bf16[448,1024]{1,0:T(8,128)(2,1)S(1)} %collective-permute-done.24.refs_25_), channel_id=1, source_target_pairs={{0,96},{16,112},{32,0},{48,16},{64,32},{80,48},{96,64},{112,80},{1... | collective-permute-start | bytes 2752520 | tf_op jit(solution)/shard_map/ppermute | solution.py:30
  147.9 19.3 %collective-permute-done.26.refs_27_ = bf16[448,1024]{1,0:T(8,128)(2,1)S(1)} collective-permute-done((bf16[448,1024]{1,0:T(8,128)(2,1)S(1)}, bf16[448,1024]{1,0:T(8,128)(2,1)S(1)}, u32[]{:S(2)}, u32[]{:S(2)}) %collective-permute-start.26) | collective-permute-done | bytes 917536 | tf_op jit(solution)/shard_map/ppermute | solution.py:30
  167.2 4.3 %collective-permute-done.19.refs_19_ = bf16[576,1024]{1,0:T(8,128)(2,1)S(1)} collective-permute-done((bf16[576,1024]{1,0:T(8,128)(2,1)S(1)}, bf16[576,1024]{1,0:T(8,128)(2,1)S(1)}, u32[]{:S(2)}, u32[]{:S(2)}) %collective-permute-start.19) | collective-permute-done | bytes 1179680 | tf_op jit(solution)/shard_map/ppermute | solution.py:30
  171.5 1.0 constant_dynamic-update-slice_fusion.3
  173.8 3.8 %collective-permute-start.33 = (bf16[576,1024]{1,0:T(8,128)(2,1)}, bf16[576,1024]{1,0:T(8,128)(2,1)}, u32[]{:S(2)}, u32[]{:S(2)}) collective-permute-start(bf16[576,1024]{1,0:T(8,128)(2,1)} %constant_dynamic-update-slice_fusion.2), channel_id=1, source_target_pairs={{0,12},{1,13},{2,14},{3,15},{4,0},{5,1},{6,2},{7,3},{8,4},{9,5},{1... | collective-permute-start | bytes 3538952 | tf_op jit(solution)/shard_map/ppermute | solution.py:30
  177.7 2.8 %collective-permute-start.41 = (bf16[288,1024]{1,0:T(8,128)(2,1)S(1)}, bf16[288,1024]{1,0:T(8,128)(2,1)S(1)}, u32[]{:S(2)}, u32[]{:S(2)}) collective-permute-start(bf16[288,1024]{1,0:T(8,128)(2,1)S(1)} %collective-permute-done.40.refs_7_), channel_id=1, source_target_pairs={{0,3},{1,2},{2,1},{3,0},{4,7},{5,6},{6,5},{7,4},{8,11},{9,10},{10,... | collective-permute-start | bytes 1769480 | tf_op jit(solution)/shard_map/ppermute | solution.py:30
  180.6 2.0 fusion.refs_32_
  183.7 8.4 %shard_map.46.refs_31_ = f32[2,288,1024]{2,1,0:T(8,128)} custom-call(s32[8]{0:T(128)S(1)} %bitcast.17, s32[1]{0:T(128)S(6)} %copy.7.own_count, s32[16]{0:T(128)S(1)} %collective-permute-done.far, bf16[288,1024]{1,0:T(8,128)(2,1)S(1)} %copy-done.1, bf16[288,1024]{1,0:T(8,128)(2,1)S(1)} %collective-permute-done.1.refs_1_, ...), custom_call_target="tpu_custom_call" | custom-call | tf_op jit(solution)/shard_map/pallas_call | solution.py:289
  193.0 14.5 %shard_map.47 = (bf16[2,288,1024]{2,1,0:T(8,128)(2,1)}, bf16[2,144,1024]{2,1,0:T(8,128)(2,1)S(1)}, bf16[2,144,1024]{2,1,0:T(8,128)(2,1)S(1)}) custom-call(s32[8]{0:T(128)S(1)} %bitcast.18, s32[1]{0:T(128)S(6)} %copy.7.own_count, s32[16]{0:T(128)S(1)} %collective-permute-done.far, bf16[288,1024]{1,0:T(8,128)(2,1)S(1)} %copy-done.1, ...), custom_call_target="tpu_custom_call" | custom-call | tf_op jit(solution)/shard_map/pallas_call | solution.py:289
  209.0 1.3 copy-done.13
  210.3 13.4 %shard_map.48.refs_31_ = f32[2,288,1024]{2,1,0:T(8,128)} custom-call(s32[8]{0:T(128)S(1)} %bitcast.19, s32[1]{0:T(128)S(6)} %copy.7.own_count, s32[16]{0:T(128)S(1)} %collective-permute-done.far, bf16[288,1024]{1,0:T(8,128)(2,1)S(1)} %copy-done, bf16[288,1024]{1,0:T(8,128)(2,1)} %collective-permute-done.31.refs_1_, ...), custom_call_target="tpu_custom_call" | custom-call | tf_op jit(solution)/shard_map/pallas_call | solution.py:289
  223.8 8.9 %shard_map.49 = (bf16[2,288,1024]{2,1,0:T(8,128)(2,1)}, bf16[144,1024]{1,0:T(8,128)(2,1)S(1)}, bf16[144,1024]{1,0:T(8,128)(2,1)S(1)}, bf16[2,144,1024]{2,1,0:T(8,128)(2,1)S(1)}) custom-call(s32[8]{0:T(128)S(1)} %bitcast.20, s32[1]{0:T(128)S(6)} %copy.7.own_count, s32[16]{0:T(128)S(1)} %collective-permute-done.far, bf16[288,1024]{1,0:T(8,128)(2,1)S(1)} %copy-done, ...), custom_call_target="tpu_custom_call" | custom-call | tf_op jit(solution)/shard_map/pallas_call | solution.py:289
  232.7 2.5 collective-permute-start.45
  235.2 2.3 collective-permute-start.46
  239.4 10.5 %collective-permute-done.48 = bf16[144,1024]{1,0:T(8,128)(2,1)S(1)} collective-permute-done((bf16[144,1024]{1,0:T(8,128)(2,1)S(1)}, bf16[144,1024]{1,0:T(8,128)(2,1)S(1)}, u32[]{:S(2)}, u32[]{:S(2)}) %collective-permute-start.48) | collective-permute-done | bytes 294944 | tf_op jit(solution)/shard_map/ppermute | solution.py:30
  250.1 2.1 collective-permute-start.50
  252.2 9.7 %collective-permute-done.49.refs_8_ = bf16[144,1024]{1,0:T(8,128)(2,1)S(1)} collective-permute-done((bf16[144,1024]{1,0:T(8,128)(2,1)S(1)}, bf16[144,1024]{1,0:T(8,128)(2,1)S(1)}, u32[]{:S(2)}, u32[]{:S(2)}) %collective-permute-start.49) | collective-permute-done | bytes 294944 | tf_op jit(solution)/shard_map/ppermute | solution.py:30
  261.9 5.6 %collective-permute-done.50.refs_9_ = bf16[144,1024]{1,0:T(8,128)(2,1)S(1)} collective-permute-done((bf16[144,1024]{1,0:T(8,128)(2,1)S(1)}, bf16[144,1024]{1,0:T(8,128)(2,1)S(1)}, u32[]{:S(2)}, u32[]{:S(2)}) %collective-permute-start.50) | collective-permute-done | bytes 294944 | tf_op jit(solution)/shard_map/ppermute | solution.py:30
  268.4 3.9 %join_rows.1 = bf16[1152,1024]{1,0:T(8,128)(2,1)} custom-call(bf16[2,288,1024]{2,1,0:T(8,128)(2,1)} %get-tuple-element.18.refs_0_, bf16[2,288,1024]{2,1,0:T(8,128)(2,1)} %get-tuple-element.21.refs_1_, bf16[2,144,1024]{2,1,0:T(8,128)(2,1)} %copy-done.32, bf16[2,144,1024]{2,1,0:T(8,128)(2,1)} %copy-done.33, bf16[1,144,1024]{2,1,0:T(8,128)(2,1)} %bitcast.25, ...), custom_call_target="tpu_custom_call" | custom-call | tf_op jit(solution)/shard_map/join_rows/pallas_call | solution.py:132
  (162 shorter events, 14.5 us)
Async XLA Ops:
  3.4 15.9 %collective-permute-start.1 = (bf16[288,1024]{1,0:T(8,128)(2,1)}, bf16[288,1024]{1,0:T(8,128)(2,1)S(1)}, u32[]{:S(2)}, u32[]{:S(2)}) collective-permute-start(bf16[288,1024]{1,0:T(8,128)(2,1)} %get-tuple-element.17), channel_id=1, source_target_pairs={{0,1},{1,0},{2,3},{3,2},{4,5},{5,4},{6,7},{7,6},{8,9},{9,8},{10,11... | collective-permute-start | bytes 1769480 | tf_op jit(solution)/shard_map/ppermute | solution.py:30
  4.3 16.2 %collective-permute-start.2 = (bf16[288,1024]{1,0:T(8,128)(2,1)}, bf16[288,1024]{1,0:T(8,128)(2,1)S(1)}, u32[]{:S(2)}, u32[]{:S(2)}) collective-permute-start(bf16[288,1024]{1,0:T(8,128)(2,1)} %get-tuple-element.16.refs_0_.refs_6_.refs_10_), channel_id=1, source_target_pairs={{0,3},{1,2},{2,1},{3,0},{4,7},{5,6},{6,5},{7,4},{8,11},{9,10},{10,... | collective-permute-start | bytes 1769480 | tf_op jit(solution)/shard_map/ppermute | solution.py:30
  5.4 16.4 %collective-permute-start.4 = (bf16[288,1024]{1,0:T(8,128)(2,1)}, bf16[288,1024]{1,0:T(8,128)(2,1)S(1)}, u32[]{:S(2)}, u32[]{:S(2)}) collective-permute-start(bf16[288,1024]{1,0:T(8,128)(2,1)} %get-tuple-element.16.refs_0_.refs_6_.refs_10_), channel_id=1, source_target_pairs={{0,12},{1,13},{2,14},{3,15},{4,0},{5,1},{6,2},{7,3},{8,4},{9,5},{1... | collective-permute-start | bytes 1769480 | tf_op jit(solution)/shard_map/ppermute | solution.py:30
  5.5 17.1 %collective-permute-start.7 = (bf16[288,1024]{1,0:T(8,128)(2,1)}, bf16[288,1024]{1,0:T(8,128)(2,1)S(1)}, u32[]{:S(2)}, u32[]{:S(2)}) collective-permute-start(bf16[288,1024]{1,0:T(8,128)(2,1)} %get-tuple-element.16.refs_0_.refs_6_.refs_10_), channel_id=1, source_target_pairs={{0,4},{1,5},{2,6},{3,7},{4,8},{5,9},{6,10},{7,11},{8,12},{9,13},{1... | collective-permute-start | bytes 1769480 | tf_op jit(solution)/shard_map/ppermute | solution.py:30
  18.8 15.5 %collective-permute-start.30 = (bf16[288,1024]{1,0:T(8,128)(2,1)}, bf16[288,1024]{1,0:T(8,128)(2,1)S(1)}, u32[]{:S(2)}, u32[]{:S(2)}) collective-permute-start(bf16[288,1024]{1,0:T(8,128)(2,1)} %get-tuple-element.19.refs_0_.refs_6_.refs_10_.refs_13_.refs_1_.refs_2_.refs_3_.refs_4_.refs_5_.refs_7_.refs_8_.refs, ...), channel_id=1, source_target_pairs={{0,3},{1,2},{2,1},{3,0},{4,7},{5,6},{6,5},{7,4},{8,11},{9,10},{10,... | collective-permute-start | bytes 1769480 | tf_op jit(solution)/shard_map/ppermute | solution.py:30
  19.3 16.5 %collective-permute-start.31 = (bf16[288,1024]{1,0:T(8,128)(2,1)}, bf16[288,1024]{1,0:T(8,128)(2,1)}, u32[]{:S(2)}, u32[]{:S(2)}) collective-permute-start(bf16[288,1024]{1,0:T(8,128)(2,1)} %get-tuple-element.20), channel_id=1, source_target_pairs={{0,1},{1,0},{2,3},{3,2},{4,5},{5,4},{6,7},{7,6},{8,9},{9,8},{10,11... | collective-permute-start | bytes 1769480 | tf_op jit(solution)/shard_map/ppermute | solution.py:30
  20.5 18.1 %collective-permute-start.38 = (bf16[288,1024]{1,0:T(8,128)(2,1)}, bf16[288,1024]{1,0:T(8,128)(2,1)S(1)}, u32[]{:S(2)}, u32[]{:S(2)}) collective-permute-start(bf16[288,1024]{1,0:T(8,128)(2,1)} %get-tuple-element.19.refs_0_.refs_6_.refs_10_.refs_13_.refs_1_.refs_2_.refs_3_.refs_4_.refs_5_.refs_7_.refs_8_.refs, ...), channel_id=1, source_target_pairs={{0,12},{1,13},{2,14},{3,15},{4,0},{5,1},{6,2},{7,3},{8,4},{9,5},{1... | collective-permute-start | bytes 1769480 | tf_op jit(solution)/shard_map/ppermute | solution.py:30
  21.8 33.5 %collective-permute-start.22 = (bf16[448,1024]{1,0:T(8,128)(2,1)S(1)}, bf16[448,1024]{1,0:T(8,128)(2,1)S(1)}, u32[]{:S(2)}, u32[]{:S(2)}) collective-permute-start(bf16[448,1024]{1,0:T(8,128)(2,1)S(1)} %dynamic-slice_bitcast_fusion.1), channel_id=1, source_target_pairs={{0,1},{1,0},{2,3},{3,2},{4,5},{5,4},{6,7},{7,6},{8,9},{9,8},{10,11... | collective-permute-start | bytes 2752520 | tf_op jit(solution)/shard_map/ppermute | solution.py:30
  22.7 16.0 %collective-permute-start.42 = (bf16[288,1024]{1,0:T(8,128)(2,1)S(1)}, bf16[288,1024]{1,0:T(8,128)(2,1)S(1)}, u32[]{:S(2)}, u32[]{:S(2)}) collective-permute-start(bf16[288,1024]{1,0:T(8,128)(2,1)S(1)} %copy-done), channel_id=1, source_target_pairs={{0,4},{1,5},{2,6},{3,7},{4,8},{5,9},{6,10},{7,11},{8,12},{9,13},{1... | collective-permute-start | bytes 1769480 | tf_op jit(solution)/shard_map/ppermute | solution.py:30
  34.3 43.9 %collective-permute-start.14 = (bf16[576,1024]{1,0:T(8,128)(2,1)S(1)}, bf16[576,1024]{1,0:T(8,128)(2,1)S(1)}, u32[]{:S(2)}, u32[]{:S(2)}) collective-permute-start(bf16[576,1024]{1,0:T(8,128)(2,1)S(1)} %dynamic-slice_bitcast_fusion), channel_id=1, source_target_pairs={{0,1},{1,0},{2,3},{3,2},{4,5},{5,4},{6,7},{7,6},{8,9},{9,8},{10,11... | collective-permute-start | bytes 3538952 | tf_op jit(solution)/shard_map/ppermute | solution.py:30
  35.8 21.5 %collective-permute-start.3 = (bf16[288,1024]{1,0:T(8,128)(2,1)S(1)}, bf16[288,1024]{1,0:T(8,128)(2,1)S(1)}, u32[]{:S(2)}, u32[]{:S(2)}) collective-permute-start(bf16[288,1024]{1,0:T(8,128)(2,1)S(1)} %collective-permute-done.1.refs_1_), channel_id=1, source_target_pairs={{0,3},{1,2},{2,1},{3,0},{4,7},{5,6},{6,5},{7,4},{8,11},{9,10},{10,... | collective-permute-start | bytes 1769480 | tf_op jit(solution)/shard_map/ppermute | solution.py:30
  38.6 21.5 %collective-permute-start.5 = (bf16[288,1024]{1,0:T(8,128)(2,1)S(1)}, bf16[288,1024]{1,0:T(8,128)(2,1)S(1)}, u32[]{:S(2)}, u32[]{:S(2)}) collective-permute-start(bf16[288,1024]{1,0:T(8,128)(2,1)S(1)} %collective-permute-done.1.refs_1_), channel_id=1, source_target_pairs={{0,12},{1,13},{2,14},{3,15},{4,0},{5,1},{6,2},{7,3},{8,4},{9,5},{1... | collective-permute-start | bytes 1769480 | tf_op jit(solution)/shard_map/ppermute | solution.py:30
  38.7 23.0 %collective-permute-start.8 = (bf16[288,1024]{1,0:T(8,128)(2,1)S(1)}, bf16[288,1024]{1,0:T(8,128)(2,1)S(1)}, u32[]{:S(2)}, u32[]{:S(2)}) collective-permute-start(bf16[288,1024]{1,0:T(8,128)(2,1)S(1)} %collective-permute-done.7.refs_11_), channel_id=1, source_target_pairs={{0,4},{1,5},{2,6},{3,7},{4,8},{5,9},{6,10},{7,11},{8,12},{9,13},{1... | collective-permute-start | bytes 1769480 | tf_op jit(solution)/shard_map/ppermute | solution.py:30
  55.4 16.2 %collective-permute-start.12 = (bf16[288,1024]{1,0:T(8,128)(2,1)S(1)}, bf16[288,1024]{1,0:T(8,128)(2,1)S(1)}, u32[]{:S(2)}, u32[]{:S(2)}) collective-permute-start(bf16[288,1024]{1,0:T(8,128)(2,1)S(1)} %collective-permute-done.1.refs_1_), channel_id=1, source_target_pairs={{0,4},{1,5},{2,6},{3,7},{4,8},{5,9},{6,10},{7,11},{8,12},{9,13},{1... | collective-permute-start | bytes 1769480 | tf_op jit(solution)/shard_map/ppermute | solution.py:30
  57.3 21.0 %collective-permute-start.32 = (bf16[288,1024]{1,0:T(8,128)(2,1)}, bf16[288,1024]{1,0:T(8,128)(2,1)S(1)}, u32[]{:S(2)}, u32[]{:S(2)}) collective-permute-start(bf16[288,1024]{1,0:T(8,128)(2,1)} %collective-permute-done.31.refs_1_), channel_id=1, source_target_pairs={{0,3},{1,2},{2,1},{3,0},{4,7},{5,6},{6,5},{7,4},{8,11},{9,10},{10,... | collective-permute-start | bytes 1769480 | tf_op jit(solution)/shard_map/ppermute | solution.py:30
  60.0 21.1 %collective-permute-start.34 = (bf16[288,1024]{1,0:T(8,128)(2,1)}, bf16[288,1024]{1,0:T(8,128)(2,1)S(1)}, u32[]{:S(2)}, u32[]{:S(2)}) collective-permute-start(bf16[288,1024]{1,0:T(8,128)(2,1)} %collective-permute-done.31.refs_1_), channel_id=1, source_target_pairs={{0,4},{1,5},{2,6},{3,7},{4,8},{5,9},{6,10},{7,11},{8,12},{9,13},{1... | collective-permute-start | bytes 1769480 | tf_op jit(solution)/shard_map/ppermute | solution.py:30
  61.7 21.5 %collective-permute-start.40 = (bf16[288,1024]{1,0:T(8,128)(2,1)S(1)}, bf16[288,1024]{1,0:T(8,128)(2,1)S(1)}, u32[]{:S(2)}, u32[]{:S(2)}) collective-permute-start(bf16[288,1024]{1,0:T(8,128)(2,1)S(1)} %collective-permute-done.38.refs_4_), channel_id=1, source_target_pairs={{0,12},{1,13},{2,14},{3,15},{4,0},{5,1},{6,2},{7,3},{8,4},{9,5},{1... | collective-permute-start | bytes 1769480 | tf_op jit(solution)/shard_map/ppermute | solution.py:30
  71.6 12.5 %collective-permute-start.9 = (bf16[288,1024]{1,0:T(8,128)(2,1)S(1)}, bf16[288,1024]{1,0:T(8,128)(2,1)S(1)}, u32[]{:S(2)}, u32[]{:S(2)}) collective-permute-start(bf16[288,1024]{1,0:T(8,128)(2,1)S(1)} %collective-permute-done.5.refs_5_), channel_id=1, source_target_pairs={{0,12},{1,13},{2,14},{3,15},{4,0},{5,1},{6,2},{7,3},{8,4},{9,5},{1... | collective-permute-start | bytes 1769480 | tf_op jit(solution)/shard_map/ppermute | solution.py:30
  78.3 20.1 %collective-permute-start.23 = (bf16[448,1024]{1,0:T(8,128)(2,1)S(1)}, bf16[448,1024]{1,0:T(8,128)(2,1)S(1)}, u32[]{:S(2)}, u32[]{:S(2)}) collective-permute-start(bf16[448,1024]{1,0:T(8,128)(2,1)S(1)} %collective-permute-done.22.refs_23_), channel_id=1, source_target_pairs={{0,16},{16,0},{32,48},{48,32},{64,80},{80,64},{96,112},{112,96},{1... | collective-permute-start | bytes 2752520 | tf_op jit(solution)/shard_map/ppermute | solution.py:30
  78.3 16.9 %collective-permute-start.10 = (bf16[288,1024]{1,0:T(8,128)(2,1)S(1)}, bf16[288,1024]{1,0:T(8,128)(2,1)S(1)}, u32[]{:S(2)}, u32[]{:S(2)}) collective-permute-start(bf16[288,1024]{1,0:T(8,128)(2,1)S(1)} %collective-permute-done.8.refs_7_), channel_id=1, source_target_pairs={{0,3},{1,2},{2,1},{3,0},{4,7},{5,6},{6,5},{7,4},{8,11},{9,10},{10,... | collective-permute-start | bytes 1769480 | tf_op jit(solution)/shard_map/ppermute | solution.py:30
  81.1 15.7 %collective-permute-start.35 = (bf16[288,1024]{1,0:T(8,128)(2,1)S(1)}, bf16[288,1024]{1,0:T(8,128)(2,1)S(1)}, u32[]{:S(2)}, u32[]{:S(2)}) collective-permute-start(bf16[288,1024]{1,0:T(8,128)(2,1)S(1)} %collective-permute-done.34.refs_12_), channel_id=1, source_target_pairs={{0,4},{1,5},{2,6},{3,7},{4,8},{5,9},{6,10},{7,11},{8,12},{9,13},{1... | collective-permute-start | bytes 1769480 | tf_op jit(solution)/shard_map/ppermute | solution.py:30
  83.2 38.3 %collective-permute-start.6 = (bf16[576,1024]{1,0:T(8,128)(2,1)S(1)}, bf16[576,1024]{1,0:T(8,128)(2,1)S(1)}, u32[]{:S(2)}, u32[]{:S(2)}) collective-permute-start(bf16[576,1024]{1,0:T(8,128)(2,1)S(1)} %constant_dynamic-update-slice_fusion), channel_id=1, source_target_pairs={{0,12},{1,13},{2,14},{3,15},{4,0},{5,1},{6,2},{7,3},{8,4},{9,5},{1... | collective-permute-start | bytes 3538952 | tf_op jit(solution)/shard_map/ppermute | solution.py:30
  84.1 21.9 %collective-permute-start.24 = (bf16[448,1024]{1,0:T(8,128)(2,1)S(1)}, bf16[448,1024]{1,0:T(8,128)(2,1)S(1)}, u32[]{:S(2)}, u32[]{:S(2)}) collective-permute-start(bf16[448,1024]{1,0:T(8,128)(2,1)S(1)} %collective-permute-done.22.refs_23_), channel_id=1, source_target_pairs={{0,96},{16,112},{32,0},{48,16},{64,32},{80,48},{96,64},{112,80},{1... | collective-permute-start | bytes 2752520 | tf_op jit(solution)/shard_map/ppermute | solution.py:30
  95.2 24.4 %collective-permute-start.28 = (bf16[448,1024]{1,0:T(8,128)(2,1)S(1)}, bf16[448,1024]{1,0:T(8,128)(2,1)S(1)}, u32[]{:S(2)}, u32[]{:S(2)}) collective-permute-start(bf16[448,1024]{1,0:T(8,128)(2,1)S(1)} %collective-permute-done.22.refs_23_), channel_id=1, source_target_pairs={{0,32},{16,48},{32,64},{48,80},{64,96},{80,112},{96,0},{112,16},{1... | collective-permute-start | bytes 2752520 | tf_op jit(solution)/shard_map/ppermute | solution.py:30
  96.8 46.8 %collective-permute-start.18 = (bf16[576,1024]{1,0:T(8,128)(2,1)S(1)}, bf16[576,1024]{1,0:T(8,128)(2,1)S(1)}, u32[]{:S(2)}, u32[]{:S(2)}) collective-permute-start(bf16[576,1024]{1,0:T(8,128)(2,1)S(1)} %collective-permute-done.14.refs_15_), channel_id=1, source_target_pairs={{0,32},{16,48},{32,64},{48,80},{64,96},{80,112},{96,0},{112,16},{1... | collective-permute-start | bytes 3538952 | tf_op jit(solution)/shard_map/ppermute | solution.py:30
  98.4 45.5 %collective-permute-start.13 = (bf16[576,1024]{1,0:T(8,128)(2,1)S(1)}, bf16[576,1024]{1,0:T(8,128)(2,1)S(1)}, u32[]{:S(2)}, u32[]{:S(2)}) collective-permute-start(bf16[576,1024]{1,0:T(8,128)(2,1)S(1)} %constant_dynamic-update-slice_fusion), channel_id=1, source_target_pairs={{0,4},{1,5},{2,6},{3,7},{4,8},{5,9},{6,10},{7,11},{8,12},{9,13},{1... | collective-permute-start | bytes 3538952 | tf_op jit(solution)/shard_map/ppermute | solution.py:30
  106.0 38.0 %collective-permute-start.11 = (bf16[288,1024]{1,0:T(8,128)(2,1)S(1)}, bf16[288,1024]{1,0:T(8,128)(2,1)S(1)}, u32[]{:S(2)}, u32[]{:S(2)}) collective-permute-start(bf16[288,1024]{1,0:T(8,128)(2,1)S(1)} %collective-permute-done.9.refs_8_), channel_id=1, source_target_pairs={{0,3},{1,2},{2,1},{3,0},{4,7},{5,6},{6,5},{7,4},{8,11},{9,10},{10,... | collective-permute-start | bytes 1769480 | tf_op jit(solution)/shard_map/ppermute | solution.py:30
  119.7 27.5 %collective-permute-start.16 = (bf16[576,1024]{1,0:T(8,128)(2,1)S(1)}, bf16[576,1024]{1,0:T(8,128)(2,1)S(1)}, u32[]{:S(2)}, u32[]{:S(2)}) collective-permute-start(bf16[576,1024]{1,0:T(8,128)(2,1)S(1)} %collective-permute-done.14.refs_15_), channel_id=1, source_target_pairs={{0,96},{16,112},{32,0},{48,16},{64,32},{80,48},{96,64},{112,80},{1... | collective-permute-start | bytes 3538952 | tf_op jit(solution)/shard_map/ppermute | solution.py:30
  121.5 25.7 %collective-permute-start.15 = (bf16[576,1024]{1,0:T(8,128)(2,1)S(1)}, bf16[576,1024]{1,0:T(8,128)(2,1)S(1)}, u32[]{:S(2)}, u32[]{:S(2)}) collective-permute-start(bf16[576,1024]{1,0:T(8,128)(2,1)S(1)} %collective-permute-done.14.refs_15_), channel_id=1, source_target_pairs={{0,16},{16,0},{32,48},{48,32},{64,80},{80,64},{96,112},{112,96},{1... | collective-permute-start | bytes 3538952 | tf_op jit(solution)/shard_map/ppermute | solution.py:30
  143.6 27.9 %collective-permute-start.19 = (bf16[576,1024]{1,0:T(8,128)(2,1)S(1)}, bf16[576,1024]{1,0:T(8,128)(2,1)S(1)}, u32[]{:S(2)}, u32[]{:S(2)}) collective-permute-start(bf16[576,1024]{1,0:T(8,128)(2,1)S(1)} %collective-permute-done.18.refs_21_), channel_id=1, source_target_pairs={{0,32},{16,48},{32,64},{48,80},{64,96},{80,112},{96,0},{112,16},{1... | collective-permute-start | bytes 3538952 | tf_op jit(solution)/shard_map/ppermute | solution.py:30
  144.0 23.2 %collective-permute-start.26 = (bf16[448,1024]{1,0:T(8,128)(2,1)S(1)}, bf16[448,1024]{1,0:T(8,128)(2,1)S(1)}, u32[]{:S(2)}, u32[]{:S(2)}) collective-permute-start(bf16[448,1024]{1,0:T(8,128)(2,1)S(1)} %collective-permute-done.24.refs_25_), channel_id=1, source_target_pairs={{0,96},{16,112},{32,0},{48,16},{64,32},{80,48},{96,64},{112,80},{1... | collective-permute-start | bytes 2752520 | tf_op jit(solution)/shard_map/ppermute | solution.py:30
  147.1 26.6 %collective-permute-start.17 = (bf16[576,1024]{1,0:T(8,128)(2,1)S(1)}, bf16[576,1024]{1,0:T(8,128)(2,1)S(1)}, u32[]{:S(2)}, u32[]{:S(2)}) collective-permute-start(bf16[576,1024]{1,0:T(8,128)(2,1)S(1)} %collective-permute-done.16.refs_17_), channel_id=1, source_target_pairs={{0,16},{16,0},{32,48},{48,32},{64,80},{80,64},{96,112},{112,96},{1... | collective-permute-start | bytes 3538952 | tf_op jit(solution)/shard_map/ppermute | solution.py:30
  147.3 30.4 %collective-permute-start.21 = (bf16[576,1024]{1,0:T(8,128)(2,1)S(1)}, bf16[576,1024]{1,0:T(8,128)(2,1)S(1)}, u32[]{:S(2)}, u32[]{:S(2)}) collective-permute-start(bf16[576,1024]{1,0:T(8,128)(2,1)S(1)} %collective-permute-done.18.refs_21_), channel_id=1, source_target_pairs={{0,16},{16,0},{32,48},{48,32},{64,80},{80,64},{96,112},{112,96},{1... | collective-permute-start | bytes 3538952 | tf_op jit(solution)/shard_map/ppermute | solution.py:30
  147.7 25.7 %collective-permute-start.29 = (bf16[448,1024]{1,0:T(8,128)(2,1)S(1)}, bf16[448,1024]{1,0:T(8,128)(2,1)S(1)}, u32[]{:S(2)}, u32[]{:S(2)}) collective-permute-start(bf16[448,1024]{1,0:T(8,128)(2,1)S(1)} %collective-permute-done.28.refs_29_), channel_id=1, source_target_pairs={{0,16},{16,0},{32,48},{48,32},{64,80},{80,64},{96,112},{112,96},{1... | collective-permute-start | bytes 2752520 | tf_op jit(solution)/shard_map/ppermute | solution.py:30
  171.5 11.1 %collective-permute-start.20 = (bf16[576,1024]{1,0:T(8,128)(2,1)S(1)}, bf16[576,1024]{1,0:T(8,128)(2,1)S(1)}, u32[]{:S(2)}, u32[]{:S(2)}) collective-permute-start(bf16[576,1024]{1,0:T(8,128)(2,1)S(1)} %collective-permute-done.19.refs_19_), channel_id=1, source_target_pairs={{0,16},{16,0},{32,48},{48,32},{64,80},{80,64},{96,112},{112,96},{1... | collective-permute-start | bytes 3538952 | tf_op jit(solution)/shard_map/ppermute | solution.py:30
  173.4 34.1 %collective-permute-start.39 = (bf16[288,1024]{1,0:T(8,128)(2,1)}, bf16[288,1024]{1,0:T(8,128)(2,1)S(1)}, u32[]{:S(2)}, u32[]{:S(2)}) collective-permute-start(bf16[288,1024]{1,0:T(8,128)(2,1)} %collective-permute-done.31.refs_1_), channel_id=1, source_target_pairs={{0,12},{1,13},{2,14},{3,15},{4,0},{5,1},{6,2},{7,3},{8,4},{9,5},{1... | collective-permute-start | bytes 1769480 | tf_op jit(solution)/shard_map/ppermute | solution.py:30
  173.8 49.9 %collective-permute-start.33 = (bf16[576,1024]{1,0:T(8,128)(2,1)}, bf16[576,1024]{1,0:T(8,128)(2,1)}, u32[]{:S(2)}, u32[]{:S(2)}) collective-permute-start(bf16[576,1024]{1,0:T(8,128)(2,1)} %constant_dynamic-update-slice_fusion.2), channel_id=1, source_target_pairs={{0,12},{1,13},{2,14},{3,15},{4,0},{5,1},{6,2},{7,3},{8,4},{9,5},{1... | collective-permute-start | bytes 3538952 | tf_op jit(solution)/shard_map/ppermute | solution.py:30
  177.7 46.1 %collective-permute-start.37 = (bf16[576,1024]{1,0:T(8,128)(2,1)}, bf16[576,1024]{1,0:T(8,128)(2,1)}, u32[]{:S(2)}, u32[]{:S(2)}) collective-permute-start(bf16[576,1024]{1,0:T(8,128)(2,1)} %constant_dynamic-update-slice_fusion.2), channel_id=1, source_target_pairs={{0,4},{1,5},{2,6},{3,7},{4,8},{5,9},{6,10},{7,11},{8,12},{9,13},{1... | collective-permute-start | bytes 3538952 | tf_op jit(solution)/shard_map/ppermute | solution.py:30
  177.7 29.9 %collective-permute-start.41 = (bf16[288,1024]{1,0:T(8,128)(2,1)S(1)}, bf16[288,1024]{1,0:T(8,128)(2,1)S(1)}, u32[]{:S(2)}, u32[]{:S(2)}) collective-permute-start(bf16[288,1024]{1,0:T(8,128)(2,1)S(1)} %collective-permute-done.40.refs_7_), channel_id=1, source_target_pairs={{0,3},{1,2},{2,1},{3,0},{4,7},{5,6},{6,5},{7,4},{8,11},{9,10},{10,... | collective-permute-start | bytes 1769480 | tf_op jit(solution)/shard_map/ppermute | solution.py:30
  182.6 41.1 %collective-permute-start.36 = (bf16[288,1024]{1,0:T(8,128)(2,1)S(1)}, bf16[288,1024]{1,0:T(8,128)(2,1)S(1)}, u32[]{:S(2)}, u32[]{:S(2)}) collective-permute-start(bf16[288,1024]{1,0:T(8,128)(2,1)S(1)} %collective-permute-done.35.refs_8_), channel_id=1, source_target_pairs={{0,3},{1,2},{2,1},{3,0},{4,7},{5,6},{6,5},{7,4},{8,11},{9,10},{10,... | collective-permute-start | bytes 1769480 | tf_op jit(solution)/shard_map/ppermute | solution.py:30
  207.5 30.8 %collective-permute-start.43 = (bf16[2,144,1024]{2,1,0:T(8,128)(2,1)S(1)}, bf16[2,144,1024]{2,1,0:T(8,128)(2,1)S(1)}, u32[]{:S(2)}, u32[]{:S(2)}) collective-permute-start(bf16[2,144,1024]{2,1,0:T(8,128)(2,1)S(1)} %get-tuple-element.22), channel_id=1, source_target_pairs={{0,48},{1,33},{2,34},{3,51},{4,52},{5,37},{6,38},{7,55},{8,56},{9,... | collective-permute-start | bytes 1769480 | tf_op jit(solution)/shard_map/ppermute | solution.py:30
  208.4 29.9 %collective-permute-start.44 = (bf16[2,144,1024]{2,1,0:T(8,128)(2,1)S(1)}, bf16[2,144,1024]{2,1,0:T(8,128)(2,1)S(1)}, u32[]{:S(2)}, u32[]{:S(2)}) collective-permute-start(bf16[2,144,1024]{2,1,0:T(8,128)(2,1)S(1)} %get-tuple-element.23), channel_id=1, source_target_pairs={{0,96},{1,113},{2,114},{3,99},{4,100},{5,117},{6,118},{7,103},{8,1... | collective-permute-start | bytes 1769480 | tf_op jit(solution)/shard_map/ppermute | solution.py:30
  232.7 19.5 %collective-permute-start.45 = (bf16[144,1024]{1,0:T(8,128)(2,1)S(1)}, bf16[144,1024]{1,0:T(8,128)(2,1)S(1)}, u32[]{:S(2)}, u32[]{:S(2)}) collective-permute-start(bf16[144,1024]{1,0:T(8,128)(2,1)S(1)} %get-tuple-element.24), channel_id=1, source_target_pairs={{0,64},{1,81},{2,82},{3,67},{4,68},{5,85},{6,86},{7,71},{8,72},{9,... | collective-permute-start | bytes 884744 | tf_op jit(solution)/shard_map/ppermute | solution.py:30
  235.2 14.8 %collective-permute-start.46 = (bf16[2,144,1024]{2,1,0:T(8,128)(2,1)S(1)}, bf16[2,144,1024]{2,1,0:T(8,128)(2,1)S(1)}, u32[]{:S(2)}, u32[]{:S(2)}) collective-permute-start(bf16[2,144,1024]{2,1,0:T(8,128)(2,1)S(1)} %get-tuple-element.25), channel_id=1, source_target_pairs={{0,16},{1,1},{2,2},{3,19},{4,20},{5,5},{6,6},{7,23},{8,24},{9,9},{... | collective-permute-start | bytes 1769480 | tf_op jit(solution)/shard_map/ppermute | solution.py:30
  237.5 12.3 %collective-permute-start.48 = (bf16[144,1024]{1,0:T(8,128)(2,1)S(1)}, bf16[144,1024]{1,0:T(8,128)(2,1)S(1)}, u32[]{:S(2)}, u32[]{:S(2)}) collective-permute-start(bf16[144,1024]{1,0:T(8,128)(2,1)S(1)} %get-tuple-element.26), channel_id=1, source_target_pairs={{0,64},{1,81},{2,82},{3,67},{4,68},{5,85},{6,86},{7,71},{8,72},{9,... | collective-permute-start | bytes 884744 | tf_op jit(solution)/shard_map/ppermute | solution.py:30
  239.3 28.1 %collective-permute-start.47 = (bf16[288,1024]{1,0:T(8,128)(2,1)S(1)}, bf16[288,1024]{1,0:T(8,128)(2,1)S(1)}, u32[]{:S(2)}, u32[]{:S(2)}) collective-permute-start(bf16[288,1024]{1,0:T(8,128)(2,1)S(1)} %pad_maximum_fusion), channel_id=1, source_target_pairs={{0,1},{1,0},{2,3},{3,2},{4,5},{5,4},{6,7},{7,6},{8,9},{9,8},{10,11... | collective-permute-start | bytes 1769480 | tf_op jit(solution)/shard_map/ppermute | solution.py:30
  249.9 12.0 %collective-permute-start.49 = (bf16[144,1024]{1,0:T(8,128)(2,1)S(1)}, bf16[144,1024]{1,0:T(8,128)(2,1)S(1)}, u32[]{:S(2)}, u32[]{:S(2)}) collective-permute-start(bf16[144,1024]{1,0:T(8,128)(2,1)S(1)} %fusion.1), channel_id=1, source_target_pairs={{0,1},{1,0},{2,3},{3,2},{4,5},{5,4},{6,7},{7,6},{8,9},{9,8},{10,11... | collective-permute-start | bytes 884744 | tf_op jit(solution)/shard_map/ppermute | solution.py:30
  250.1 17.3 %collective-permute-start.50 = (bf16[144,1024]{1,0:T(8,128)(2,1)S(1)}, bf16[144,1024]{1,0:T(8,128)(2,1)S(1)}, u32[]{:S(2)}, u32[]{:S(2)}) collective-permute-start(bf16[144,1024]{1,0:T(8,128)(2,1)S(1)} %fusion.4), channel_id=1, source_target_pairs={{0,1},{1,0},{2,3},{3,2},{4,5},{5,4},{6,7},{7,6},{8,9},{9,8},{10,11... | collective-permute-start | bytes 884744 | tf_op jit(solution)/shard_map/ppermute | solution.py:30
  (44 other events, 1077.5 us)
